TPU v7x, 32 devices: a whole 2x2x4 slice. The times are simulated.
32 devices in a mesh: dp: 8 (over z, y), fsdp: 4 (over x, core).
Axes of the slice: x: 2, y: 2, z: 4, core: 2. Of those that a mesh axis runs over, the one named last changes fastest.
Arguments:
- inputs: bfloat16 [64, 128, 768], P(('dp', 'fsdp')), may hold values from -6 to 6
- species: int32 [64], P(('dp', 'fsdp')), may hold values 0 or 1
- gene_ids: int32 [64, 128], P(('dp', 'fsdp')), may hold values from 0 to 35999, as said below
- cotangent: bfloat16 [64, 128, 768], P(('dp', 'fsdp')), may hold values from -6 to 6
- table: bfloat16 [2, 768], P(None, 'fsdp'), may hold values from -3 to 3
- w_query: bfloat16 [768, 768], P('fsdp'), may hold values from -0.3125 to 0.3125
- b_query: bfloat16 [768], P('fsdp'), may hold values from -2 to 2
- w_key: bfloat16 [768, 768], P('fsdp'), may hold values from -0.3125 to 0.3125
- w_value: bfloat16 [768, 768], P('fsdp'), may hold values from -0.21875 to 0.21875
- b_value: bfloat16 [768], P('fsdp'), may hold values from -0.59765625 to 0.59765625
- w_out: bfloat16 [768, 768], P('fsdp'), may hold values from -0.875 to 0.875
- b_out: bfloat16 [768], P('fsdp'), may hold values from -2 to 2
- gain_one: bfloat16 [768], P('fsdp'), may hold values from 0.5 to 1.5
- shift_one: bfloat16 [768], P('fsdp'), may hold values from -2 to 2
- w_up: bfloat16 [768, 3072], P('fsdp'), may hold values from -0.21875 to 0.21875
- b_up: bfloat16 [3072], P('fsdp'), may hold values from -2 to 2
- w_down: bfloat16 [3072, 768], P('fsdp'), may hold values from -0.109375 to 0.109375
- b_down: bfloat16 [768], P('fsdp'), may hold values from -2 to 2
- gain_two: bfloat16 [768], P('fsdp'), may hold values from 0.5 to 1.5
- shift_two: bfloat16 [768], P('fsdp'), may hold values from -2 to 2
Outputs:
- output: bfloat16 [64, 128, 768], P(('dp', 'fsdp'))
- input_grad: bfloat16 [64, 128, 768], P(('dp', 'fsdp'))
- grad_table: float32 [2, 768], P(None, 'fsdp')
- grad_w_query: float32 [768, 768], P('fsdp')
- grad_b_query: float32 [768], P('fsdp')
- grad_w_key: float32 [768, 768], P('fsdp')
- grad_w_value: float32 [768, 768], P('fsdp')
- grad_b_value: float32 [768], P('fsdp')
- grad_w_out: float32 [768, 768], P('fsdp')
- grad_b_out: float32 [768], P('fsdp')
- grad_gain_one: float32 [768], P('fsdp')
- grad_shift_one: float32 [768], P('fsdp')
- grad_w_up: float32 [768, 3072], P('fsdp')
- grad_b_up: float32 [3072], P('fsdp')
- grad_w_down: float32 [3072, 768], P('fsdp')
- grad_b_down: float32 [768], P('fsdp')
- grad_gain_two: float32 [768], P('fsdp')
- grad_shift_two: float32 [768], P('fsdp')
Inputs may be any that keep to these rules, and one draw needn't show every extreme that they name: `gene_ids`: 0 marks a padding position; the live genes of a cell come first and are at least 32; the first cell has all 128 positions live.
All inputs are finite; a program needn't handle non-finite values. No bound on the sum of `species` on one device may be relied on, other than what follows from the above.
Results may differ from a plain program's by a relative error of at most 0.02.
The roundings to bfloat16 on the way count: a program that leaves them out, or rounds other values in their place, can miss the bound.
Values may be sent and summed in bfloat16 or wider, within the bound.
No kernel may reach another device: no remote copies, remote signals or barrier semaphores. Data moves between devices by JAX's collectives and lax.ppermute only.
A program may use at most 192 MiB of HBM per device.

v0:
```python
from functools import partial

import jax
import jax.numpy as jnp
from jax import lax
from jax.sharding import PartitionSpec as P

HEAD_DIM = 64


norm_eps = 1e-12
masked_score = -1e30


def layer_forward(residual, gain, shift):
    average = jnp.mean(residual, axis=-1, keepdims=True)
    centred = residual - average
    inverse = lax.rsqrt(jnp.mean(centred * centred, axis=-1, keepdims=True) + norm_eps)
    normal_form = centred * inverse
    return (normal_form * gain + shift, normal_form, inverse)


def layer_backward(grad_out, normal_form, inverse, gain):
    scaled = grad_out * gain
    first_term = jnp.mean(scaled, axis=-1, keepdims=True)
    second_term = jnp.mean(scaled * normal_form, axis=-1, keepdims=True)
    grad_in = inverse * (scaled - first_term - normal_form * second_term)
    return (grad_in, jnp.sum(grad_out * normal_form, axis=0), jnp.sum(grad_out, axis=0))


def attend_forward(query_rows, key_rows, value_rows, live_keys, score_scale):
    cell_count, length, head_count, head_size = query_rows.shape
    block_rows = min(512, length)
    block_count = length // block_rows

    def attend_one_block(position):
        cell_index = position // block_count
        row_start = position % block_count * block_rows
        query_part = lax.dynamic_slice(
            query_rows, (cell_index, row_start, 0, 0), (1, block_rows, head_count, head_size)
        )[0]
        key_cell = lax.dynamic_index_in_dim(key_rows, cell_index, 0, keepdims=False)
        value_cell = lax.dynamic_index_in_dim(value_rows, cell_index, 0, keepdims=False)
        live_cell = lax.dynamic_index_in_dim(live_keys, cell_index, 0, keepdims=False)
        scores = (
            jnp.einsum("qhe,khe->hqk", query_part, key_cell, preferred_element_type=jnp.float32)
            * score_scale
        )
        scores = jnp.where(live_cell[None, None, :], scores, masked_score)
        row_max = jnp.max(scores, axis=-1, keepdims=True)
        expo_rows = jnp.exp(scores - row_max)
        row_total = jnp.sum(expo_rows, axis=-1, keepdims=True)
        soft_low = (expo_rows / row_total).astype(jnp.bfloat16)
        attended = jnp.einsum(
            "hqk,khe->qhe", soft_low, value_cell, preferred_element_type=jnp.float32
        )
        return (attended.astype(jnp.bfloat16), (row_max + jnp.log(row_total))[..., 0])

    attended, log_total = lax.map(attend_one_block, jnp.arange(cell_count * block_count))
    attended = attended.reshape(cell_count, length, head_count * head_size)
    log_total = log_total.reshape(cell_count, block_count, head_count, block_rows)
    log_total = log_total.transpose(0, 2, 1, 3).reshape(cell_count, head_count, length)
    return (attended, log_total)


def attend_backward(
    query_rows, key_rows, value_rows, live_keys, log_total, grad_attended, score_scale
):
    cell_count, length, head_count, head_size = query_rows.shape
    block_rows = min(512, length)
    block_count = length // block_rows

    def one_cell(cell_index):
        query_cell = lax.dynamic_index_in_dim(query_rows, cell_index, 0, keepdims=False)
        key_cell = lax.dynamic_index_in_dim(key_rows, cell_index, 0, keepdims=False)
        value_cell = lax.dynamic_index_in_dim(value_rows, cell_index, 0, keepdims=False)
        live_cell = lax.dynamic_index_in_dim(live_keys, cell_index, 0, keepdims=False)
        log_cell = lax.dynamic_index_in_dim(log_total, cell_index, 0, keepdims=False)
        grad_cell = lax.dynamic_index_in_dim(grad_attended, cell_index, 0, keepdims=False)

        def one_one_block(carry, block_index):
            grad_key_sum, grad_value_sum = carry
            scores = (
                jnp.einsum("qhe,khe->hqk", query_cell, key_cell, preferred_element_type=jnp.float32)
                * score_scale
            )
            scores = jnp.where(live_cell[None, None, :], scores, masked_score)
            soft_rows = jnp.exp(scores - log_cell[..., None])
            grad_soft = jnp.einsum(
                "qhe,khe->hqk", grad_cell, value_cell, preferred_element_type=jnp.float32
            )
            inner_sum = jnp.sum(soft_rows * grad_soft, axis=-1, keepdims=True)
            grad_scores = (soft_rows * (grad_soft - inner_sum)).astype(jnp.bfloat16)
            grad_value_sum = grad_value_sum + jnp.einsum(
                "hqk,qhe->khe",
                soft_rows.astype(jnp.bfloat16),
                grad_cell,
                preferred_element_type=jnp.float32,
            )
            grad_query_part = (
                jnp.einsum(
                    "hqk,khe->qhe", grad_scores, key_cell, preferred_element_type=jnp.float32
                )
                * score_scale
            )
            grad_key_sum = (
                grad_key_sum
                + jnp.einsum(
                    "hqk,qhe->khe", grad_scores, query_cell, preferred_element_type=jnp.float32
                )
                * score_scale
            )
            return ((grad_key_sum, grad_value_sum), grad_query_part.astype(jnp.bfloat16))

        zero_start = jnp.zeros((length, head_count, head_size), jnp.float32)
        (grad_key_sum, grad_value_sum), grad_query_blocks = lax.scan(
            one_one_block, (zero_start, zero_start), jnp.arange(block_count)
        )
        grad_query_cell = grad_query_blocks.reshape(length, head_count, head_size)
        return (
            grad_query_cell,
            grad_key_sum.astype(jnp.bfloat16),
            grad_value_sum.astype(jnp.bfloat16),
        )

    return lax.map(one_cell, jnp.arange(cell_count))


def transposed_dot(left_rows, right_rows):
    return jnp.einsum("ti,tj->ij", left_rows, right_rows, preferred_element_type=jnp.float32)


def column_total(rows_low):
    return jnp.sum(rows_low.astype(jnp.float32), axis=0)


def pack_terms(terms, dims, fsdp_count, dp_count):
    columns = []
    for term, term_dim in zip(terms, dims):
        moved = jnp.moveaxis(term, term_dim, 0)
        blocks = moved.reshape(fsdp_count, dp_count, -1).swapaxes(0, 1)
        columns.append(blocks)
    packed = jnp.concatenate(columns, axis=2)
    return packed.reshape(dp_count * fsdp_count, packed.shape[2])


def unpack_terms(packed, terms, dims, fsdp_count):
    piece_rows = packed.shape[0]
    results = []
    offset = 0
    for term, term_dim in zip(terms, dims):
        moved_shape = jnp.moveaxis(term, term_dim, 0).shape
        local_rows = moved_shape[0] // fsdp_count
        width_each = term.size // (fsdp_count * piece_rows)
        piece = packed[:, offset : offset + width_each]
        offset = offset + width_each
        restored = piece.reshape((local_rows,) + moved_shape[1:])
        results.append(jnp.moveaxis(restored, 0, term_dim))
    return tuple(results)


def local(
    inputs,
    species,
    gene_ids,
    cotangent,
    table,
    w_query,
    b_query,
    w_key,
    w_value,
    b_value,
    w_out,
    b_out,
    gain_one,
    shift_one,
    w_up,
    b_up,
    w_down,
    b_down,
    gain_two,
    shift_two,
):
    cell_count, length, width_all = inputs.shape
    token_count = cell_count * length
    head_count = width_all // HEAD_DIM
    score_scale = HEAD_DIM ** (-0.5)
    split_shape = (cell_count, length, head_count, HEAD_DIM)
    fsdp_count = lax.axis_size("fsdp")
    attn_local = (w_query, w_key, w_value, w_out, b_query, b_value, b_out, table)
    ffn_local = (w_up, w_down, b_up, b_down, gain_one, shift_one, gain_two, shift_two)
    attn_full = (
        lax.all_gather(attn_local[0], "fsdp", axis=0, tiled=True),
        lax.all_gather(attn_local[1], "fsdp", axis=0, tiled=True),
        lax.all_gather(attn_local[2], "fsdp", axis=0, tiled=True),
        lax.all_gather(attn_local[3], "fsdp", axis=0, tiled=True),
        lax.all_gather(attn_local[4], "fsdp", axis=0, tiled=True),
        lax.all_gather(attn_local[5], "fsdp", axis=0, tiled=True),
        lax.all_gather(attn_local[6], "fsdp", axis=0, tiled=True),
        lax.all_gather(attn_local[7], "fsdp", axis=1, tiled=True),
    )
    ffn_full = (
        lax.all_gather(ffn_local[0], "fsdp", axis=0, tiled=True),
        lax.all_gather(ffn_local[1], "fsdp", axis=0, tiled=True),
        lax.all_gather(ffn_local[2], "fsdp", axis=0, tiled=True),
        lax.all_gather(ffn_local[3], "fsdp", axis=0, tiled=True),
        lax.all_gather(ffn_local[4], "fsdp", axis=0, tiled=True),
        lax.all_gather(ffn_local[5], "fsdp", axis=0, tiled=True),
        lax.all_gather(ffn_local[6], "fsdp", axis=0, tiled=True),
        lax.all_gather(ffn_local[7], "fsdp", axis=0, tiled=True),
    )
    (
        whole_query,
        whole_key,
        whole_value,
        whole_out,
        bias_query,
        bias_value,
        bias_out,
        whole_table,
    ) = attn_full
    (
        whole_up,
        whole_down,
        bias_up,
        bias_down,
        norm_gain_one,
        norm_shift_one,
        norm_gain_two,
        norm_shift_two,
    ) = ffn_full
    onehot = (species[:, None] == jnp.arange(2, dtype=jnp.int32)[None, :]).astype(jnp.float32)
    offsets = jnp.dot(onehot, whole_table.astype(jnp.float32), precision=lax.Precision.HIGHEST)
    summed = (inputs.astype(jnp.float32) + offsets[:, None, :]).reshape(token_count, width_all)
    summed_low = summed.astype(jnp.bfloat16)
    query_rows = (
        jnp.dot(summed_low, whole_query, preferred_element_type=jnp.float32)
        + bias_query.astype(jnp.float32)
    ).astype(jnp.bfloat16)
    key_rows = jnp.dot(summed_low, whole_key, preferred_element_type=jnp.float32).astype(
        jnp.bfloat16
    )
    value_rows = (
        jnp.dot(summed_low, whole_value, preferred_element_type=jnp.float32)
        + bias_value.astype(jnp.float32)
    ).astype(jnp.bfloat16)
    live_keys = gene_ids != 0
    attended, log_total = attend_forward(
        query_rows.reshape(split_shape),
        key_rows.reshape(split_shape),
        value_rows.reshape(split_shape),
        live_keys,
        score_scale,
    )
    attended_rows = attended.reshape(token_count, width_all)
    branch = jnp.dot(
        attended_rows, whole_out, preferred_element_type=jnp.float32
    ) + bias_out.astype(jnp.float32)
    residual = summed + branch
    normed, normal_one, inverse_one = layer_forward(
        residual, norm_gain_one.astype(jnp.float32), norm_shift_one.astype(jnp.float32)
    )
    normed_low = normed.astype(jnp.bfloat16)
    up_input = jnp.dot(normed_low, whole_up, preferred_element_type=jnp.float32) + bias_up.astype(
        jnp.float32
    )
    active = jax.nn.gelu(up_input, approximate=False).astype(jnp.bfloat16)
    branch_two = jnp.dot(active, whole_down, preferred_element_type=jnp.float32) + bias_down.astype(
        jnp.float32
    )
    output_rows, normal_two, inverse_two = layer_forward(
        normed + branch_two, norm_gain_two.astype(jnp.float32), norm_shift_two.astype(jnp.float32)
    )
    output = output_rows.astype(jnp.bfloat16).reshape(inputs.shape)
    ffn_back = (
        lax.all_gather(ffn_local[0], "fsdp", axis=0, tiled=True),
        lax.all_gather(ffn_local[1], "fsdp", axis=0, tiled=True),
        lax.all_gather(ffn_local[2], "fsdp", axis=0, tiled=True),
        lax.all_gather(ffn_local[3], "fsdp", axis=0, tiled=True),
        lax.all_gather(ffn_local[4], "fsdp", axis=0, tiled=True),
        lax.all_gather(ffn_local[5], "fsdp", axis=0, tiled=True),
        lax.all_gather(ffn_local[6], "fsdp", axis=0, tiled=True),
        lax.all_gather(ffn_local[7], "fsdp", axis=0, tiled=True),
    )
    (
        back_up,
        back_down,
        unused_up,
        unused_down,
        back_gain_one,
        unused_one,
        back_gain_two,
        unused_two,
    ) = ffn_back
    grad_rows = cotangent.astype(jnp.float32).reshape(token_count, width_all)
    grad_second, grad_gain_two, grad_shift_two = layer_backward(
        grad_rows, normal_two, inverse_two, back_gain_two.astype(jnp.float32)
    )
    grad_branch_two = grad_second.astype(jnp.bfloat16)
    grad_w_down = transposed_dot(active, grad_branch_two)
    grad_b_down = column_total(grad_branch_two)
    grad_active = jnp.dot(grad_branch_two, back_down.T, preferred_element_type=jnp.float32)
    gelu_pull = jax.vjp(partial(jax.nn.gelu, approximate=False), up_input)[1]
    grad_up_input = gelu_pull(grad_active)[0].astype(jnp.bfloat16)
    grad_w_up = transposed_dot(normed_low, grad_up_input)
    grad_b_up = column_total(grad_up_input)
    grad_normed = grad_second + jnp.dot(
        grad_up_input, back_up.T, preferred_element_type=jnp.float32
    )
    grad_residual, grad_gain_one, grad_shift_one = layer_backward(
        grad_normed, normal_one, inverse_one, back_gain_one.astype(jnp.float32)
    )
    ffn_terms = (
        grad_w_up,
        grad_w_down,
        grad_b_up,
        grad_b_down,
        grad_gain_one,
        grad_shift_one,
        grad_gain_two,
        grad_shift_two,
    )
    ffn_dims = (0, 0, 0, 0, 0, 0, 0, 0)
    ffn_packed = pack_terms(ffn_terms, ffn_dims, fsdp_count, 1)
    ffn_piece = lax.psum_scatter(
        ffn_packed.astype(jnp.bfloat16), "fsdp", scatter_dimension=0, tiled=True
    ).astype(jnp.float32)
    ffn_shares = unpack_terms(ffn_piece, ffn_terms, ffn_dims, fsdp_count)
    attn_back = (
        lax.all_gather(attn_local[0], "fsdp", axis=0, tiled=True),
        lax.all_gather(attn_local[1], "fsdp", axis=0, tiled=True),
        lax.all_gather(attn_local[2], "fsdp", axis=0, tiled=True),
        lax.all_gather(attn_local[3], "fsdp", axis=0, tiled=True),
        lax.all_gather(attn_local[4], "fsdp", axis=0, tiled=True),
        lax.all_gather(attn_local[5], "fsdp", axis=0, tiled=True),
        lax.all_gather(attn_local[6], "fsdp", axis=0, tiled=True),
        lax.all_gather(attn_local[7], "fsdp", axis=1, tiled=True),
    )
    back_query, back_key, back_value, back_out, unused_bq, unused_bv, unused_bo, unused_table = (
        attn_back
    )
    grad_branch = grad_residual.astype(jnp.bfloat16)
    grad_w_out = transposed_dot(attended_rows, grad_branch)
    grad_b_out = column_total(grad_branch)
    grad_attended = jnp.dot(grad_branch, back_out.T, preferred_element_type=jnp.float32).astype(
        jnp.bfloat16
    )
    grad_queries, grad_keys, grad_values = attend_backward(
        query_rows.reshape(split_shape),
        key_rows.reshape(split_shape),
        value_rows.reshape(split_shape),
        live_keys,
        log_total,
        grad_attended.reshape(split_shape),
        score_scale,
    )
    grad_queries = grad_queries.reshape(token_count, width_all)
    grad_keys = grad_keys.reshape(token_count, width_all)
    grad_values = grad_values.reshape(token_count, width_all)
    grad_w_query = transposed_dot(summed_low, grad_queries)
    grad_b_query = column_total(grad_queries)
    grad_w_key = transposed_dot(summed_low, grad_keys)
    grad_w_value = transposed_dot(summed_low, grad_values)
    grad_b_value = column_total(grad_values)
    grad_summed = (
        grad_residual
        + jnp.dot(grad_queries, back_query.T, preferred_element_type=jnp.float32)
        + jnp.dot(grad_keys, back_key.T, preferred_element_type=jnp.float32)
        + jnp.dot(grad_values, back_value.T, preferred_element_type=jnp.float32)
    )
    input_grad = grad_summed.astype(jnp.bfloat16).reshape(inputs.shape)
    cell_sums = jnp.sum(grad_summed.reshape(cell_count, length, width_all), axis=1)
    grad_table = jnp.dot(onehot.T, cell_sums, precision=lax.Precision.HIGHEST)
    attn_terms = (
        grad_w_query,
        grad_w_key,
        grad_w_value,
        grad_w_out,
        grad_b_query,
        grad_b_value,
        grad_b_out,
        grad_table,
    )
    attn_dims = (0, 0, 0, 0, 0, 0, 0, 1)
    attn_packed = pack_terms(attn_terms, attn_dims, fsdp_count, 1)
    attn_piece = lax.psum_scatter(
        attn_packed.astype(jnp.bfloat16), "fsdp", scatter_dimension=0, tiled=True
    ).astype(jnp.float32)
    attn_shares = unpack_terms(attn_piece, attn_terms, attn_dims, fsdp_count)
    share_up, share_down, share_b_up, share_b_down, share_g1, share_s1, share_g2, share_s2 = (
        ffn_shares
    )
    share_wq, share_wk, share_wv, share_wo, share_bq, share_bv, share_bo, share_table = attn_shares
    (
        share_up,
        share_down,
        share_b_up,
        share_b_down,
        share_g1,
        share_s1,
        share_g2,
        share_s2,
        share_wq,
        share_wk,
        share_wv,
        share_wo,
        share_bq,
        share_bv,
        share_bo,
        share_table,
    ) = (
        lax.psum(share_up.astype(jnp.bfloat16), "dp").astype(jnp.float32),
        lax.psum(share_down.astype(jnp.bfloat16), "dp").astype(jnp.float32),
        lax.psum(share_b_up.astype(jnp.bfloat16), "dp").astype(jnp.float32),
        lax.psum(share_b_down.astype(jnp.bfloat16), "dp").astype(jnp.float32),
        lax.psum(share_g1.astype(jnp.bfloat16), "dp").astype(jnp.float32),
        lax.psum(share_s1.astype(jnp.bfloat16), "dp").astype(jnp.float32),
        lax.psum(share_g2.astype(jnp.bfloat16), "dp").astype(jnp.float32),
        lax.psum(share_s2.astype(jnp.bfloat16), "dp").astype(jnp.float32),
        lax.psum(share_wq.astype(jnp.bfloat16), "dp").astype(jnp.float32),
        lax.psum(share_wk.astype(jnp.bfloat16), "dp").astype(jnp.float32),
        lax.psum(share_wv.astype(jnp.bfloat16), "dp").astype(jnp.float32),
        lax.psum(share_wo.astype(jnp.bfloat16), "dp").astype(jnp.float32),
        lax.psum(share_bq.astype(jnp.bfloat16), "dp").astype(jnp.float32),
        lax.psum(share_bv.astype(jnp.bfloat16), "dp").astype(jnp.float32),
        lax.psum(share_bo.astype(jnp.bfloat16), "dp").astype(jnp.float32),
        lax.psum(share_table.astype(jnp.bfloat16), "dp").astype(jnp.float32),
    )
    return (
        output,
        input_grad,
        share_table,
        share_wq,
        share_bq,
        share_wk,
        share_wv,
        share_bv,
        share_wo,
        share_bo,
        share_g1,
        share_s1,
        share_up,
        share_b_up,
        share_down,
        share_b_down,
        share_g2,
        share_s2,
    )


def solution(mesh):
    placed = (
        P(("dp", "fsdp"), None, None),
        P(("dp", "fsdp")),
        P(("dp", "fsdp"), None),
        P(("dp", "fsdp"), None, None),
        P(None, "fsdp"),
        P("fsdp", None),
        P("fsdp"),
        P("fsdp", None),
        P("fsdp", None),
        P("fsdp"),
        P("fsdp", None),
        P("fsdp"),
        P("fsdp"),
        P("fsdp"),
        P("fsdp", None),
        P("fsdp"),
        P("fsdp", None),
        P("fsdp"),
        P("fsdp"),
        P("fsdp"),
    )
    return jax.shard_map(
        local,
        mesh=mesh,
        in_specs=placed,
        out_specs=(
            P(("dp", "fsdp"), None, None),
            P(("dp", "fsdp"), None, None),
            P(None, "fsdp"),
            P("fsdp", None),
            P("fsdp"),
            P("fsdp", None),
            P("fsdp", None),
            P("fsdp"),
            P("fsdp", None),
            P("fsdp"),
            P("fsdp"),
            P("fsdp"),
            P("fsdp", None),
            P("fsdp"),
            P("fsdp", None),
            P("fsdp"),
            P("fsdp"),
            P("fsdp"),
        ),
        check_vma=False,
    )
```

profile of v0, /device:TPU:0, one launch (start us, length us, event | category | flops | bytes accessed | tf_op | source)
XLA Modules:
  0.0 738.4 jit_solution(7132789960559723021)
XLA Ops:
  14.5 13.5 %all-reduce.12 = (bf16[768]{0:T(1024)(128)(2,1)S(1)}, bf16[768]{0:T(1024)(128)(2,1)S(1)}, bf16[768]{0:T(1024)(128)(2,1)S(1)}, bf16[768]{0:T(1024)(128)(2,1)S(1)}...) all-reduce(bf16[768]{0:T(1024)(128)(2,1)S(1)} %dynamic-update-slice, ...), channel_id=1, replica_groups=mesh['dp'=8,'fsdp'=4] {'fsdp'}, use_global_device_ids=true, to_apply=%add.1 | all-reduce | flops 6144 | bytes 24576
  28.7 5.2 all-gather.1
  34.5 5.1 all-gather
  42.6 1.8 fusion.53
  44.7 4.4 all-gather.11.cloned.1.call-done
  49.1 1.7 fusion.54
  51.2 16.9 %all-gather.13.cloned.1.call-done = bf16[768,768]{1,0:T(8,128)(2,1)} async-done(((bf16[192,768]{1,0:T(8,128)(2,1)}), bf16[768,768]{1,0:T(8,128)(2,1)}) %all-gather.13.cloned.1.call-update) | async-done | bytes 1179664 | tf_op jit(solution)/shard_map/all_gather | solution.py:194
  68.1 1.7 convolution_convert_fusion.9
  70.4 9.2 %while.34 = (s32[]{:T(128)}, bf16[2,128,12,64]{1,3,2,0:T(8,128)(2,1)S(1)}, f32[2,12,128]{2,1,0:T(8,128)}, s32[2]{0:T(128)S(1)}, bf16[2,128,12,64]{1,3,2,0:T(8,12...) while((s32[]{:T(128)}, ...), condition=%wide.region_3.4_spmd, body=%wide.region_0.3_spmd.sunk | while | flops 52001284 | bytes 3305451 | solution.py:59
  80.7 6.3 all-gather.15.cloned.1.call-done
  87.0 2.0 fusion.96
  89.3 36.6 %all-gather.17.cloned.1.call-done = bf16[768,3072]{1,0:T(8,128)(2,1)} async-done(((bf16[192,3072]{1,0:T(8,128)(2,1)}), bf16[768,3072]{1,0:T(8,128)(2,1)}) %all-gather.17.cloned.1.call-update) | async-done | bytes 4718608 | tf_op jit(solution)/shard_map/all_gather | solution.py:203
  125.9 11.9 %multiply_convert_fusion.1 = (bf16[256,3072]{1,0:T(8,128)(2,1)}, f32[256,3072]{1,0:T(8,128)}, f32[256,3072]{1,0:T(8,128)}) fusion(f32[3072]{0:T(1024)} %bitcast.240, bf16[768,3072]{1,0:T(8,128)(2,1)} %all-gather.17.cloned.1.call-done, f32[256,768]{1,0:T(8,128)S(1)} %get-tuple-element.409, f32[768]{0:T(1024)S(1)} %convert_element_type.273, ...), kind=kOutput, calls=%fused_computation.65 | convolution fusion | flops 1260847104 | bytes 13389824 | tf_op jit(solution)/shard_map/dot_general | solution.py:264
  137.8 27.0 %all-gather.19.cloned.1.call-done = bf16[3072,768]{1,0:T(8,128)(2,1)} async-done(((bf16[768,768]{1,0:T(8,128)(2,1)}), bf16[3072,768]{1,0:T(8,128)(2,1)}) %all-gather.19.cloned.1.call-update) | async-done | bytes 4718608 | tf_op jit(solution)/shard_map/all_gather | solution.py:204
  164.8 4.4 fusion.97
  169.5 1.7 fusion.61
  172.2 3.8 convolution_convert_fusion.2
  176.0 2.8 fusion.99
  178.8 3.7 convolution_convert_fusion.3
  182.5 2.2 multiply_reduce_fusion.1
  185.7 1.5 convolution_convert_fusion.4
  189.6 21.3 %while.35 = (s32[]{:T(128)}, bf16[2,128,12,64]{1,3,2,0:T(8,128)(2,1)S(1)}, bf16[2,128,12,64]{1,3,2,0:T(8,128)(2,1)}, bf16[2,128,12,64]{1,3,2,0:T(8,128)(2,1)S(1)...) while((s32[]{:T(128)}, ...), condition=%wide.region_14.15_spmd, body=%wide.region_12.14_spmd.sunk | while | flops 128088576 | bytes 11045907 | solution.py:126
  211.3 2.3 copy.89
  214.1 1.5 convolution_convert_fusion.7
  215.6 2.2 transpose_reshape.64
  217.8 1.3 constant_dynamic-update-slice_fusion.3
  219.0 1.5 convolution_convert_fusion.6
  220.6 1.9 transpose_reshape.65
  223.0 1.9 transpose_reshape.66
  224.9 2.3 transpose_reshape.67
  230.6 2.0 convolution_add_fusion.3
  233.2 1.3 fusion.98
  235.2 8.1 %transpose_reshape.72 = bf16[1,4,589824]{2,1,0:T(4,128)(2,1)} reshape(bf16[768,3072]{1,0:T(8,128)(2,1)} %convolution_convert_fusion.3) | data formatting | bytes 9437184 | tf_op jit(solution)/shard_map/transpose;reshape | solution.py:141
  243.4 6.9 constant_dynamic-update-slice_fusion.7
  250.3 8.2 %transpose_reshape.73 = bf16[1,4,589824]{2,1,0:T(4,128)(2,1)} reshape(bf16[3072,768]{1,0:T(8,128)(2,1)} %convolution_convert_fusion.2) | data formatting | bytes 9437184 | tf_op jit(solution)/shard_map/transpose;reshape | solution.py:141
  259.3 1.3 transpose_reshape.75
  260.7 1.3 transpose_reshape.76
  262.0 1.3 transpose_reshape.77
  267.8 3.8 constant_dynamic-update-slice_fusion.6
  272.2 1.3 dynamic-update-slice.11
  273.6 1.4 dynamic-update-slice.12
  275.0 1.3 dynamic-update-slice.13
  276.3 1.4 dynamic-update-slice.14
  278.3 1.3 dynamic-update-slice.20
  279.6 1.4 dynamic-update-slice.21
  281.0 1.3 dynamic-update-slice.22
  282.4 1.5 dynamic-update-slice.23
  283.9 247.0 %all-reduce.19.cloned.1.call-done = (bf16[4,590784]{1,0:T(4,128)(2,1)}, bf16[4,1181376]{1,0:T(4,128)(2,1)}) async-done(((bf16[4,590784]{1,0:T(4,128)(2,1)}, bf16[4,1181376]{1,0:T(4,128)(2,1)}), (bf16[4,590784]{1,0:T(4,128)(2,1)}, bf16[4,1181376]{1,0:T(4,128)(2,1)})) %all-reduce.19.cloned.1.call-update) | async-done | bytes 14177296
  530.9 13.9 %dynamic-slice_reduce_fusion.2 = (bf16[147456]{0:T(1024)(128)(2,1)S(1)}, bf16[147456]{0:T(1024)(128)(2,1)S(1)}, bf16[147456]{0:T(1024)(128)(2,1)S(1)}, bf16[147456]{0:T(1024)(128)(2,1)S(1)}) fusion(bf16[4,590784]{1,0:T(4,128)(2,1)} %get-tuple-element.391, u32[]{:T(128)} %bitcast.40, u32[]{:T(128)S(6)} %convert.107, u32[]{:T(128)S(6)} %convert.105, ...), kind=kLoop, calls=%fused_computation.124 | loop fusion | bytes 2359312 | tf_op jit(solution)/shard_map/slice | solution.py:155
  548.8 27.6 %dynamic-slice_reduce_fusion = (bf16[589824]{0:T(1024)(128)(2,1)S(1)}, bf16[589824]{0:T(1024)(128)(2,1)S(1)}) fusion(bf16[4,1181376]{1,0:T(4,128)(2,1)} %get-tuple-element.392, u32[]{:T(128)} %bitcast.40, u32[]{:T(128)S(6)} %convert.103), kind=kLoop, calls=%fused_computation.79 | loop fusion | bytes 4718600 | tf_op jit(solution)/shard_map/slice | solution.py:155
  576.4 1.4 convert_element_type.317
  577.8 1.9 convert_element_type.321
  579.6 1.4 dynamic-slice_reduce_fusion.7
  581.2 1.4 dynamic-slice_reduce_fusion.6
  582.7 1.5 dynamic-slice_reduce_fusion.13
  584.2 1.5 dynamic-slice_reduce_fusion.8
  585.7 40.3 %all-reduce.10 = (bf16[2,192]{0,1:T(8,128)(2,1)S(1)}, bf16[192]{0:T(256)(128)(2,1)S(1)}, bf16[192]{0:T(256)(128)(2,1)S(1)}, bf16[192]{0:T(256)(128)(2,1)S(1)}, b...) all-reduce(bf16[2,192]{0,1:T(8,128)(2,1)S(1)} %bitcast.239, ...), channel_id=1, replica_groups=mesh['dp'=8,'fsdp'=4] {'dp'}, use_global_device_ids=true, to_apply=%region_20.21 | all-reduce | flops 2688 | bytes 10752 | tf_op jit(solution)/shard_map/psum | solution.py:427
  631.8 88.6 %all-reduce.17.cloned.1.call-done = (bf16[192,768]{1,0:T(8,128)(2,1)}, bf16[192,768]{1,0:T(8,128)(2,1)}, bf16[192,768]{1,0:T(8,128)(2,1)}, bf16[192,768]{1,0:T(8...) async-done(((bf16[192,768]{1,0:T(8,128)(2,1)}, bf16[192,768]{1,0:T(8,128)(2,1)}, bf16[192,768]{1,0:T(8,128)(2,1)}, bf16[192,768]{1,0:T(8,128)(2,1)}, ...) | async-done | bytes 3538960 | tf_op jit(solution)/shard_map/psum | solution.py:420
  720.4 1.9 convert_element_type.297
  722.3 1.9 convert_element_type.301
  724.2 1.8 convert_element_type.303
  726.0 1.8 convert_element_type.307
  727.8 1.7 convert_element_type.318
  729.5 1.6 convert_element_type.322
  (274 shorter events, 53.4 us)
Async XLA Ops:
  7.2 4.2 copy-start.37
  7.2 5.5 copy-start.41
  7.2 5.7 copy-start.42
  7.2 5.9 copy-start.43
  7.2 6.1 copy-start.44
  7.2 6.4 copy-start.45
  7.3 6.6 copy-start.46
  7.3 6.8 copy-start.47
  7.3 7.0 copy-start.48
  7.3 21.4 %copy-start.38 = (bf16[768]{0:T(1024)(128)(2,1)S(1)}, bf16[768]{0:T(1024)(128)(2,1)}, u32[]{:S(2)}) copy-start(bf16[768]{0:T(1024)(128)(2,1)} %param.39) | copy-start | bytes 4612
  7.3 27.2 %copy-start.39 = (bf16[2,192]{1,0:T(2,128)(2,1)S(1)}, bf16[2,192]{1,0:T(2,128)(2,1)}, u32[]{:S(2)}) copy-start(bf16[2,192]{1,0:T(2,128)(2,1)} %param.28) | copy-start | bytes 2308
  7.3 32.9 %copy-start.1 = (bf16[2,128,768]{2,1,0:T(8,128)(2,1)S(1)}, bf16[2,128,768]{2,1,0:T(8,128)(2,1)}, u32[]{:S(2)}) copy-start(bf16[2,128,768]{2,1,0:T(8,128)(2,1)} %param.27) | copy-start | bytes 1179652
  7.3 33.8 %copy-start.40 = (s32[2,128]{1,0:T(2,128)S(1)}, s32[2,128]{1,0:T(2,128)}, u32[]{:S(2)}) copy-start(s32[2,128]{1,0:T(2,128)} %param.26) | copy-start | bytes 3076
  7.3 34.9 %copy-start.49 = (s32[2]{0:T(128)S(1)}, s32[2]{0:T(128)}, u32[]{:S(2)}) copy-start(s32[2]{0:T(128)} %param.25) | copy-start | bytes 28
  7.3 35.1 %copy-start.18 = (bf16[2,128,768]{2,1,0:T(8,128)(2,1)S(1)}, bf16[2,128,768]{2,1,0:T(8,128)(2,1)}, u32[]{:S(2)}) copy-start(bf16[2,128,768]{2,1,0:T(8,128)(2,1)} %param.24) | copy-start | bytes 1179652
  7.3 35.2 %all-gather.9.cloned.1.call-start = ((), (), s32[]{:S(2)}) async-start(), calls=%async_computation | async-start | bytes 1474560 | tf_op jit(solution)/shard_map/all_gather | solution.py:195
  8.1 41.0 %all-gather.11.cloned.1.call-start = ((), (), s32[]{:S(2)}) async-start(), calls=%async_computation.1 | async-start | bytes 1474560 | tf_op jit(solution)/shard_map/all_gather | solution.py:193
  8.8 59.3 %all-gather.13.cloned.1.call-start = ((), (), s32[]{:S(2)}) async-start(), calls=%async_computation.2 | async-start | bytes 1474560 | tf_op jit(solution)/shard_map/all_gather | solution.py:194
  9.6 77.5 %all-gather.15.cloned.1.call-start = ((), (), s32[]{:S(2)}) async-start(), calls=%async_computation.3 | async-start | bytes 1474560 | tf_op jit(solution)/shard_map/all_gather | solution.py:196
  10.1 115.8 %all-gather.17.cloned.1.call-start = ((), (), s32[]{:S(2)}) async-start(), calls=%async_computation.4 | async-start | bytes 5898240 | tf_op jit(solution)/shard_map/all_gather | solution.py:203
  10.7 154.0 %all-gather.19.cloned.1.call-start = ((), (), s32[]{:S(2)}) async-start(), calls=%async_computation.5 | async-start | bytes 5898240 | tf_op jit(solution)/shard_map/all_gather | solution.py:204
  11.3 519.6 %all-reduce.19.cloned.1.call-start = ((), (), s32[]{:S(2)}) async-start(), calls=%async_computation.7 | async-start | bytes 28356608
  70.4 4.0 copy-start.19
  75.0 4.0 copy-start.19
  89.3 75.5 %copy-start.23 = (f32[256]{0:T(256)}, f32[256]{0:T(256)S(1)}, u32[]{:S(2)}) copy-start(f32[256]{0:T(256)S(1)} %add_rsqrt_fusion.1) | copy-start | bytes 3076
  125.9 38.9 %copy-start.36 = (f32[768]{0:T(1024)S(1)}, f32[768]{0:T(1024)}, u32[]{:S(2)}) copy-start(f32[768]{0:T(1024)} %convert_element_type.277) | copy-start | bytes 9220
  164.8 4.7 copy-start.22
  164.8 6.5 copy-start.35
  164.8 11.2 %slice-start.2 = ((s8[4718592]{0:T(1024)(128)(4,1)}), s8[4194304]{0:T(1024)(128)(4,1)S(1)}, s32[]{:S(2)}) async-start(s8[4718592]{0:T(1024)(128)(4,1)} %bitcast.244), calls=%async_computation.10 | async-start | bytes 8388608
  169.2 2.9 copy-start.6
  169.5 6.5 slice-start.3
  171.3 4.7 copy-start.52
  172.1 3.9 copy-start.51
  172.1 10.4 %slice-start = ((s8[4718592]{0:T(1024)(128)(4,1)}), s8[4194304]{0:T(1024)(128)(4,1)S(1)}, s32[]{:S(2)}) async-start(s8[4718592]{0:T(1024)(128)(4,1)} %bitcast.242), calls=%async_computation.8 | async-start | bytes 8388608
  176.0 2.8 copy-start.24
  176.0 6.5 slice-start.1
  182.5 3.1 copy-start.8
  184.8 2.4 copy-start.5
  187.2 2.4 copy-start.21
  198.9 1.8 copy-start.13
  210.9 6.9 copy-start.7
  211.3 2.7 copy-start.12
  214.0 8.4 %copy-start.9 = (bf16[2,128,12,64]{1,0,3,2:T(2,128)(2,1)}, bf16[2,128,12,64]{1,0,3,2:T(2,128)(2,1)S(1)}, u32[]{:S(2)}) copy-start(bf16[2,128,12,64]{1,0,3,2:T(2,128)(2,1)S(1)} %copy.90) | copy-start | bytes 1179652
  223.0 6.9 copy-start.34
  224.9 7.7 %copy-start.2 = (bf16[768,768]{1,0:T(8,128)(2,1)S(1)}, bf16[768,768]{1,0:T(8,128)(2,1)}, u32[]{:S(2)}) copy-start(bf16[768,768]{1,0:T(8,128)(2,1)} %all-gather.13.cloned.1.call-done) | copy-start | bytes 3538948
  230.6 2.1 copy-start.11
  230.6 2.6 copy-start.10
  230.6 2.6 copy-start.15
  232.6 1.9 copy-start.50
  250.3 13.1 %copy-start.25 = (bf16[768]{0:T(1024)(128)(2,1)S(1)}, bf16[768]{0:T(1024)(128)(2,1)}, u32[]{:S(2)}) copy-start(bf16[768]{0:T(1024)(128)(2,1)} %get-tuple-element.325) | copy-start | bytes 4612
  250.3 13.7 %copy-start.3 = (bf16[1,4,147456]{2,1,0:T(4,128)(2,1)S(1)}, bf16[1,4,147456]{2,1,0:T(4,128)(2,1)}, u32[]{:S(2)}) copy-start(bf16[1,4,147456]{2,1,0:T(4,128)(2,1)} %transpose_reshape.65) | copy-start | bytes 3538948
  258.5 6.7 copy-start.4
  264.0 3.7 copy-start
  267.7 4.5 copy-start.33
  267.7 5.8 copy-start.31
  267.7 7.2 copy-start.32
  267.8 8.5 %copy-start.30 = (bf16[1,4,192]{2,1,0:T(4,128)(2,1)S(1)}, bf16[1,4,192]{2,1,0:T(4,128)(2,1)}, u32[]{:S(2)}) copy-start(bf16[1,4,192]{2,1,0:T(4,128)(2,1)} %transpose_reshape.78) | copy-start | bytes 4612
  267.8 9.9 %copy-start.26 = (bf16[1,4,192]{2,1,0:T(4,128)(2,1)S(1)}, bf16[1,4,192]{2,1,0:T(4,128)(2,1)}, u32[]{:S(2)}) copy-start(bf16[1,4,192]{2,1,0:T(4,128)(2,1)} %transpose_reshape.79) | copy-start | bytes 4612
  267.8 10.5 %copy-start.27 = (bf16[1,4,192]{2,1,0:T(4,128)(2,1)S(1)}, bf16[1,4,192]{2,1,0:T(4,128)(2,1)}, u32[]{:S(2)}) copy-start(bf16[1,4,192]{2,1,0:T(4,128)(2,1)} %transpose_reshape.68) | copy-start | bytes 4612
  267.8 11.8 %copy-start.28 = (bf16[1,4,192]{2,1,0:T(4,128)(2,1)S(1)}, bf16[1,4,192]{2,1,0:T(4,128)(2,1)}, u32[]{:S(2)}) copy-start(bf16[1,4,192]{2,1,0:T(4,128)(2,1)} %transpose_reshape.69) | copy-start | bytes 4612
  267.8 13.2 %copy-start.29 = (bf16[1,4,192]{2,1,0:T(4,128)(2,1)S(1)}, bf16[1,4,192]{2,1,0:T(4,128)(2,1)}, u32[]{:S(2)}) copy-start(bf16[1,4,192]{2,1,0:T(4,128)(2,1)} %transpose_reshape.70) | copy-start | bytes 4612
  283.8 436.5 %all-reduce.17.cloned.1.call-start = ((), (), s32[]{:S(2)}) async-start(), calls=%async_computation.6 | async-start | bytes 7077888 | tf_op jit(solution)/shard_map/psum | solution.py:420
  720.4 7.5 %copy-start.17 = (bf16[192,3072]{1,0:T(8,128)(2,1)S(1)}, bf16[192,3072]{1,0:T(8,128)(2,1)}, u32[]{:S(2)}) copy-start(bf16[192,3072]{1,0:T(8,128)(2,1)} %get-tuple-element.381) | copy-start | bytes 3538948
  722.3 7.2 copy-start.16
  (5 other events, 4.5 us)
Sparse Core Ops, SparseCore 0:
  9.7 20.3 all-gather.8
  31.6 17.4 all-gather.10
  50.7 17.4 all-gather.12
  69.6 17.4 all-gather.14
  88.4 37.4 all-gather.16
  127.3 37.4 all-gather.18
  284.0 246.9 all-reduce.18
  579.8 140.5 all-reduce.16
where the time goes:
time: 748 us; the launch traced here: 738 us
  waiting for transfers between devices  430 us (57%)
  local copies, waits for them, and re-layouts  135 us (18%)
  blocking collectives  64.1 us (9%)
  matrix products  50.8 us (7%)
  other arithmetic  24.9 us (3%)
  loops' own time  17.1 us (2%)
  between operations  16.1 us (2%)
    unnamed x9, waiting for transfers between devices  251 us
    psum x1, waiting for transfers between devices, local(): lax.psum(share_wq.astype(jnp.bfloat16), 'dp').astype(jnp.float32)  88.6 us
    slice x6, local copies, waits for them, and re-layouts, unpack_terms(): piece = packed[:, offset:offset + width_each]  47.4 us
    psum x1, blocking collectives, local(): lax.psum(share_table.astype(jnp.bfloat16), 'dp').astype(jnp.float32)  40.3 us
    all_gather x1, waiting for transfers between devices, local(): lax.all_gather(ffn_local[0], 'fsdp', axis=0, tiled=True)  36.6 us
    another operation x16, local copies, waits for them, and re-layouts, pack_terms(): blocks = moved.reshape(fsdp_count, dp_count, -1).swapaxes(0, 1)  33 us
    unnamed x140, local copies, waits for them, and re-layouts  29.2 us
    all_gather x1, waiting for transfers between devices, local(): lax.all_gather(ffn_local[1], 'fsdp', axis=0, tiled=True)  27 us
  transfers between devices with their start and end apart: 8, of which 7 were waited for; matrix products, arithmetic and copies ran while one was open for 6% of the time, Pallas kernels for 0%

commit v1 on v0

v1 whole, which is shorter than its diff:
```python
from functools import partial

import jax
import jax.numpy as jnp
from jax import lax
from jax.experimental import pallas as pl
from jax.experimental.pallas import tpu as pltpu
from jax.sharding import PartitionSpec as P

HEAD_DIM = 64
norm_eps = 1e-12
masked_score = -1e30
f32 = jnp.float32
bf16 = jnp.bfloat16

BQ, BV, BO, G1, S1, BD, G2, S2, TB, BU = 0, 1, 2, 3, 4, 5, 6, 7, 8, 10
VEC_ROWS = 16
COST = 1024
ATTEND_COST = 1024
VMEM_LIMIT = 56 * 1024 * 1024


def dot(a, b):
    return jnp.dot(a, b, preferred_element_type=f32)


def dot_nt(a, b):
    return lax.dot_general(a, b, (((1,), (1,)), ((), ())), preferred_element_type=f32)


def dot_tn(a, b):
    return lax.dot_general(a, b, (((0,), (0,)), ((), ())), preferred_element_type=f32)


def swap(x, axis, distance):
    count = lax.axis_size(axis)
    with jax.named_scope(f"swap_{axis}{distance}"):
        return lax.ppermute(x, axis, [(i, i ^ distance) for i in range(count)])


def half_columns(x, bit):
    width = x.shape[1] // 2
    return lax.dynamic_slice_in_dim(x, bit * width, width, 1)


def tie(x, *others):
    return lax.optimization_barrier((x,) + others)[0]


def piece_slots(where_ref, width, count):
    f, y = where_ref[0], where_ref[1]
    if count == 4:
        return tuple((f ^ n, 0, width) for n in range(4))
    half = width // 2
    low = pl.multiple_of(y * half, 128)
    high = pl.multiple_of((1 - y) * half, 128)
    return (
        (f, 0, width),
        (f ^ 1, 0, width),
        (f ^ 2, low, half),
        (f ^ 2, high, half),
        (f ^ 3, low, half),
        (f ^ 3, high, half),
    )


def start_rows(pieces, where_ref, first_row, rows, width, target, sems, base):
    copies = []
    for n, (piece, (shard, col, cols)) in enumerate(zip(pieces, piece_slots(where_ref, width, len(pieces)))):
        copy = pltpu.make_async_copy(
            piece.at[pl.ds(first_row, rows), :],
            target.at[pl.ds(pl.multiple_of(shard * rows, 8), rows), pl.ds(col, cols)],
            sems.at[base + n],
        )
        copy.start()
        copies.append(copy)
    return copies


def wait_all(copies):
    for copy in copies:
        copy.wait()


def call(kernel, out_shapes, n_smem, n_vmem, n_any, scratch, name, cost=COST):
    return pl.pallas_call(
        kernel,
        out_shape=out_shapes,
        in_specs=[pl.BlockSpec(memory_space=pltpu.SMEM)] * n_smem
        + [pl.BlockSpec(memory_space=pltpu.VMEM)] * n_vmem
        + [pl.BlockSpec(memory_space=pl.ANY)] * n_any,
        out_specs=jax.tree.map(lambda _: pl.BlockSpec(memory_space=pltpu.VMEM), out_shapes),
        scratch_shapes=scratch,
        compiler_params=pltpu.CompilerParams(vmem_limit_bytes=VMEM_LIMIT),
        cost_estimate=pl.CostEstimate(flops=cost, bytes_accessed=cost, transcendentals=0),
        name=name,
    )


def sds(shape, dtype):
    return jax.ShapeDtypeStruct(shape, dtype)


def norm_forward(residual):
    average = jnp.mean(residual, axis=-1, keepdims=True)
    centred = residual - average
    inverse = lax.rsqrt(jnp.mean(centred * centred, axis=-1, keepdims=True) + norm_eps)
    return centred * inverse, inverse


def norm_backward(grad_out, normal, inverse, gain):
    scaled = grad_out * gain
    first = jnp.mean(scaled, axis=-1, keepdims=True)
    second = jnp.mean(scaled * normal, axis=-1, keepdims=True)
    return inverse * (scaled - first - normal * second)


def column_sum(x):
    return jnp.sum(x, axis=0, keepdims=True)


def head_mask(h, rows):
    lane = lax.broadcasted_iota(jnp.int32, (rows, 2 * HEAD_DIM), 1)
    return (lane // HEAD_DIM) == h


def soft_rows(q_pair, k_pair, dead, mask):
    scale = HEAD_DIM ** (-0.5)
    q_head = jnp.where(mask, q_pair, jnp.zeros_like(q_pair))
    scores = dot_nt(q_head, k_pair) * scale
    scores = jnp.where(dead, masked_score, scores)
    expo = jnp.exp(scores - jnp.max(scores, axis=-1, keepdims=True))
    return expo / jnp.sum(expo, axis=-1, keepdims=True)


def pack_kernel(where_ref, q_ref, k_ref, v_ref, o_ref, up_ref, *refs):
    vectors, table_ref, b_up_ref = refs[:TB], refs[TB], refs[TB + 1]
    all_ref, half_ref, half_up_ref, spread = refs[TB + 2 :]
    rows, width = q_ref.shape
    f, y = where_ref[0], where_ref[1]
    half = half_ref.shape[1]
    half_up = half_up_ref.shape[1]
    cols = pl.ds(pl.multiple_of(y * half, 128), half)
    for m, ref in enumerate((q_ref, k_ref, v_ref, o_ref)):
        at = slice(m * rows, (m + 1) * rows)
        half_ref[at, :] = ref[:, cols]
        all_ref[at, :] = ref[...]
    half_up_ref[...] = up_ref[:, pl.ds(pl.multiple_of(y * half_up, 128), half_up)]
    spread[...] = jnp.zeros(spread.shape, f32)
    table = table_ref[...].astype(f32)
    for k in range(4):

        @pl.when(f == k)
        def _():
            mine = slice(k * rows, (k + 1) * rows)
            for n, ref in enumerate(vectors):
                spread[n : n + 1, mine] = ref[...].astype(f32).reshape(1, rows)
            spread[TB : TB + 2, mine] = table
            spread[BU + k : BU + k + 1, :] = b_up_ref[...].astype(f32).reshape(1, width)

    all_ref[4 * rows :, :] = spread[...].astype(bf16)
    half_ref[4 * rows :, :] = spread[:, cols].astype(bf16)


def put_blocks(value, f, blocks, targets, at):
    rows = value.shape[1] // 4
    for i in range(4):
        blocks[i] = value[:, i * rows : (i + 1) * rows]
    for n, target in enumerate(targets):
        target[at] = blocks[f ^ n]
        target[at + 1] = blocks[f ^ 2 ^ n]


def attend_kernel(
    where_ref,
    species_ref,
    x_ref,
    ids_ref,
    *refs,
    length,
):
    pieces = refs[:6]
    (
        q_ref,
        k_ref,
        v_ref,
        own_ref,
        share_ref,
        n1_ref,
        inv_ref,
        low_ref,
        low_own_ref,
        low_share_ref,
        vec_ref,
        wbuf,
        vbuf,
        abuf,
        blocks,
        sems,
    ) = refs[6:]
    f = where_ref[0]
    tokens, width = x_ref.shape
    cells = tokens // length
    rows = width // 4
    copies = []
    for m in range(4):
        copies.append(
            start_rows(pieces, where_ref, m * rows, rows, width, wbuf.at[m], sems, 6 * m)
        )
    vec_copies = start_rows(pieces, where_ref, 4 * rows, VEC_ROWS, width, vbuf, sems, 24)
    wait_all(vec_copies)
    vec = vbuf[0:VEC_ROWS, :].astype(f32)
    for i in range(1, 4):
        vec = vec + vbuf[i * VEC_ROWS : (i + 1) * VEC_ROWS, :].astype(f32)
    vec_ref[...] = vec
    summed = []
    for c in range(cells):
        offset = jnp.where(species_ref[c] == 1, vec[TB + 1 : TB + 2, :], vec[TB : TB + 1, :])
        summed.append(x_ref[c * length : (c + 1) * length, :].astype(f32) + offset)
    summed = jnp.concatenate(summed, axis=0)
    summed_low = summed.astype(bf16)
    put_blocks(summed_low, f, blocks, (own_ref, share_ref), 2)
    wait_all(copies[0])
    q_ref[...] = (dot(summed_low, wbuf[0]) + vec[BQ : BQ + 1, :]).astype(bf16)
    wait_all(copies[1])
    k_ref[...] = dot(summed_low, wbuf[1]).astype(bf16)
    wait_all(copies[2])
    v_ref[...] = (dot(summed_low, wbuf[2]) + vec[BV : BV + 1, :]).astype(bf16)
    pair = 2 * HEAD_DIM
    masks = [head_mask(h, length) for h in range(2)]
    for c in range(cells):
        at = slice(c * length, (c + 1) * length)
        dead = jnp.broadcast_to(ids_ref[c : c + 1, :], (length, length)) == 0
        for p in range(width // pair):
            cols = slice(p * pair, (p + 1) * pair)
            q_pair, k_pair, v_pair = q_ref[at, cols], k_ref[at, cols], v_ref[at, cols]
            total = None
            for h in range(2):
                soft = soft_rows(q_pair, k_pair, dead, masks[h]).astype(bf16)
                part = dot(soft, jnp.where(masks[h], v_pair, jnp.zeros_like(v_pair)))
                total = part if total is None else total + part
            abuf[at, cols] = total.astype(bf16)
    attended = abuf[...]
    put_blocks(attended, f, blocks, (own_ref, share_ref), 0)
    wait_all(copies[3])
    branch = dot(attended, wbuf[3]) + vec[BO : BO + 1, :]
    normal, inverse = norm_forward(summed + branch)
    n1_ref[...] = normal
    inv_ref[...] = jnp.broadcast_to(inverse, inv_ref.shape)
    low = (normal * vec[G1 : G1 + 1, :] + vec[S1 : S1 + 1, :]).astype(bf16)
    low_ref[...] = low
    put_blocks(low, f, blocks, (low_own_ref, low_share_ref), 0)


def up_kernel(where_ref, low_ref, vec_ref, *refs):
    pieces = refs[:6]
    act_ref, own_ref, near_ref, across_ref, slope_ref, wbuf, sems = refs[6:]
    f = where_ref[0]
    hidden = wbuf.shape[1]
    rows = wbuf.shape[0] // 4
    block = hidden // 4
    wait_all(start_rows(pieces, where_ref, 0, rows, hidden, wbuf, sems, 0))
    low = low_ref[...]
    for j in range(4):
        up = dot(low, wbuf[:, j * block : (j + 1) * block]) + vec_ref[BU + j : BU + j + 1, :]
        half_cdf = 0.5 * (1.0 + lax.erf(up * (0.5**0.5)))
        density = jnp.exp(-0.5 * up * up) * 0.3989422804014327
        act_ref[j] = (up * half_cdf).astype(bf16)
        slope_ref[j] = half_cdf + up * density
    own_ref[...] = act_ref[f]
    near_ref[...] = act_ref[f ^ 1]
    across_ref[0] = act_ref[f ^ 2]
    across_ref[1] = act_ref[f ^ 3]


def down_kernel(where_ref, act_ref, n1_ref, vec_ref, cot_ref, *refs):
    pieces = refs[:4]
    out_ref, gsec_ref, glow_ref, sm_ref, wbuf, sems = refs[4:]
    rows = wbuf.shape[0] // 4
    width = wbuf.shape[1]
    copies = start_rows(pieces, where_ref, 0, rows, width, wbuf, sems, 0)
    vec = vec_ref[...]
    wait_all(copies)
    branch = None
    for j in range(4):
        part = dot(act_ref[j], wbuf[j * rows : (j + 1) * rows, :])
        branch = part if branch is None else branch + part
    normed = n1_ref[...] * vec[G1 : G1 + 1, :] + vec[S1 : S1 + 1, :]
    normal, inverse = norm_forward(normed + (branch + vec[BD : BD + 1, :]))
    gain = vec[G2 : G2 + 1, :]
    out_ref[...] = (normal * gain + vec[S2 : S2 + 1, :]).astype(bf16)
    cot = cot_ref[...].astype(f32)
    grad = norm_backward(cot, normal, inverse, gain)
    gsec_ref[...] = grad
    low = grad.astype(bf16)
    glow_ref[...] = low
    sm_ref[0:1, :] = column_sum(cot * normal)
    sm_ref[1:2, :] = column_sum(cot)
    sm_ref[2:3, :] = column_sum(low.astype(f32))
    sm_ref[3:8, :] = jnp.zeros((5, width), f32)


def near_up_kernel(where_ref, own_ref, got_ref, *refs):
    rights, got_rights, outs = refs[:4], refs[4:8], refs[8:]
    block = rights[0].shape[1]
    for slot, out in ((1, outs[0]), (0, outs[1])):
        for j in range(4):
            total = dot_tn(own_ref[slot], rights[j][...]) + dot_tn(got_ref[slot], got_rights[j][...])
            out[:, j * block : (j + 1) * block] = total.astype(bf16)


def near_attn_kernel(where_ref, own_ref, got_ref, *refs):
    rights, got_rights = refs[:4], refs[4:8]
    send_ref, keep_ref, send_y_ref, keep_y_ref = refs[8:]
    y = where_ref[1]
    rows = own_ref.shape[2]

    def block(left, n):
        return dot_tn(own_ref[left], rights[n][...]) + dot_tn(got_ref[left], got_rights[n][...])

    for slot, ref in ((1, send_ref), (0, keep_ref)):
        ref[0:rows, :] = block(slot, 0).astype(bf16)
        ref[rows : 2 * rows, :] = block(2 + slot, 1).astype(bf16)
    for ref, first in ((send_y_ref, 1 - y), (keep_y_ref, y)):
        right = jnp.where(first == 0, rights[2][...], rights[3][...])
        got_right = jnp.where(first == 0, got_rights[2][...], got_rights[3][...])
        for slot in (0, 1):
            total = dot_tn(own_ref[2 + slot], right) + dot_tn(got_ref[2 + slot], got_right)
            ref[slot] = total.astype(bf16)


def down_grad_kernel(where_ref, *refs):
    lefts, rights, outs = refs[:4], refs[4:8], refs[8:]
    z = where_ref[2]
    rows = outs[0].shape[0]
    for half, out in ((1 - z, outs[0]), (z, outs[1])):
        cols = pl.ds(pl.multiple_of(half * rows, 128), rows)
        total = None
        for n, (left, right) in enumerate(zip(lefts, rights)):
            part = dot_tn(left[0, :, cols] if n == 2 else left[:, cols], right[...])
            total = part if total is None else total + part
        out[...] = total.astype(bf16)


def hidden_back_kernel(where_ref, glow_ref, slope_ref, *refs):
    pieces = refs[:4]
    guis, sm_ref, wbuf, sems = refs[4:8], refs[8], refs[9], refs[10]
    rows = wbuf.shape[0] // 4
    width = wbuf.shape[1]
    wait_all(start_rows(pieces, where_ref, 0, rows, width, wbuf, sems, 0))
    glow = glow_ref[...]
    for j in range(4):
        grad = dot_nt(glow, wbuf[j * rows : (j + 1) * rows, :]) * slope_ref[j]
        low = grad.astype(bf16)
        guis[j][...] = low
        sm_ref[j : j + 1, :] = column_sum(low.astype(f32))
    sm_ref[4:8, :] = jnp.zeros((4, rows), f32)


def norm_back_kernel(where_ref, gsec_ref, n1_ref, inv_ref, vec_ref, *refs):
    guis, pieces, attn_pieces = refs[:4], refs[4:10], refs[10:16]
    gres_ref, gbr_ref, gatt_ref, sm_ref, wbuf, obuf, sems = refs[16:]
    rows = wbuf.shape[0] // 4
    hidden = wbuf.shape[1]
    width = obuf.shape[1]
    copies = start_rows(pieces, where_ref, 0, rows, hidden, wbuf, sems, 0)
    out_copies = start_rows(attn_pieces, where_ref, 3 * rows, rows, width, obuf, sems, 6)
    wait_all(copies)
    block = hidden // 4
    grad_normed = gsec_ref[...]
    for j in range(4):
        grad_normed = grad_normed + dot_nt(guis[j][...], wbuf[:, j * block : (j + 1) * block])
    normal = n1_ref[...]
    grad = norm_backward(grad_normed, normal, inv_ref[:, 0:1], vec_ref[G1 : G1 + 1, :])
    gres_ref[...] = grad
    low = grad.astype(bf16)
    gbr_ref[...] = low
    sm_ref[0:1, :] = column_sum(grad_normed * normal)
    sm_ref[1:2, :] = column_sum(grad_normed)
    sm_ref[2:3, :] = column_sum(low.astype(f32))
    sm_ref[3:8, :] = jnp.zeros((5, width), f32)
    wait_all(out_copies)
    gatt_ref[...] = dot_nt(low, obuf[...]).astype(bf16)


def attend_back_kernel(q_ref, k_ref, v_ref, gatt_ref, ids_ref, gq_ref, gk_ref, gv_ref, *, length):
    tokens, width = q_ref.shape
    cells = tokens // length
    scale = HEAD_DIM ** (-0.5)
    pair = 2 * HEAD_DIM
    masks = [head_mask(h, length) for h in range(2)]
    for c in range(cells):
        at = slice(c * length, (c + 1) * length)
        dead = jnp.broadcast_to(ids_ref[c : c + 1, :], (length, length)) == 0
        for p in range(width // pair):
            cols = slice(p * pair, (p + 1) * pair)
            q_pair, k_pair, v_pair = q_ref[at, cols], k_ref[at, cols], v_ref[at, cols]
            g_pair = gatt_ref[at, cols]
            zero = jnp.zeros_like(q_pair)
            gq = gk = gv = jnp.zeros((length, pair), f32)
            for h in range(2):
                mask = masks[h]
                soft = soft_rows(q_pair, k_pair, dead, mask)
                g_head = jnp.where(mask, g_pair, zero)
                grad_soft = dot_nt(g_head, v_pair)
                inner = jnp.sum(soft * grad_soft, axis=-1, keepdims=True)
                grad_scores = (soft * (grad_soft - inner)).astype(bf16)
                gv = gv + dot_tn(soft.astype(bf16), g_head)
                gq = gq + dot(grad_scores, jnp.where(mask, k_pair, zero))
                gk = gk + dot_tn(grad_scores, jnp.where(mask, q_pair, zero))
            gq_ref[at, cols] = (gq * scale).astype(bf16)
            gk_ref[at, cols] = (gk * scale).astype(bf16)
            gv_ref[at, cols] = gv.astype(bf16)


def input_back_kernel(
    where_ref, species_ref, gres_ref, gq_ref, gk_ref, gv_ref, sm2_ref, smu_ref, sm1_ref, *refs,
    length,
):
    pieces = refs[:6]
    gin_ref, sm_ref, wbuf, sems = refs[6:]
    tokens, width = gres_ref.shape
    rows = width // 4
    copies = [
        start_rows(pieces, where_ref, m * rows, rows, width, wbuf.at[m], sems, 6 * m)
        for m in range(3)
    ]
    sm_ref[BQ : BQ + 1, :] = column_sum(gq_ref[...].astype(f32))
    sm_ref[BV : BV + 1, :] = column_sum(gv_ref[...].astype(f32))
    sm_ref[BO : BO + 1, :] = sm1_ref[2:3, :]
    sm_ref[G1 : G1 + 2, :] = sm1_ref[0:2, :]
    sm_ref[BD : BD + 1, :] = sm2_ref[2:3, :]
    sm_ref[G2 : G2 + 2, :] = sm2_ref[0:2, :]
    sm_ref[BU : BU + 4, :] = smu_ref[0:4, :]
    sm_ref[BU + 4 : VEC_ROWS, :] = jnp.zeros((VEC_ROWS - BU - 4, width), f32)
    total = gres_ref[...]
    for m, grad in enumerate((gq_ref, gk_ref, gv_ref)):
        wait_all(copies[m])
        total = total + dot_nt(grad[...], wbuf[m])
    gin_ref[...] = total.astype(bf16)
    for s in range(2):
        row = jnp.zeros((1, width), f32)
        for c in range(tokens // length):
            cell = column_sum(total[c * length : (c + 1) * length, :])
            row = row + jnp.where(species_ref[c] == s, cell, jnp.zeros_like(cell))
        sm_ref[TB + s : TB + s + 1, :] = row


def half_rows(x, bit):
    rows = x.shape[-2] // 2
    return lax.dynamic_slice_in_dim(x, bit * rows, rows, x.ndim - 2)


def add(a, b):
    return (a.astype(f32) + b.astype(f32)).astype(bf16)


def scatter_cells(keep, got, dp_index, steps):
    for step in steps:
        bit = (dp_index >> step) & 1
        sent = add(half_rows(keep, 1 - bit), half_rows(got, 1 - bit))
        keep = add(half_rows(keep, bit), half_rows(got, bit))
        got = swap(sent, "dp", 1 << step)
    return keep, got


def gather_cells(total, dp_index, order):
    total = add(total, swap(total, "dp", 1 << order[-1]))
    for step in reversed(order[:-1]):
        bit = (dp_index >> step) & 1
        other = swap(total, "dp", 1 << step)
        total = jnp.where(
            bit == 0,
            jnp.concatenate([total, other], axis=0),
            jnp.concatenate([other, total], axis=0),
        )
    return total


def reduce_cells(keep, got, dp_index, order, done=0):
    return gather_cells(
        add(*scatter_cells(keep, got, dp_index, order[done:-1])), dp_index, order
    )


def local(
    inputs,
    species,
    gene_ids,
    cotangent,
    table,
    w_query,
    b_query,
    w_key,
    w_value,
    b_value,
    w_out,
    b_out,
    gain_one,
    shift_one,
    w_up,
    b_up,
    w_down,
    b_down,
    gain_two,
    shift_two,
):
    cells, length, width = inputs.shape
    tokens = cells * length
    rows = w_query.shape[0]
    hidden = w_up.shape[1]
    shard_hidden = w_down.shape[0]
    shards = lax.axis_size("fsdp")
    f = lax.axis_index("fsdp")
    d = lax.axis_index("dp")
    y_bit = d & 1
    where = jnp.stack([f, y_bit, (d >> 1) & 1]).astype(jnp.int32)
    order = tuple(range((lax.axis_size("dp") - 1).bit_length()))
    other_order = (1, 0) + order[2:]

    packed_rows = shards * rows + VEC_ROWS
    packed, half, half_up = call(
        pack_kernel,
        (
            sds((packed_rows, width), bf16),
            sds((packed_rows, width // 2), bf16),
            sds((rows, hidden // 2), bf16),
        ),
        1,
        7 + TB,
        0,
        [pltpu.VMEM((VEC_ROWS, width), f32)],
        "pack",
    )(
        where,
        w_query,
        w_key,
        w_value,
        w_out,
        w_up,
        b_query,
        b_value,
        b_out,
        gain_one,
        shift_one,
        b_down,
        gain_two,
        shift_two,
        table,
        b_up,
    )
    across = swap(half, "fsdp", 2)
    relayed = swap(across, "dp", 1)
    attn = (
        packed,
        swap(packed, "fsdp", 1),
        across,
        relayed,
        swap(across, "fsdp", 1),
        swap(relayed, "fsdp", 1),
    )
    across_up = swap(tie(half_up, across), "fsdp", 2)
    relayed_up = swap(across_up, "dp", 1)
    up = (
        w_up,
        swap(w_up, "fsdp", 1),
        across_up,
        relayed_up,
        swap(across_up, "fsdp", 1),
    )
    across_down = swap(tie(w_down, across_up), "fsdp", 2)

    x_rows = inputs.reshape(tokens, width)
    cot_rows = cotangent.reshape(tokens, width)
    flat_low = sds((tokens, width), bf16)
    flat = sds((tokens, width), f32)
    small = sds((8, width), f32)
    q, k, v, own_attn, share_attn, n1, inv1, low, low_own, low_share, vec = call(
        partial(attend_kernel, length=length),
        (
            flat_low,
            flat_low,
            flat_low,
            sds((4, tokens, rows), bf16),
            sds((4, tokens, rows), bf16),
            flat,
            sds((tokens, 128), f32),
            flat_low,
            sds((2, tokens, rows), bf16),
            sds((2, tokens, rows), bf16),
            sds((VEC_ROWS, width), f32),
        ),
        2,
        2,
        6,
        [
            pltpu.VMEM((4, width, width), bf16),
            pltpu.VMEM((4 * VEC_ROWS, width), bf16),
            pltpu.VMEM((tokens, width), bf16),
            pltpu.VMEM((4, tokens, rows), bf16),
            pltpu.SemaphoreType.DMA((30,)),
        ],
        "attend",
        ATTEND_COST,
    )(where, species, x_rows, gene_ids, *attn)
    up += (swap(tie(relayed_up, q), "fsdp", 1),)
    act, act_own, act_near, act_across, slope = call(
        up_kernel,
        (
            sds((shards, tokens, shard_hidden), bf16),
            *(sds((tokens, shard_hidden), bf16),) * 2,
            sds((2, tokens, shard_hidden), bf16),
            sds((shards, tokens, shard_hidden), f32),
        ),
        1,
        2,
        6,
        [pltpu.VMEM((width, hidden), bf16), pltpu.SemaphoreType.DMA((6,))],
        "up",
    )(where, low, vec, *up)
    down = (
        w_down,
        swap(w_down, "fsdp", 1),
        across_down,
        swap(tie(across_down, act_own), "fsdp", 1),
    )
    output, gsec, glow, sm2 = call(
        down_kernel,
        (flat_low, flat, flat_low, small),
        1,
        4,
        4,
        [pltpu.VMEM((hidden, width), bf16), pltpu.SemaphoreType.DMA((4,))],
        "down",
    )(where, act, n1, vec, cot_rows, *down)
    act_got = swap(act_across, "fsdp", 2)
    glow_across = swap(glow, "fsdp", 2)
    *guis, smu = call(
        hidden_back_kernel,
        (*(sds((tokens, shard_hidden), bf16),) * 4, sds((8, shard_hidden), f32)),
        1,
        2,
        4,
        [pltpu.VMEM((hidden, width), bf16), pltpu.SemaphoreType.DMA((4,))],
        "hidden_back",
    )(where, glow, slope, *down)
    guis_got = [swap(part, "fsdp", 1) for part in guis]
    gres, gbr, gatt, sm1 = call(
        norm_back_kernel,
        (flat, flat_low, flat_low, small),
        1,
        8,
        12,
        [
            pltpu.VMEM((width, hidden), bf16),
            pltpu.VMEM((width, width), bf16),
            pltpu.SemaphoreType.DMA((12,)),
        ],
        "norm_back",
    )(where, gsec, n1, inv1, vec, *guis, *up, *attn)
    act_all = (
        act_own,
        swap(tie(act_near, gbr), "fsdp", 1),
        act_got,
        swap(tie(act_got, gbr)[1], "fsdp", 1),
    )
    glow_all = (
        glow,
        swap(tie(glow, gbr), "fsdp", 1),
        glow_across,
        swap(tie(glow_across, gbr), "fsdp", 1),
    )
    send_up, keep_up = call(
        near_up_kernel, (sds((rows, hidden), bf16),) * 2, 1, 10, 0, [], "near_up"
    )(tie(where, gbr), low_own, swap(low_share, "fsdp", 1), *guis, *guis_got)
    got_up = swap(send_up, "fsdp", 2)
    down_half = sds((shard_hidden // 2, width), bf16)
    send_down, keep_down = call(down_grad_kernel, (down_half,) * 2, 1, 8, 0, [], "down_grad")(
        tie(where, send_up), *act_all, *glow_all
    )
    got_down = swap(send_down, "dp", 2)
    grad_down = reduce_cells(keep_down, got_down, d, other_order, 1)
    gq, gk, gv = call(
        partial(attend_back_kernel, length=length),
        (flat_low, flat_low, flat_low),
        0,
        5,
        0,
        [],
        "attend_back",
    )(q, k, v, tie(gatt, keep_down), gene_ids)
    grad_up = reduce_cells(keep_up, got_up, d, order)
    rights = [gbr, gv, gq, gk]
    rights_got = [swap(right, "fsdp", 1) for right in rights]
    gin, sm = call(
        partial(input_back_kernel, length=length),
        (flat_low, sds((VEC_ROWS, width), f32)),
        2,
        7,
        6,
        [pltpu.VMEM((3, width, width), bf16), pltpu.SemaphoreType.DMA((18,))],
        "input_back",
    )(where, species, gres, gq, gk, gv, sm2, smu, sm1, *attn)
    pair = sds((2 * rows, width), bf16)
    both = sds((2, rows, width), bf16)
    send_ov, keep_ov, send_qk, keep_qk = call(
        near_attn_kernel, (pair, pair, both, both), 1, 10, 0, [], "near_attn"
    )(tie(where, gin, got_down), own_attn, swap(share_attn, "fsdp", 1), *rights, *rights_got)
    got_ov = swap(tie(send_ov, got_up), "fsdp", 2)
    grad_ov = reduce_cells(keep_ov, got_ov, d, order)
    keep_qk, got_qk = scatter_cells(keep_qk, swap(send_qk, "dp", 1), d, order[1:-1])
    sent_qk = add(keep_qk[1], got_qk[1])
    grad_qk = gather_cells(
        (
            keep_qk[0].astype(f32) + got_qk[0].astype(f32) + swap(sent_qk, "fsdp", 2).astype(f32)
        ).astype(bf16),
        d,
        order,
    )

    sm = tie(sm, got_ov)
    sm = sm + swap(sm, "fsdp", 1)
    sm = sm + swap(sm, "fsdp", 2)
    for step in order:
        sm = sm + swap(sm, "dp", 1 << step)
    mine = lax.dynamic_slice_in_dim(sm, f * rows, rows, 1)
    b_up_grad = lax.dynamic_slice_in_dim(sm, BU + f, 1, 0)[0]

    return (
        output.reshape(inputs.shape),
        gin.reshape(inputs.shape),
        mine[TB : TB + 2],
        grad_qk[:rows].astype(f32),
        mine[BQ],
        grad_qk[rows:].astype(f32),
        grad_ov[rows:].astype(f32),
        mine[BV],
        grad_ov[:rows].astype(f32),
        mine[BO],
        mine[G1],
        mine[S1],
        grad_up.astype(f32),
        b_up_grad,
        grad_down.astype(f32),
        mine[BD],
        mine[G2],
        mine[S2],
    )


def solution(mesh):
    cells = P(("dp", "fsdp"), None, None)
    vector = P("fsdp")
    matrix = P("fsdp", None)
    table = P(None, "fsdp")
    return jax.shard_map(
        local,
        mesh=mesh,
        in_specs=(
            cells,
            P(("dp", "fsdp")),
            P(("dp", "fsdp"), None),
            cells,
            table,
            matrix,
            vector,
            matrix,
            matrix,
            vector,
            matrix,
            vector,
            vector,
            vector,
            matrix,
            vector,
            matrix,
            vector,
            vector,
            vector,
        ),
        out_specs=(
            cells,
            cells,
            table,
            matrix,
            vector,
            matrix,
            matrix,
            vector,
            matrix,
            vector,
            vector,
            vector,
            matrix,
            vector,
            matrix,
            vector,
            vector,
            vector,
        ),
        check_vma=False,
    )
```

time: 748 us -> 247 us (0.33); the launches traced: 738 us -> 247 us
  waiting for transfers between devices: 430 us -> 101 us
  local copies, waits for them, and re-layouts: 135 us -> 8.21 us
  Pallas kernels: 0 us -> 73.4 us
  blocking collectives: 64.1 us -> 0 us
  starting transfers between devices: 0.31 us -> 53.8 us
  matrix products: 50.8 us -> 0 us
  loops' own time: 17.1 us -> 0 us
  other arithmetic: 24.9 us -> 9.34 us
  between operations: 16.1 us -> 1.12 us
    unnamed x9 -> x0, waiting for transfers between devices: 251 us -> none
    ppermute x0 -> x57, waiting for transfers between devices: none -> 101 us  [swap(): return lax.ppermute(x, axis, [(i, i ^ distance) for i in range(count)])]
    all_gather x6 -> x0, waiting for transfers between devices: 91.2 us -> none  [the longest x1 36.6 us: local(): lax.all_gather(ffn_local[0], 'fsdp', axis=0, tiled=True)]
    psum x1 -> x0, waiting for transfers between devices: 88.6 us -> none  [local(): lax.psum(share_wq.astype(jnp.bfloat16), 'dp').astype(jnp.float32)]
    pallas_call x0 -> x11, Pallas kernels: none -> 73.4 us  [the longest x1 11.9 us: local(): call(partial(attend_kernel, length=length), (flat_low, flat_low, flat_low...]
    ppermute x0 -> x57, starting transfers between devices: none -> 53.8 us  [swap(): return lax.ppermute(x, axis, [(i, i ^ distance) for i in range(count)])]
    dot_general x34 -> x0, matrix products: 50.8 us -> none  [the longest x6 12.7 us: transposed_dot(): jnp.einsum('ti,tj->ij', left_rows, right_rows, preferred_element_type=jnp...]
    slice x6 -> x2, local copies, waits for them, and re-layouts: 47.4 us -> 1.32 us  [the longest x1 0.67 us: local(): mine[S2]]
  transfers between devices with their start and end apart: 8 -> 57, of which waited for: 7 -> 20; matrix products, arithmetic and copies ran while one was open for 6% -> 4% of each run, Pallas kernels for 0% -> 28%
where the time goes in v1:
time: 247 us
  waiting for transfers between devices  101 us (41%)
  Pallas kernels  73.4 us (30%)
  starting transfers between devices  53.8 us (22%)
  other arithmetic  9.34 us (4%)
  local copies, waits for them, and re-layouts  8.21 us (3%)
    ppermute x57, waiting for transfers between devices, swap(): return lax.ppermute(x, axis, [(i, i ^ distance) for i in range(count)])  101 us
    ppermute x57, starting transfers between devices, swap(): return lax.ppermute(x, axis, [(i, i ^ distance) for i in range(count)])  53.8 us
    pallas_call x1, Pallas kernels, local(): call(partial(attend_kernel, length=length), (flat_low, flat_low, flat_low...  11.9 us
    pallas_call x1, Pallas kernels, local(): call(up_kernel, (sds((shards, tokens, shard_hidden), bf16), *(sds((tokens...  8.64 us
    pallas_call x1, Pallas kernels, local(): call(partial(attend_back_kernel, length=length), (flat_low, flat_low, fla...  8.58 us
    pallas_call x1, Pallas kernels, local(): call(norm_back_kernel, (flat, flat_low, flat_low, small), 1, 8, 12, [pltp...  8.16 us
    pallas_call x1, Pallas kernels, local(): call(down_kernel, (flat_low, flat, flat_low, small), 1, 4, 4, [pltpu.VMEM...  7.15 us
    pallas_call x1, Pallas kernels, local(): call(hidden_back_kernel, (*(sds((tokens, shard_hidden), bf16),) * 4, sds(...  6.59 us
  transfers between devices with their start and end apart: 57, of which 20 were waited for; matrix products, arithmetic and copies ran while one was open for 4% of the time, Pallas kernels for 28%

profile of v1, /device:TPU:0, one launch (start us, length us, event | category | flops | bytes accessed | tf_op | source)
XLA Modules:
  0.0 246.5 jit_solution(9951965534241458512)
XLA Ops:
  1.3 3.4 %pack.1 = (bf16[784,768]{1,0:T(8,128)(2,1)}, bf16[784,384]{1,0:T(8,128)(2,1)}, bf16[192,1536]{1,0:T(8,128)(2,1)}) custom-call(s32[3]{0:T(128)} %pad_add_fusion.where_ref, bf16[192,768]{1,0:T(8,128)(2,1)} %q_ref.1, bf16[192,768]{1,0:T(8,128)(2,1)} %k_ref.1, bf16[192,768]{1,0:T(8,128)(2,1)} %v_ref.1, bf16[192,768]{1,0:T(8,128)(2,1)} %o_ref.1, ...), custom_call_target="tpu_custom_call" | custom-call | flops 1024 | bytes 1024 | tf_op jit(solution)/shard_map/pack/pallas_call | solution.py:522
  4.7 3.0 %collective-permute-start.1 = (bf16[784,384]{1,0:T(8,128)(2,1)}, bf16[784,384]{1,0:T(8,128)(2,1)S(1)}, u32[]{:S(2)}, u32[]{:S(2)}) collective-permute-start(bf16[784,384]{1,0:T(8,128)(2,1)} %get-tuple-element.78), channel_id=1, source_target_pairs={{0,2},{1,3},{2,0},{3,1},{4,6},{5,7},{6,4},{7,5},{8,10},{9,11},{10,... | collective-permute-start | bytes 1806344 | tf_op jit(solution)/shard_map/swap_fsdp2/ppermute | solution.py:38
  7.7 13.9 %collective-permute-done.1.refs_2_.refs_12_ = bf16[784,384]{1,0:T(8,128)(2,1)S(1)} collective-permute-done((bf16[784,384]{1,0:T(8,128)(2,1)}, bf16[784,384]{1,0:T(8,128)(2,1)S(1)}, u32[]{:S(2)}, u32[]{:S(2)}) %collective-permute-start.1) | collective-permute-done | bytes 602144 | tf_op jit(solution)/shard_map/swap_fsdp2/ppermute | solution.py:38
  21.5 1.8 collective-permute-start.2
  23.3 1.5 collective-permute-start.6
  24.8 11.6 %collective-permute-done.2.refs_3_.refs_13_ = bf16[784,384]{1,0:T(8,128)(2,1)S(1)} collective-permute-done((bf16[784,384]{1,0:T(8,128)(2,1)S(1)}, bf16[784,384]{1,0:T(8,128)(2,1)S(1)}, u32[]{:S(2)}, u32[]{:S(2)}) %collective-permute-start.2) | collective-permute-done | bytes 602144 | tf_op jit(solution)/shard_map/swap_dp1/ppermute | solution.py:38
  36.4 3.0 %collective-permute-done.6.refs_2_.refs_6_ = bf16[192,1536]{1,0:T(8,128)(2,1)} collective-permute-done((bf16[192,1536]{1,0:T(8,128)(2,1)}, bf16[192,1536]{1,0:T(8,128)(2,1)}, u32[]{:S(2)}, u32[]{:S(2)}) %collective-permute-start.6) | collective-permute-done | bytes 589856 | tf_op jit(solution)/shard_map/swap_fsdp2/ppermute | solution.py:38
  39.7 1.8 collective-permute-start.11
  41.7 0.8 copy-done
  42.7 11.9 %attend.1 = (bf16[256,768]{1,0:T(8,128)(2,1)}, bf16[256,768]{1,0:T(8,128)(2,1)}, bf16[256,768]{1,0:T(8,128)(2,1)}, bf16[4,256,192]{2,1,0:T(8,128)(2,1)}, bf16[4,...) custom-call(s32[3]{0:T(128)} %pad_add_fusion.where_ref, ...), custom_call_target="tpu_custom_call" | custom-call | flops 1024 | bytes 1024 | tf_op jit(solution)/shard_map/attend/pallas_call | solution.py:578
  55.2 1.7 collective-permute-done.9.refs_5_.refs_9_
  57.7 8.6 %up.1 = (bf16[4,256,768]{2,1,0:T(8,128)(2,1)}, bf16[256,768]{1,0:T(8,128)(2,1)}, bf16[256,768]{1,0:T(8,128)(2,1)}, bf16[2,256,768]{2,1,0:T(8,128)(2,1)}, f32[4,256,768]{2,1,0:T(8,128)}) custom-call(s32[3]{0:T(128)} %pad_add_fusion.where_ref, bf16[256,768]{1,0:T(8,128)(2,1)} %get-tuple-element.79.low_ref, f32[16,768]{1,0:T(8,128)} %get-tuple-element.80.vec_ref, ...), custom_call_target="tpu_custom_call" | custom-call | flops 1024 | bytes 1024 | tf_op jit(solution)/shard_map/up/pallas_call | solution.py:607
  66.4 1.8 collective-permute-done.11.refs_2_
  68.2 1.7 collective-permute-start.19
  69.9 1.3 collective-permute-done.12.refs_3_
  71.2 1.0 copy-done.9
  72.3 7.2 %down.1 = (bf16[256,768]{1,0:T(8,128)(2,1)}, f32[256,768]{1,0:T(8,128)}, bf16[256,768]{1,0:T(8,128)(2,1)}, f32[8,768]{1,0:T(8,128)}) custom-call(s32[3]{0:T(128)} %pad_add_fusion.where_ref, bf16[4,256,768]{2,1,0:T(8,128)(2,1)} %get-tuple-element.85.act_ref, f32[256,768]{1,0:T(8,128)} %get-tuple-element.86.n1_ref, f32[16,768]{1,0:T(8,128)} %get-tuple-element.80.vec_ref, ...), custom_call_target="tpu_custom_call" | custom-call | flops 1024 | bytes 1024 | tf_op jit(solution)/shard_map/down/pallas_call | solution.py:627
  79.4 1.8 collective-permute-start.22
  81.2 6.6 %hidden_back.1 = (bf16[256,768]{1,0:T(8,128)(2,1)}, bf16[256,768]{1,0:T(8,128)(2,1)}, bf16[256,768]{1,0:T(8,128)(2,1)}, bf16[256,768]{1,0:T(8,128)(2,1)}, f32[8,768]{1,0:T(8,128)}) custom-call(s32[3]{0:T(128)} %pad_add_fusion.where_ref, bf16[256,768]{1,0:T(8,128)(2,1)} %get-tuple-element.113.glow_ref.refs_4_, f32[4,256,768]{2,1,0:T(8,128)} %get-tuple-element.94.slope_ref, ...), custom_call_target="tpu_custom_call" | custom-call | flops 1024 | bytes 1024 | tf_op jit(solution)/shard_map/hidden_back/pallas_call | solution.py:638
  88.5 8.2 %norm_back.1 = (f32[256,768]{1,0:T(8,128)}, bf16[256,768]{1,0:T(8,128)(2,1)}, bf16[256,768]{1,0:T(8,128)(2,1)}, f32[8,768]{1,0:T(8,128)}) custom-call(s32[3]{0:T(128)} %pad_add_fusion.where_ref, f32[256,768]{1,0:T(8,128)} %get-tuple-element.91.gsec_ref, f32[256,768]{1,0:T(8,128)} %get-tuple-element.86.n1_ref, f32[256,128]{1,0:T(8,128)} %get-tuple-element.92.inv_ref, ...), custom_call_target="tpu_custom_call" | custom-call | flops 1024 | bytes 1024 | tf_op jit(solution)/shard_map/norm_back/pallas_call | solution.py:648
  97.4 1.0 collective-permute-done.13.got_ref
  100.2 4.4 %near_up.1 = (bf16[192,3072]{1,0:T(8,128)(2,1)}, bf16[192,3072]{1,0:T(8,128)(2,1)}) custom-call(s32[3]{0:T(128)} %pad_add_fusion.where_ref, bf16[2,256,192]{2,1,0:T(8,128)(2,1)} %get-tuple-element.105.own_ref, bf16[2,256,192]{2,1,0:T(8,128)(2,1)} %copy-done.33, bf16[256,768]{1,0:T(8,128)(2,1)} %get-tuple-element.95.refs_0_, ...), custom_call_target="tpu_custom_call" | custom-call | flops 1024 | bytes 1024 | tf_op jit(solution)/shard_map/near_up/pallas_call | solution.py:673
  104.7 0.8 collective-permute-start.30
  107.3 4.4 %down_grad.1 = (bf16[384,768]{1,0:T(8,128)(2,1)}, bf16[384,768]{1,0:T(8,128)(2,1)}) custom-call(s32[3]{0:T(128)} %pad_add_fusion.where_ref, bf16[256,768]{1,0:T(8,128)(2,1)} %get-tuple-element.88.refs_0_, bf16[256,768]{1,0:T(8,128)(2,1)} %copy-done.30, bf16[2,256,768]{2,1,0:T(8,128)(2,1)} %copy-done.11, bf16[256,768]{1,0:T(8,128)(2,1)} %copy-done.29, ...), custom_call_target="tpu_custom_call" | custom-call | flops 1024 | bytes 1024 | tf_op jit(solution)/shard_map/down_grad/pallas_call | solution.py:678
  111.8 1.6 collective-permute-start.24
  113.8 8.6 %attend_back.1 = (bf16[256,768]{1,0:T(8,128)(2,1)}, bf16[256,768]{1,0:T(8,128)(2,1)}, bf16[256,768]{1,0:T(8,128)(2,1)}) custom-call(bf16[256,768]{1,0:T(8,128)(2,1)} %get-tuple-element.83.q_ref, bf16[256,768]{1,0:T(8,128)(2,1)} %get-tuple-element.100.k_ref, bf16[256,768]{1,0:T(8,128)(2,1)} %get-tuple-element.101.v_ref, ...), custom_call_target="tpu_custom_call" | custom-call | flops 1024 | bytes 1024 | tf_op jit(solution)/shard_map/attend_back/pallas_call | solution.py:683
  122.9 4.1 %collective-permute-done.24 = bf16[384,768]{1,0:T(8,128)(2,1)S(1)} collective-permute-done((bf16[384,768]{1,0:T(8,128)(2,1)}, bf16[384,768]{1,0:T(8,128)(2,1)S(1)}, u32[]{:S(2)}, u32[]{:S(2)}) %collective-permute-start.24) | collective-permute-done | bytes 589856 | tf_op jit(solution)/shard_map/swap_dp2/ppermute | solution.py:38
  127.1 5.6 %input_back.1 = (bf16[256,768]{1,0:T(8,128)(2,1)}, f32[16,768]{1,0:T(8,128)}) custom-call(s32[3]{0:T(128)} %pad_add_fusion.where_ref, s32[2]{0:T(128)} %species_ref.3, f32[256,768]{1,0:T(8,128)} %get-tuple-element.99.gres_ref, bf16[256,768]{1,0:T(8,128)(2,1)} %get-tuple-element.117.gq_ref.refs_2_, bf16[256,768]{1,0:T(8,128)(2,1)} %get-tuple-element.118.gk_ref.refs_3_, ...), custom_call_target="tpu_custom_call" | custom-call | flops 1024 | bytes 1024 | tf_op jit(solution)/shard_map/input_back/pallas_call | solution.py:695
  132.8 1.6 collective-permute-start.53
  135.2 4.5 %near_attn.1 = (bf16[384,768]{1,0:T(8,128)(2,1)}, bf16[384,768]{1,0:T(8,128)(2,1)}, bf16[2,192,768]{2,1,0:T(8,128)(2,1)}, bf16[2,192,768]{2,1,0:T(8,128)(2,1)}) custom-call(s32[3]{0:T(128)} %pad_add_fusion.where_ref, bf16[4,256,192]{2,1,0:T(8,128)(2,1)} %get-tuple-element.127.own_ref, bf16[4,256,192]{2,1,0:T(8,128)(2,1)} %copy-done.20, ...), custom_call_target="tpu_custom_call" | custom-call | flops 1024 | bytes 1024 | tf_op jit(solution)/shard_map/near_attn/pallas_call | solution.py:706
  140.2 1.5 collective-permute-start.31
  141.7 1.4 add_convert_fusion.1
  143.1 1.5 collective-permute-start.48
  144.8 2.6 %collective-permute-start.54 = (bf16[192,768]{1,0:T(8,128)(2,1)S(1)}, bf16[192,768]{1,0:T(8,128)(2,1)S(1)}, u32[]{:S(2)}, u32[]{:S(2)}) collective-permute-start(bf16[192,768]{1,0:T(8,128)(2,1)S(1)} %add_convert_fusion.3), channel_id=1, source_target_pairs={{0,16},{4,20},{8,24},{12,28},{16,0},{20,4},{24,8},{28,12},{1,17},{... | collective-permute-start | bytes 884744 | tf_op jit(solution)/shard_map/swap_dp4/ppermute | solution.py:38
  147.4 8.7 %collective-permute-done.37 = bf16[2,192,768]{2,1,0:T(8,128)(2,1)S(1)} collective-permute-done((bf16[2,192,768]{2,1,0:T(8,128)(2,1)}, bf16[2,192,768]{2,1,0:T(8,128)(2,1)S(1)}, u32[]{:S(2)}, u32[]{:S(2)}) %collective-permute-start.37) | collective-permute-done | bytes 589856 | tf_op jit(solution)/shard_map/swap_dp1/ppermute | solution.py:38
  156.2 1.6 collective-permute-start.38
  157.9 2.3 collective-permute-done.54
  161.5 7.2 %collective-permute-done.48 = bf16[96,3072]{1,0:T(8,128)(2,1)S(1)} collective-permute-done((bf16[96,3072]{1,0:T(8,128)(2,1)}, bf16[96,3072]{1,0:T(8,128)(2,1)S(1)}, u32[]{:S(2)}, u32[]{:S(2)}) %collective-permute-start.48) | collective-permute-done | bytes 589856 | tf_op jit(solution)/shard_map/swap_dp1/ppermute | solution.py:38
  168.8 1.6 collective-permute-start.49
  170.4 0.9 collective-permute-start.34
  171.4 1.6 collective-permute-start.39
  173.0 2.2 collective-permute-done.34
  175.2 1.6 collective-permute-start.35
  177.0 1.2 collective-permute-start.43
  178.1 1.2 collective-permute-done.35
  179.3 2.6 %collective-permute-start.36 = (f32[16,768]{1,0:T(8,128)S(1)}, f32[16,768]{1,0:T(8,128)S(1)}, u32[]{:S(2)}, u32[]{:S(2)}) collective-permute-start(f32[16,768]{1,0:T(8,128)S(1)} %add.136), channel_id=1, source_target_pairs={{0,16},{4,20},{8,24},{12,28},{16,0},{20,4},{24,8},{28,12},{1,17},{... | collective-permute-start | bytes 147464 | tf_op jit(solution)/shard_map/swap_dp4/ppermute | solution.py:38
  182.2 1.6 collective-permute-start.56
  184.6 3.1 %collective-permute-start.40 = (bf16[96,768]{1,0:T(8,128)(2,1)S(1)}, bf16[96,768]{1,0:T(8,128)(2,1)S(1)}, u32[]{:S(2)}, u32[]{:S(2)}) collective-permute-start(bf16[96,768]{1,0:T(8,128)(2,1)S(1)} %fusion.2), channel_id=1, source_target_pairs={{0,16},{4,20},{8,24},{12,28},{16,0},{20,4},{24,8},{28,12},{1,17},{... | collective-permute-start | bytes 442376 | tf_op jit(solution)/shard_map/swap_dp4/ppermute | solution.py:38
  189.6 1.7 collective-permute-start.44
  191.3 9.4 %collective-permute-done.40 = bf16[96,768]{1,0:T(8,128)(2,1)S(1)} collective-permute-done((bf16[96,768]{1,0:T(8,128)(2,1)S(1)}, bf16[96,768]{1,0:T(8,128)(2,1)S(1)}, u32[]{:S(2)}, u32[]{:S(2)}) %collective-permute-start.40) | collective-permute-done | bytes 147488 | tf_op jit(solution)/shard_map/swap_dp4/ppermute | solution.py:38
  201.1 2.8 %collective-permute-done.44 = bf16[96,768]{1,0:T(8,128)(2,1)S(1)} collective-permute-done((bf16[96,768]{1,0:T(8,128)(2,1)S(1)}, bf16[96,768]{1,0:T(8,128)(2,1)S(1)}, u32[]{:S(2)}, u32[]{:S(2)}) %collective-permute-start.44) | collective-permute-done | bytes 147488 | tf_op jit(solution)/shard_map/swap_dp2/ppermute | solution.py:38
  203.9 1.1 collective-permute-start.45
  205.2 1.9 collective-permute-start.50
  207.2 1.3 collective-permute-start.42
  208.5 9.0 %collective-permute-done.45 = bf16[96,768]{1,0:T(8,128)(2,1)S(1)} collective-permute-done((bf16[96,768]{1,0:T(8,128)(2,1)S(1)}, bf16[96,768]{1,0:T(8,128)(2,1)S(1)}, u32[]{:S(2)}, u32[]{:S(2)}) %collective-permute-start.45) | collective-permute-done | bytes 147488 | tf_op jit(solution)/shard_map/swap_dp4/ppermute | solution.py:38
  218.1 4.5 %collective-permute-done.50 = bf16[48,3072]{1,0:T(8,128)(2,1)S(1)} collective-permute-done((bf16[48,3072]{1,0:T(8,128)(2,1)S(1)}, bf16[48,3072]{1,0:T(8,128)(2,1)S(1)}, u32[]{:S(2)}, u32[]{:S(2)}) %collective-permute-start.50) | collective-permute-done | bytes 294944 | tf_op jit(solution)/shard_map/swap_dp4/ppermute | solution.py:38
  222.8 1.6 fusion.1
  224.5 1.7 collective-permute-start.47
  226.3 4.1 %collective-permute-done.51 = bf16[48,3072]{1,0:T(8,128)(2,1)S(1)} collective-permute-done((bf16[48,3072]{1,0:T(8,128)(2,1)S(1)}, bf16[48,3072]{1,0:T(8,128)(2,1)S(1)}, u32[]{:S(2)}, u32[]{:S(2)}) %collective-permute-start.51) | collective-permute-done | bytes 294944 | tf_op jit(solution)/shard_map/swap_dp2/ppermute | solution.py:38
  230.6 1.7 collective-permute-start.52
  232.3 1.1 slice_convert_fusion.2
  233.6 1.1 slice_convert_fusion
  234.7 10.2 %collective-permute-done.52 = bf16[96,3072]{1,0:T(8,128)(2,1)S(1)} collective-permute-done((bf16[96,3072]{1,0:T(8,128)(2,1)S(1)}, bf16[96,3072]{1,0:T(8,128)(2,1)S(1)}, u32[]{:S(2)}, u32[]{:S(2)}) %collective-permute-start.52) | collective-permute-done | bytes 589856 | tf_op jit(solution)/shard_map/swap_dp1/ppermute | solution.py:38
  244.9 1.7 fusion
  (172 shorter events, 16.8 us)
Async XLA Ops:
  1.3 38.4 %copy-start.1 = (bf16[192,3072]{1,0:T(8,128)(2,1)S(1)}, bf16[192,3072]{1,0:T(8,128)(2,1)}, u32[]{:S(2)}) copy-start(bf16[192,3072]{1,0:T(8,128)(2,1)} %refs_4_.3) | copy-start | bytes 3538948
  1.3 38.4 %copy-start.7 = (bf16[768,768]{1,0:T(8,128)(2,1)S(1)}, bf16[768,768]{1,0:T(8,128)(2,1)}, u32[]{:S(2)}) copy-start(bf16[768,768]{1,0:T(8,128)(2,1)} %refs_0_.7) | copy-start | bytes 3538948
  4.7 16.8 %collective-permute-start.1 = (bf16[784,384]{1,0:T(8,128)(2,1)}, bf16[784,384]{1,0:T(8,128)(2,1)S(1)}, u32[]{:S(2)}, u32[]{:S(2)}) collective-permute-start(bf16[784,384]{1,0:T(8,128)(2,1)} %get-tuple-element.78), channel_id=1, source_target_pairs={{0,2},{1,3},{2,0},{3,1},{4,6},{5,7},{6,4},{7,5},{8,10},{9,11},{10,... | collective-permute-start | bytes 1806344 | tf_op jit(solution)/shard_map/swap_fsdp2/ppermute | solution.py:38
  7.7 33.8 %collective-permute-start = (bf16[784,768]{1,0:T(8,128)(2,1)}, bf16[784,768]{1,0:T(8,128)(2,1)S(1)}, u32[]{:S(2)}, u32[]{:S(2)}) collective-permute-start(bf16[784,768]{1,0:T(8,128)(2,1)} %get-tuple-element.77.refs_0_.refs_10_), channel_id=1, source_target_pairs={{0,1},{1,0},{2,3},{3,2},{4,5},{5,4},{6,7},{7,6},{8,9},{9,8},{10,11... | collective-permute-start | bytes 3612680 | tf_op jit(solution)/shard_map/swap_fsdp1/ppermute | solution.py:38
  21.5 20.1 %copy-start.2 = (bf16[784,384]{1,0:T(8,128)(2,1)}, bf16[784,384]{1,0:T(8,128)(2,1)S(1)}, u32[]{:S(2)}) copy-start(bf16[784,384]{1,0:T(8,128)(2,1)S(1)} %collective-permute-done.1.refs_2_.refs_12_) | copy-start | bytes 1806340
  21.5 14.8 %collective-permute-start.2 = (bf16[784,384]{1,0:T(8,128)(2,1)S(1)}, bf16[784,384]{1,0:T(8,128)(2,1)S(1)}, u32[]{:S(2)}, u32[]{:S(2)}) collective-permute-start(bf16[784,384]{1,0:T(8,128)(2,1)S(1)} %collective-permute-done.1.refs_2_.refs_12_), channel_id=1, source_target_pairs={{0,4},{4,0},{8,12},{12,8},{16,20},{20,16},{24,28},{28,24},{1,5},{5... | collective-permute-start | bytes 1806344 | tf_op jit(solution)/shard_map/swap_dp1/ppermute | solution.py:38
  23.3 16.3 %collective-permute-start.3 = (bf16[784,384]{1,0:T(8,128)(2,1)S(1)}, bf16[784,384]{1,0:T(8,128)(2,1)S(1)}, u32[]{:S(2)}, u32[]{:S(2)}) collective-permute-start(bf16[784,384]{1,0:T(8,128)(2,1)S(1)} %collective-permute-done.1.refs_2_.refs_12_), channel_id=1, source_target_pairs={{0,1},{1,0},{2,3},{3,2},{4,5},{5,4},{6,7},{7,6},{8,9},{9,8},{10,11... | collective-permute-start | bytes 1806344 | tf_op jit(solution)/shard_map/swap_fsdp1/ppermute | solution.py:38
  23.3 16.1 %collective-permute-start.6 = (bf16[192,1536]{1,0:T(8,128)(2,1)}, bf16[192,1536]{1,0:T(8,128)(2,1)}, u32[]{:S(2)}, u32[]{:S(2)}) collective-permute-start(bf16[192,1536]{1,0:T(8,128)(2,1)} %get-tuple-element.82), channel_id=1, source_target_pairs={{0,2},{1,3},{2,0},{3,1},{4,6},{5,7},{6,4},{7,5},{8,10},{9,11},{10,... | collective-permute-start | bytes 1769480 | tf_op jit(solution)/shard_map/swap_fsdp2/ppermute | solution.py:38
  36.4 5.3 %collective-permute-start.4 = (bf16[784,384]{1,0:T(8,128)(2,1)S(1)}, bf16[784,384]{1,0:T(8,128)(2,1)S(1)}, u32[]{:S(2)}, u32[]{:S(2)}) collective-permute-start(bf16[784,384]{1,0:T(8,128)(2,1)S(1)} %collective-permute-done.2.refs_3_.refs_13_), channel_id=1, source_target_pairs={{0,1},{1,0},{2,3},{3,2},{4,5},{5,4},{6,7},{7,6},{8,9},{9,8},{10,11... | collective-permute-start | bytes 1806344 | tf_op jit(solution)/shard_map/swap_fsdp1/ppermute | solution.py:38
  39.4 15.3 %collective-permute-start.7 = (bf16[192,1536]{1,0:T(8,128)(2,1)}, bf16[192,1536]{1,0:T(8,128)(2,1)}, u32[]{:S(2)}, u32[]{:S(2)}) collective-permute-start(bf16[192,1536]{1,0:T(8,128)(2,1)} %collective-permute-done.6.refs_2_.refs_6_), channel_id=1, source_target_pairs={{0,4},{4,0},{8,12},{12,8},{16,20},{20,16},{24,28},{28,24},{1,5},{5... | collective-permute-start | bytes 1769480 | tf_op jit(solution)/shard_map/swap_dp1/ppermute | solution.py:38
  39.6 15.6 %collective-permute-start.5 = (bf16[192,3072]{1,0:T(8,128)(2,1)S(1)}, bf16[192,3072]{1,0:T(8,128)(2,1)S(1)}, u32[]{:S(2)}, u32[]{:S(2)}) collective-permute-start(bf16[192,3072]{1,0:T(8,128)(2,1)S(1)} %copy-done.1), channel_id=1, source_target_pairs={{0,1},{1,0},{2,3},{3,2},{4,5},{5,4},{6,7},{7,6},{8,9},{9,8},{10,11... | collective-permute-start | bytes 3538952 | tf_op jit(solution)/shard_map/swap_fsdp1/ppermute | solution.py:38
  39.7 28.5 %collective-permute-start.11 = (bf16[768,768]{1,0:T(8,128)(2,1)S(1)}, bf16[768,768]{1,0:T(8,128)(2,1)}, u32[]{:S(2)}, u32[]{:S(2)}) collective-permute-start(bf16[768,768]{1,0:T(8,128)(2,1)S(1)} %copy-done.7), channel_id=1, source_target_pairs={{0,2},{1,3},{2,0},{3,1},{4,6},{5,7},{6,4},{7,5},{8,10},{9,11},{10,... | collective-permute-start | bytes 3538952 | tf_op jit(solution)/shard_map/swap_fsdp2/ppermute | solution.py:38
  41.5 13.8 %collective-permute-start.8 = (bf16[192,1536]{1,0:T(8,128)(2,1)}, bf16[192,1536]{1,0:T(8,128)(2,1)}, u32[]{:S(2)}, u32[]{:S(2)}) collective-permute-start(bf16[192,1536]{1,0:T(8,128)(2,1)} %collective-permute-done.6.refs_2_.refs_6_), channel_id=1, source_target_pairs={{0,1},{1,0},{2,3},{3,2},{4,5},{5,4},{6,7},{7,6},{8,9},{9,8},{10,11... | collective-permute-start | bytes 1769480 | tf_op jit(solution)/shard_map/swap_fsdp1/ppermute | solution.py:38
  54.7 2.3 collective-permute-start.9
  54.9 15.0 %collective-permute-start.10 = (bf16[768,768]{1,0:T(8,128)(2,1)S(1)}, bf16[768,768]{1,0:T(8,128)(2,1)S(1)}, u32[]{:S(2)}, u32[]{:S(2)}) collective-permute-start(bf16[768,768]{1,0:T(8,128)(2,1)S(1)} %copy-done.7), channel_id=1, source_target_pairs={{0,1},{1,0},{2,3},{3,2},{4,5},{5,4},{6,7},{7,6},{8,9},{9,8},{10,11... | collective-permute-start | bytes 3538952 | tf_op jit(solution)/shard_map/swap_fsdp1/ppermute | solution.py:38
  68.2 3.1 %collective-permute-start.12 = (bf16[768,768]{1,0:T(8,128)(2,1)}, bf16[768,768]{1,0:T(8,128)(2,1)S(1)}, u32[]{:S(2)}, u32[]{:S(2)}) collective-permute-start(bf16[768,768]{1,0:T(8,128)(2,1)} %collective-permute-done.11.refs_2_), channel_id=1, source_target_pairs={{0,1},{1,0},{2,3},{3,2},{4,5},{5,4},{6,7},{7,6},{8,9},{9,8},{10,11... | collective-permute-start | bytes 3538952 | tf_op jit(solution)/shard_map/swap_fsdp1/ppermute | solution.py:38
  68.2 28.5 %collective-permute-start.19 = (bf16[2,256,768]{2,1,0:T(8,128)(2,1)}, bf16[2,256,768]{2,1,0:T(8,128)(2,1)S(1)}, u32[]{:S(2)}, u32[]{:S(2)}) collective-permute-start(bf16[2,256,768]{2,1,0:T(8,128)(2,1)} %get-tuple-element.111), channel_id=1, source_target_pairs={{0,2},{1,3},{2,0},{3,1},{4,6},{5,7},{6,4},{7,5},{8,10},{9,11},{10,... | collective-permute-start | bytes 2359304 | tf_op jit(solution)/shard_map/swap_fsdp2/ppermute | solution.py:38
  79.4 17.8 %collective-permute-start.22 = (bf16[256,768]{1,0:T(8,128)(2,1)}, bf16[256,768]{1,0:T(8,128)(2,1)S(1)}, u32[]{:S(2)}, u32[]{:S(2)}) collective-permute-start(bf16[256,768]{1,0:T(8,128)(2,1)} %get-tuple-element.113.glow_ref.refs_4_), channel_id=1, source_target_pairs={{0,2},{1,3},{2,0},{3,1},{4,6},{5,7},{6,4},{7,5},{8,10},{9,11},{10,... | collective-permute-start | bytes 1179656 | tf_op jit(solution)/shard_map/swap_fsdp2/ppermute | solution.py:38
  87.8 10.9 %collective-permute-start.14 = (bf16[256,768]{1,0:T(8,128)(2,1)}, bf16[256,768]{1,0:T(8,128)(2,1)S(1)}, u32[]{:S(2)}, u32[]{:S(2)}) collective-permute-start(bf16[256,768]{1,0:T(8,128)(2,1)} %get-tuple-element.95.refs_0_), channel_id=1, source_target_pairs={{0,1},{1,0},{2,3},{3,2},{4,5},{5,4},{6,7},{7,6},{8,9},{9,8},{10,11... | collective-permute-start | bytes 1179656 | tf_op jit(solution)/shard_map/swap_fsdp1/ppermute | solution.py:38
  87.9 11.0 %collective-permute-start.15 = (bf16[256,768]{1,0:T(8,128)(2,1)}, bf16[256,768]{1,0:T(8,128)(2,1)S(1)}, u32[]{:S(2)}, u32[]{:S(2)}) collective-permute-start(bf16[256,768]{1,0:T(8,128)(2,1)} %get-tuple-element.96.refs_1_), channel_id=1, source_target_pairs={{0,1},{1,0},{2,3},{3,2},{4,5},{5,4},{6,7},{7,6},{8,9},{9,8},{10,11... | collective-permute-start | bytes 1179656 | tf_op jit(solution)/shard_map/swap_fsdp1/ppermute | solution.py:38
  88.4 10.9 %collective-permute-start.16 = (bf16[256,768]{1,0:T(8,128)(2,1)}, bf16[256,768]{1,0:T(8,128)(2,1)S(1)}, u32[]{:S(2)}, u32[]{:S(2)}) collective-permute-start(bf16[256,768]{1,0:T(8,128)(2,1)} %get-tuple-element.97.refs_2_), channel_id=1, source_target_pairs={{0,1},{1,0},{2,3},{3,2},{4,5},{5,4},{6,7},{7,6},{8,9},{9,8},{10,11... | collective-permute-start | bytes 1179656 | tf_op jit(solution)/shard_map/swap_fsdp1/ppermute | solution.py:38
  88.5 10.4 %copy-start.36 = (bf16[256,768]{1,0:T(8,128)(2,1)S(1)}, bf16[256,768]{1,0:T(8,128)(2,1)}, u32[]{:S(2)}) copy-start(bf16[256,768]{1,0:T(8,128)(2,1)} %get-tuple-element.110) | copy-start | bytes 1179652
  96.7 1.7 collective-permute-start.13
  97.2 2.3 collective-permute-start.17
  98.4 7.2 %collective-permute-start.21 = (bf16[256,768]{1,0:T(8,128)(2,1)S(1)}, bf16[256,768]{1,0:T(8,128)(2,1)S(1)}, u32[]{:S(2)}, u32[]{:S(2)}) collective-permute-start(bf16[256,768]{1,0:T(8,128)(2,1)S(1)} %copy-done.12), channel_id=1, source_target_pairs={{0,1},{1,0},{2,3},{3,2},{4,5},{5,4},{6,7},{7,6},{8,9},{9,8},{10,11... | collective-permute-start | bytes 1179656 | tf_op jit(solution)/shard_map/swap_fsdp1/ppermute | solution.py:38
  98.8 6.8 %collective-permute-start.20 = (bf16[256,768]{1,0:T(8,128)(2,1)S(1)}, bf16[256,768]{1,0:T(8,128)(2,1)S(1)}, u32[]{:S(2)}, u32[]{:S(2)}) collective-permute-start(bf16[256,768]{1,0:T(8,128)(2,1)S(1)} %slice_bitcast_fusion), channel_id=1, source_target_pairs={{0,1},{1,0},{2,3},{3,2},{4,5},{5,4},{6,7},{7,6},{8,9},{9,8},{10,11... | collective-permute-start | bytes 1179656 | tf_op jit(solution)/shard_map/swap_fsdp1/ppermute | solution.py:38
  98.9 6.7 %collective-permute-start.18 = (bf16[256,768]{1,0:T(8,128)(2,1)S(1)}, bf16[256,768]{1,0:T(8,128)(2,1)S(1)}, u32[]{:S(2)}, u32[]{:S(2)}) collective-permute-start(bf16[256,768]{1,0:T(8,128)(2,1)S(1)} %copy-done.36), channel_id=1, source_target_pairs={{0,1},{1,0},{2,3},{3,2},{4,5},{5,4},{6,7},{7,6},{8,9},{9,8},{10,11... | collective-permute-start | bytes 1179656 | tf_op jit(solution)/shard_map/swap_fsdp1/ppermute | solution.py:38
  99.3 6.2 %collective-permute-start.23 = (bf16[256,768]{1,0:T(8,128)(2,1)S(1)}, bf16[256,768]{1,0:T(8,128)(2,1)S(1)}, u32[]{:S(2)}, u32[]{:S(2)}) collective-permute-start(bf16[256,768]{1,0:T(8,128)(2,1)S(1)} %collective-permute-done.22.refs_6_), channel_id=1, source_target_pairs={{0,1},{1,0},{2,3},{3,2},{4,5},{5,4},{6,7},{7,6},{8,9},{9,8},{10,11... | collective-permute-start | bytes 1179656 | tf_op jit(solution)/shard_map/swap_fsdp1/ppermute | solution.py:38
  104.7 35.4 %collective-permute-start.30 = (bf16[192,3072]{1,0:T(8,128)(2,1)}, bf16[192,3072]{1,0:T(8,128)(2,1)S(1)}, u32[]{:S(2)}, u32[]{:S(2)}) collective-permute-start(bf16[192,3072]{1,0:T(8,128)(2,1)} %get-tuple-element.107), channel_id=1, source_target_pairs={{0,2},{1,3},{2,0},{3,1},{4,6},{5,7},{6,4},{7,5},{8,10},{9,11},{10,... | collective-permute-start | bytes 3538952 | tf_op jit(solution)/shard_map/swap_fsdp2/ppermute | solution.py:38
  111.8 15.3 %collective-permute-start.24 = (bf16[384,768]{1,0:T(8,128)(2,1)}, bf16[384,768]{1,0:T(8,128)(2,1)S(1)}, u32[]{:S(2)}, u32[]{:S(2)}) collective-permute-start(bf16[384,768]{1,0:T(8,128)(2,1)} %get-tuple-element.125), channel_id=1, source_target_pairs={{0,8},{4,12},{8,0},{12,4},{16,24},{20,28},{24,16},{28,20},{1,9},{5... | collective-permute-start | bytes 1769480 | tf_op jit(solution)/shard_map/swap_dp2/ppermute | solution.py:38
  113.3 9.2 %collective-permute-start.25 = (bf16[4,256,192]{2,1,0:T(8,128)(2,1)S(1)}, bf16[4,256,192]{2,1,0:T(8,128)(2,1)S(1)}, u32[]{:S(2)}, u32[]{:S(2)}) collective-permute-start(bf16[4,256,192]{2,1,0:T(8,128)(2,1)S(1)} %copy-done.35), channel_id=1, source_target_pairs={{0,1},{1,0},{2,3},{3,2},{4,5},{5,4},{6,7},{7,6},{8,9},{9,8},{10,11... | collective-permute-start | bytes 1179656 | tf_op jit(solution)/shard_map/swap_fsdp1/ppermute | solution.py:38
  113.3 19.4 %collective-permute-start.26 = (bf16[256,768]{1,0:T(8,128)(2,1)S(1)}, bf16[256,768]{1,0:T(8,128)(2,1)S(1)}, u32[]{:S(2)}, u32[]{:S(2)}) collective-permute-start(bf16[256,768]{1,0:T(8,128)(2,1)S(1)} %copy-done.21), channel_id=1, source_target_pairs={{0,1},{1,0},{2,3},{3,2},{4,5},{5,4},{6,7},{7,6},{8,9},{9,8},{10,11... | collective-permute-start | bytes 1179656 | tf_op jit(solution)/shard_map/swap_fsdp1/ppermute | solution.py:38
  122.4 12.0 %collective-permute-start.27 = (bf16[256,768]{1,0:T(8,128)(2,1)}, bf16[256,768]{1,0:T(8,128)(2,1)S(1)}, u32[]{:S(2)}, u32[]{:S(2)}) collective-permute-start(bf16[256,768]{1,0:T(8,128)(2,1)} %get-tuple-element.119.gv_ref.refs_1_), channel_id=1, source_target_pairs={{0,1},{1,0},{2,3},{3,2},{4,5},{5,4},{6,7},{7,6},{8,9},{9,8},{10,11... | collective-permute-start | bytes 1179656 | tf_op jit(solution)/shard_map/swap_fsdp1/ppermute | solution.py:38
  122.5 11.9 %collective-permute-start.28 = (bf16[256,768]{1,0:T(8,128)(2,1)}, bf16[256,768]{1,0:T(8,128)(2,1)}, u32[]{:S(2)}, u32[]{:S(2)}) collective-permute-start(bf16[256,768]{1,0:T(8,128)(2,1)} %get-tuple-element.117.gq_ref.refs_2_), channel_id=1, source_target_pairs={{0,1},{1,0},{2,3},{3,2},{4,5},{5,4},{6,7},{7,6},{8,9},{9,8},{10,11... | collective-permute-start | bytes 1179656 | tf_op jit(solution)/shard_map/swap_fsdp1/ppermute | solution.py:38
  127.1 7.4 %collective-permute-start.29 = (bf16[256,768]{1,0:T(8,128)(2,1)}, bf16[256,768]{1,0:T(8,128)(2,1)}, u32[]{:S(2)}, u32[]{:S(2)}) collective-permute-start(bf16[256,768]{1,0:T(8,128)(2,1)} %get-tuple-element.118.gk_ref.refs_3_), channel_id=1, source_target_pairs={{0,1},{1,0},{2,3},{3,2},{4,5},{5,4},{6,7},{7,6},{8,9},{9,8},{10,11... | collective-permute-start | bytes 1179656 | tf_op jit(solution)/shard_map/swap_fsdp1/ppermute | solution.py:38
  132.8 11.8 %collective-permute-start.53 = (bf16[192,768]{1,0:T(8,128)(2,1)S(1)}, bf16[192,768]{1,0:T(8,128)(2,1)S(1)}, u32[]{:S(2)}, u32[]{:S(2)}) collective-permute-start(bf16[192,768]{1,0:T(8,128)(2,1)S(1)} %add_convert_fusion.4), channel_id=1, source_target_pairs={{0,4},{4,0},{8,12},{12,8},{16,20},{20,16},{24,28},{28,24},{1,5},{5... | collective-permute-start | bytes 884744 | tf_op jit(solution)/shard_map/swap_dp1/ppermute | solution.py:38
  139.7 16.4 %collective-permute-start.37 = (bf16[2,192,768]{2,1,0:T(8,128)(2,1)}, bf16[2,192,768]{2,1,0:T(8,128)(2,1)S(1)}, u32[]{:S(2)}, u32[]{:S(2)}) collective-permute-start(bf16[2,192,768]{2,1,0:T(8,128)(2,1)} %get-tuple-element.133), channel_id=1, source_target_pairs={{0,4},{4,0},{8,12},{12,8},{16,20},{20,16},{24,28},{28,24},{1,5},{5... | collective-permute-start | bytes 1769480 | tf_op jit(solution)/shard_map/swap_dp1/ppermute | solution.py:38
  140.2 17.7 %collective-permute-start.31 = (bf16[384,768]{1,0:T(8,128)(2,1)}, bf16[384,768]{1,0:T(8,128)(2,1)S(1)}, u32[]{:S(2)}, u32[]{:S(2)}) collective-permute-start(bf16[384,768]{1,0:T(8,128)(2,1)} %get-tuple-element.130), channel_id=1, source_target_pairs={{0,2},{1,3},{2,0},{3,1},{4,6},{5,7},{6,4},{7,5},{8,10},{9,11},{10,... | collective-permute-start | bytes 1769480 | tf_op jit(solution)/shard_map/swap_fsdp2/ppermute | solution.py:38
  143.1 13.0 %copy-start.16 = (bf16[2,192,768]{2,1,0:T(8,128)(2,1)S(1)}, bf16[2,192,768]{2,1,0:T(8,128)(2,1)}, u32[]{:S(2)}) copy-start(bf16[2,192,768]{2,1,0:T(8,128)(2,1)} %get-tuple-element.132) | copy-start | bytes 1769476
  143.1 25.6 %collective-permute-start.48 = (bf16[96,3072]{1,0:T(8,128)(2,1)}, bf16[96,3072]{1,0:T(8,128)(2,1)S(1)}, u32[]{:S(2)}, u32[]{:S(2)}) collective-permute-start(bf16[96,3072]{1,0:T(8,128)(2,1)} %get-tuple-element.137), channel_id=1, source_target_pairs={{0,4},{4,0},{8,12},{12,8},{16,20},{20,16},{24,28},{28,24},{1,5},{5... | collective-permute-start | bytes 1769480 | tf_op jit(solution)/shard_map/swap_dp1/ppermute | solution.py:38
  144.8 15.5 %collective-permute-start.54 = (bf16[192,768]{1,0:T(8,128)(2,1)S(1)}, bf16[192,768]{1,0:T(8,128)(2,1)S(1)}, u32[]{:S(2)}, u32[]{:S(2)}) collective-permute-start(bf16[192,768]{1,0:T(8,128)(2,1)S(1)} %add_convert_fusion.3), channel_id=1, source_target_pairs={{0,16},{4,20},{8,24},{12,28},{16,0},{20,4},{24,8},{28,12},{1,17},{... | collective-permute-start | bytes 884744 | tf_op jit(solution)/shard_map/swap_dp4/ppermute | solution.py:38
  147.4 10.5 %copy-start.34 = (f32[16,768]{1,0:T(8,128)S(1)}, f32[16,768]{1,0:T(8,128)}, u32[]{:S(2)}) copy-start(f32[16,768]{1,0:T(8,128)} %get-tuple-element.131) | copy-start | bytes 147460
  156.2 15.1 %collective-permute-start.38 = (bf16[2,96,768]{2,1,0:T(8,128)(2,1)S(1)}, bf16[2,96,768]{2,1,0:T(8,128)(2,1)S(1)}, u32[]{:S(2)}, u32[]{:S(2)}) collective-permute-start(bf16[2,96,768]{2,1,0:T(8,128)(2,1)S(1)} %get-tuple-element.141), channel_id=1, source_target_pairs={{0,8},{4,12},{8,0},{12,4},{16,24},{20,28},{24,16},{28,20},{1,9},{5... | collective-permute-start | bytes 884744 | tf_op jit(solution)/shard_map/swap_dp2/ppermute | solution.py:38
  157.9 19.0 %copy-start.15 = (bf16[384,768]{1,0:T(8,128)(2,1)S(1)}, bf16[384,768]{1,0:T(8,128)(2,1)}, u32[]{:S(2)}) copy-start(bf16[384,768]{1,0:T(8,128)(2,1)} %get-tuple-element.134) | copy-start | bytes 1769476
  157.9 3.1 %collective-permute-start.32 = (f32[16,768]{1,0:T(8,128)S(1)}, f32[16,768]{1,0:T(8,128)S(1)}, u32[]{:S(2)}, u32[]{:S(2)}) collective-permute-start(f32[16,768]{1,0:T(8,128)S(1)} %copy-done.34), channel_id=1, source_target_pairs={{0,1},{1,0},{2,3},{3,2},{4,5},{5,4},{6,7},{7,6},{8,9},{9,8},{10,11... | collective-permute-start | bytes 147464 | tf_op jit(solution)/shard_map/swap_fsdp1/ppermute | solution.py:38
  160.3 21.6 %collective-permute-start.55 = (bf16[192,768]{1,0:T(8,128)(2,1)S(1)}, bf16[192,768]{1,0:T(8,128)(2,1)S(1)}, u32[]{:S(2)}, u32[]{:S(2)}) collective-permute-start(bf16[192,768]{1,0:T(8,128)(2,1)S(1)} %add_convert_fusion.2), channel_id=1, source_target_pairs={{0,4},{4,0},{8,12},{12,8},{16,20},{20,16},{24,28},{28,24},{1,5},{5... | collective-permute-start | bytes 884744 | tf_op jit(solution)/shard_map/swap_dp1/ppermute | solution.py:38
  160.9 9.5 %collective-permute-start.33 = (f32[16,768]{1,0:T(8,128)S(1)}, f32[16,768]{1,0:T(8,128)S(1)}, u32[]{:S(2)}, u32[]{:S(2)}) collective-permute-start(f32[16,768]{1,0:T(8,128)S(1)} %add.133), channel_id=1, source_target_pairs={{0,2},{1,3},{2,0},{3,1},{4,6},{5,7},{6,4},{7,5},{8,10},{9,11},{10,... | collective-permute-start | bytes 147464 | tf_op jit(solution)/shard_map/swap_fsdp2/ppermute | solution.py:38
  168.8 36.3 %collective-permute-start.49 = (bf16[48,3072]{1,0:T(8,128)(2,1)S(1)}, bf16[48,3072]{1,0:T(8,128)(2,1)S(1)}, u32[]{:S(2)}, u32[]{:S(2)}) collective-permute-start(bf16[48,3072]{1,0:T(8,128)(2,1)S(1)} %add_convert_fusion.8), channel_id=1, source_target_pairs={{0,8},{4,12},{8,0},{12,4},{16,24},{20,28},{24,16},{28,20},{1,9},{5... | collective-permute-start | bytes 884744 | tf_op jit(solution)/shard_map/swap_dp2/ppermute | solution.py:38
  170.4 4.7 %collective-permute-start.34 = (f32[16,768]{1,0:T(8,128)S(1)}, f32[16,768]{1,0:T(8,128)S(1)}, u32[]{:S(2)}, u32[]{:S(2)}) collective-permute-start(f32[16,768]{1,0:T(8,128)S(1)} %add.134), channel_id=1, source_target_pairs={{0,4},{4,0},{8,12},{12,8},{16,20},{20,16},{24,28},{28,24},{1,5},{5... | collective-permute-start | bytes 147464 | tf_op jit(solution)/shard_map/swap_dp1/ppermute | solution.py:38
  171.4 13.1 %collective-permute-start.39 = (bf16[96,768]{1,0:T(8,128)(2,1)S(1)}, bf16[96,768]{1,0:T(8,128)(2,1)S(1)}, u32[]{:S(2)}, u32[]{:S(2)}) collective-permute-start(bf16[96,768]{1,0:T(8,128)(2,1)S(1)} %fusion.3), channel_id=1, source_target_pairs={{0,2},{1,3},{2,0},{3,1},{4,6},{5,7},{6,4},{7,5},{8,10},{9,11},{10,... | collective-permute-start | bytes 442376 | tf_op jit(solution)/shard_map/swap_fsdp2/ppermute | solution.py:38
  175.2 4.2 %collective-permute-start.35 = (f32[16,768]{1,0:T(8,128)S(1)}, f32[16,768]{1,0:T(8,128)S(1)}, u32[]{:S(2)}, u32[]{:S(2)}) collective-permute-start(f32[16,768]{1,0:T(8,128)S(1)} %add.135), channel_id=1, source_target_pairs={{0,8},{4,12},{8,0},{12,4},{16,24},{20,28},{24,16},{28,20},{1,9},{5... | collective-permute-start | bytes 147464 | tf_op jit(solution)/shard_map/swap_dp2/ppermute | solution.py:38
  177.0 12.6 %collective-permute-start.43 = (bf16[192,768]{1,0:T(8,128)(2,1)S(1)}, bf16[192,768]{1,0:T(8,128)(2,1)S(1)}, u32[]{:S(2)}, u32[]{:S(2)}) collective-permute-start(bf16[192,768]{1,0:T(8,128)(2,1)S(1)} %get-tuple-element.139), channel_id=1, source_target_pairs={{0,4},{4,0},{8,12},{12,8},{16,20},{20,16},{24,28},{28,24},{1,5},{5... | collective-permute-start | bytes 884744 | tf_op jit(solution)/shard_map/swap_dp1/ppermute | solution.py:38
  179.3 5.2 %collective-permute-start.36 = (f32[16,768]{1,0:T(8,128)S(1)}, f32[16,768]{1,0:T(8,128)S(1)}, u32[]{:S(2)}, u32[]{:S(2)}) collective-permute-start(f32[16,768]{1,0:T(8,128)S(1)} %add.136), channel_id=1, source_target_pairs={{0,16},{4,20},{8,24},{12,28},{16,0},{20,4},{24,8},{28,12},{1,17},{... | collective-permute-start | bytes 147464 | tf_op jit(solution)/shard_map/swap_dp4/ppermute | solution.py:38
  182.2 40.6 %collective-permute-start.56 = (bf16[384,768]{1,0:T(8,128)(2,1)S(1)}, bf16[384,768]{1,0:T(8,128)(2,1)S(1)}, u32[]{:S(2)}, u32[]{:S(2)}) collective-permute-start(bf16[384,768]{1,0:T(8,128)(2,1)S(1)} %maximum_select_fusion.5), channel_id=1, source_target_pairs={{0,8},{4,12},{8,0},{12,4},{16,24},{20,28},{24,16},{28,20},{1,9},{5... | collective-permute-start | bytes 1769480 | tf_op jit(solution)/shard_map/swap_dp2/ppermute | solution.py:38
  184.6 16.1 %collective-permute-start.40 = (bf16[96,768]{1,0:T(8,128)(2,1)S(1)}, bf16[96,768]{1,0:T(8,128)(2,1)S(1)}, u32[]{:S(2)}, u32[]{:S(2)}) collective-permute-start(bf16[96,768]{1,0:T(8,128)(2,1)S(1)} %fusion.2), channel_id=1, source_target_pairs={{0,16},{4,20},{8,24},{12,28},{16,0},{20,4},{24,8},{28,12},{1,17},{... | collective-permute-start | bytes 442376 | tf_op jit(solution)/shard_map/swap_dp4/ppermute | solution.py:38
  189.6 14.2 %collective-permute-start.44 = (bf16[96,768]{1,0:T(8,128)(2,1)S(1)}, bf16[96,768]{1,0:T(8,128)(2,1)S(1)}, u32[]{:S(2)}, u32[]{:S(2)}) collective-permute-start(bf16[96,768]{1,0:T(8,128)(2,1)S(1)} %add_convert_fusion.16), channel_id=1, source_target_pairs={{0,8},{4,12},{8,0},{12,4},{16,24},{20,28},{24,16},{28,20},{1,9},{5... | collective-permute-start | bytes 442376 | tf_op jit(solution)/shard_map/swap_dp2/ppermute | solution.py:38
  200.7 6.4 %collective-permute-start.41 = (bf16[96,768]{1,0:T(8,128)(2,1)S(1)}, bf16[96,768]{1,0:T(8,128)(2,1)S(1)}, u32[]{:S(2)}, u32[]{:S(2)}) collective-permute-start(bf16[96,768]{1,0:T(8,128)(2,1)S(1)} %add_convert_fusion.18), channel_id=1, source_target_pairs={{0,8},{4,12},{8,0},{12,4},{16,24},{20,28},{24,16},{28,20},{1,9},{5... | collective-permute-start | bytes 442376 | tf_op jit(solution)/shard_map/swap_dp2/ppermute | solution.py:38
  203.9 13.5 %collective-permute-start.45 = (bf16[96,768]{1,0:T(8,128)(2,1)S(1)}, bf16[96,768]{1,0:T(8,128)(2,1)S(1)}, u32[]{:S(2)}, u32[]{:S(2)}) collective-permute-start(bf16[96,768]{1,0:T(8,128)(2,1)S(1)} %add_convert_fusion.15), channel_id=1, source_target_pairs={{0,16},{4,20},{8,24},{12,28},{16,0},{20,4},{24,8},{28,12},{1,17},{... | collective-permute-start | bytes 442376 | tf_op jit(solution)/shard_map/swap_dp4/ppermute | solution.py:38
  205.2 17.4 %collective-permute-start.50 = (bf16[48,3072]{1,0:T(8,128)(2,1)S(1)}, bf16[48,3072]{1,0:T(8,128)(2,1)S(1)}, u32[]{:S(2)}, u32[]{:S(2)}) collective-permute-start(bf16[48,3072]{1,0:T(8,128)(2,1)S(1)} %add_convert_fusion.7), channel_id=1, source_target_pairs={{0,16},{4,20},{8,24},{12,28},{16,0},{20,4},{24,8},{28,12},{1,17},{... | collective-permute-start | bytes 884744 | tf_op jit(solution)/shard_map/swap_dp4/ppermute | solution.py:38
  207.2 19.0 %collective-permute-start.42 = (bf16[192,768]{1,0:T(8,128)(2,1)S(1)}, bf16[192,768]{1,0:T(8,128)(2,1)S(1)}, u32[]{:S(2)}, u32[]{:S(2)}) collective-permute-start(bf16[192,768]{1,0:T(8,128)(2,1)S(1)} %maximum_select_fusion.6), channel_id=1, source_target_pairs={{0,4},{4,0},{8,12},{12,8},{16,20},{20,16},{24,28},{28,24},{1,5},{5... | collective-permute-start | bytes 884744 | tf_op jit(solution)/shard_map/swap_dp1/ppermute | solution.py:38
  217.5 6.9 %collective-permute-start.46 = (bf16[96,768]{1,0:T(8,128)(2,1)S(1)}, bf16[96,768]{1,0:T(8,128)(2,1)S(1)}, u32[]{:S(2)}, u32[]{:S(2)}) collective-permute-start(bf16[96,768]{1,0:T(8,128)(2,1)S(1)} %add_convert_fusion.14), channel_id=1, source_target_pairs={{0,8},{4,12},{8,0},{12,4},{16,24},{20,28},{24,16},{28,20},{1,9},{5... | collective-permute-start | bytes 442376 | tf_op jit(solution)/shard_map/swap_dp2/ppermute | solution.py:38
  222.7 7.7 %collective-permute-start.51 = (bf16[48,3072]{1,0:T(8,128)(2,1)S(1)}, bf16[48,3072]{1,0:T(8,128)(2,1)S(1)}, u32[]{:S(2)}, u32[]{:S(2)}) collective-permute-start(bf16[48,3072]{1,0:T(8,128)(2,1)S(1)} %add_convert_fusion.6), channel_id=1, source_target_pairs={{0,8},{4,12},{8,0},{12,4},{16,24},{20,28},{24,16},{28,20},{1,9},{5... | collective-permute-start | bytes 884744 | tf_op jit(solution)/shard_map/swap_dp2/ppermute | solution.py:38
  224.5 8.9 %collective-permute-start.47 = (bf16[192,768]{1,0:T(8,128)(2,1)S(1)}, bf16[192,768]{1,0:T(8,128)(2,1)S(1)}, u32[]{:S(2)}, u32[]{:S(2)}) collective-permute-start(bf16[192,768]{1,0:T(8,128)(2,1)S(1)} %maximum_select_fusion.7), channel_id=1, source_target_pairs={{0,4},{4,0},{8,12},{12,8},{16,20},{20,16},{24,28},{28,24},{1,5},{5... | collective-permute-start | bytes 884744 | tf_op jit(solution)/shard_map/swap_dp1/ppermute | solution.py:38
  230.6 14.3 %collective-permute-start.52 = (bf16[96,3072]{1,0:T(8,128)(2,1)S(1)}, bf16[96,3072]{1,0:T(8,128)(2,1)S(1)}, u32[]{:S(2)}, u32[]{:S(2)}) collective-permute-start(bf16[96,3072]{1,0:T(8,128)(2,1)S(1)} %maximum_select_fusion.4), channel_id=1, source_target_pairs={{0,4},{4,0},{8,12},{12,8},{16,20},{20,16},{24,28},{28,24},{1,5},{5... | collective-permute-start | bytes 1769480 | tf_op jit(solution)/shard_map/swap_dp1/ppermute | solution.py:38
  (31 other events, 114.7 us)

commit v2 on v1

--- a/solution.py
+++ b/solution.py
@@ -15,9 +15,11 @@
 
 BQ, BV, BO, G1, S1, BD, G2, S2, TB, BU = 0, 1, 2, 3, 4, 5, 6, 7, 8, 10
 VEC_ROWS = 16
+TURNS = "UUDSASUUADAASUDASDUSAUADUA"
 COST = 1024
 ATTEND_COST = 1024
-VMEM_LIMIT = 56 * 1024 * 1024
+VMEM_LIMIT = 16 * 1024 * 1024
+LARGE_VMEM_LIMIT = 56 * 1024 * 1024
 
 
 def dot(a, b):
@@ -47,29 +49,29 @@
     return lax.optimization_barrier((x,) + others)[0]
 
 
-def piece_slots(where_ref, width, count):
-    f, y = where_ref[0], where_ref[1]
-    if count == 4:
-        return tuple((f ^ n, 0, width) for n in range(4))
+def halved(first, rows, top, bit):
+    return [
+        (first, top, rows, 2, bit, 0),
+        (first + 1, top, rows, 2, bit, 1),
+        (first + 2, top, rows, 3, bit, 0),
+        (first + 3, top, rows, 3, bit, 1),
+    ]
+
+
+def start_rows(plan, pieces, where_ref, shard_rows, target, sems, base):
+    width = target.shape[1]
     half = width // 2
-    low = pl.multiple_of(y * half, 128)
-    high = pl.multiple_of((1 - y) * half, 128)
-    return (
-        (f, 0, width),
-        (f ^ 1, 0, width),
-        (f ^ 2, low, half),
-        (f ^ 2, high, half),
-        (f ^ 3, low, half),
-        (f ^ 3, high, half),
-    )
-
-
-def start_rows(pieces, where_ref, first_row, rows, width, target, sems, base):
     copies = []
-    for n, (piece, (shard, col, cols)) in enumerate(zip(pieces, piece_slots(where_ref, width, len(pieces)))):
+    for n, (piece, first, rows, distance, bit, other, *at) in enumerate(plan):
+        row = pl.multiple_of((where_ref[0] ^ distance) * shard_rows + (at[0] if at else 0), 8)
+        if bit is None:
+            cols = pl.ds(0, width)
+        else:
+            side = where_ref[bit]
+            cols = pl.ds(pl.multiple_of((1 - side if other else side) * half, 128), half)
         copy = pltpu.make_async_copy(
-            piece.at[pl.ds(first_row, rows), :],
-            target.at[pl.ds(pl.multiple_of(shard * rows, 8), rows), pl.ds(col, cols)],
+            pieces[piece].at[pl.ds(first, rows), :],
+            target.at[pl.ds(row, rows), cols],
             sems.at[base + n],
         )
         copy.start()
@@ -77,12 +79,35 @@
     return copies
 
 
+def attn_plan(first, rows):
+    return [(0, first, rows, 0, None, 0), (1, first, rows, 1, None, 0)] + halved(2, rows, first, 1)
+
+
+def up_plan(rows):
+    half = rows // 2
+    plan = [(0, 0, rows, 0, None, 0), (1, 0, rows, 1, None, 0)] + halved(2, half, 0, 2)
+    return plan + [(6, 0, half, 2, None, 0, half), (7, 0, half, 3, None, 0, half)]
+
+
+def down_plan(rows):
+    half = rows // 2
+    plan = [(0, 0, rows, 0, None, 0), (1, 0, rows, 1, None, 0)] + halved(2, half, 0, 1)
+    return plan + [copy + (half,) for copy in halved(6, half, 0, 2)]
+
+
 def wait_all(copies):
     for copy in copies:
         copy.wait()
 
 
-def call(kernel, out_shapes, n_smem, n_vmem, n_any, scratch, name, cost=COST):
+def call(kernel, out_shapes, n_smem, n_vmem, n_any, scratch, name, cost=COST, resident=True, limit=VMEM_LIMIT):
+    if resident:
+        out_shapes = jax.tree.map(
+            lambda out: pltpu.VMEM(out.shape, out.dtype)
+            if isinstance(out, jax.ShapeDtypeStruct)
+            else out,
+            out_shapes,
+        )
     return pl.pallas_call(
         kernel,
         out_shape=out_shapes,
@@ -91,10 +116,16 @@
         + [pl.BlockSpec(memory_space=pl.ANY)] * n_any,
         out_specs=jax.tree.map(lambda _: pl.BlockSpec(memory_space=pltpu.VMEM), out_shapes),
         scratch_shapes=scratch,
-        compiler_params=pltpu.CompilerParams(vmem_limit_bytes=VMEM_LIMIT),
+        compiler_params=pltpu.CompilerParams(
+            vmem_limit_bytes=limit
+        ),
         cost_estimate=pl.CostEstimate(flops=cost, bytes_accessed=cost, transcendentals=0),
         name=name,
     )
+
+
+def in_hbm(x):
+    return pltpu.with_memory_space_constraint(x, pltpu.HBM)
 
 
 def sds(shape, dtype):
@@ -133,19 +164,21 @@
     return expo / jnp.sum(expo, axis=-1, keepdims=True)
 
 
-def pack_kernel(where_ref, q_ref, k_ref, v_ref, o_ref, up_ref, *refs):
+def pack_kernel(where_ref, q_ref, k_ref, v_ref, o_ref, *refs):
     vectors, table_ref, b_up_ref = refs[:TB], refs[TB], refs[TB + 1]
-    all_ref, half_ref, half_up_ref, spread = refs[TB + 2 :]
+    first_ref, second_ref, half_first_ref, half_second_ref, spread = refs[TB + 2 :]
     rows, width = q_ref.shape
     f, y = where_ref[0], where_ref[1]
-    half = half_ref.shape[1]
-    half_up = half_up_ref.shape[1]
+    half = half_first_ref.shape[1]
     cols = pl.ds(pl.multiple_of(y * half, 128), half)
-    for m, ref in enumerate((q_ref, k_ref, v_ref, o_ref)):
-        at = slice(m * rows, (m + 1) * rows)
-        half_ref[at, :] = ref[:, cols]
-        all_ref[at, :] = ref[...]
-    half_up_ref[...] = up_ref[:, pl.ds(pl.multiple_of(y * half_up, 128), half_up)]
+    for whole_ref, half_ref, pair in (
+        (first_ref, half_first_ref, (q_ref, k_ref)),
+        (second_ref, half_second_ref, (v_ref, o_ref)),
+    ):
+        for m, ref in enumerate(pair):
+            at = slice(m * rows, (m + 1) * rows)
+            half_ref[at, :] = ref[:, cols]
+            whole_ref[at, :] = ref[...]
     spread[...] = jnp.zeros(spread.shape, f32)
     table = table_ref[...].astype(f32)
     for k in range(4):
@@ -158,8 +191,8 @@
             spread[TB : TB + 2, mine] = table
             spread[BU + k : BU + k + 1, :] = b_up_ref[...].astype(f32).reshape(1, width)
 
-    all_ref[4 * rows :, :] = spread[...].astype(bf16)
-    half_ref[4 * rows :, :] = spread[:, cols].astype(bf16)
+    first_ref[2 * rows :, :] = spread[...].astype(bf16)
+    half_first_ref[2 * rows :, :] = spread[:, cols].astype(bf16)
 
 
 def put_blocks(value, f, blocks, targets, at):
@@ -179,7 +212,7 @@
     *refs,
     length,
 ):
-    pieces = refs[:6]
+    pieces, later_pieces = refs[:6], refs[6:12]
     (
         q_ref,
         k_ref,
@@ -197,17 +230,19 @@
         abuf,
         blocks,
         sems,
-    ) = refs[6:]
+    ) = refs[12:]
     f = where_ref[0]
     tokens, width = x_ref.shape
     cells = tokens // length
     rows = width // 4
+    vec_copies = start_rows(
+        attn_plan(2 * rows, VEC_ROWS), pieces, where_ref, VEC_ROWS, vbuf, sems, 24
+    )
     copies = []
     for m in range(4):
-        copies.append(
-            start_rows(pieces, where_ref, m * rows, rows, width, wbuf.at[m], sems, 6 * m)
-        )
-    vec_copies = start_rows(pieces, where_ref, 4 * rows, VEC_ROWS, width, vbuf, sems, 24)
+        from_pieces = pieces if m < 2 else later_pieces
+        plan = attn_plan((m % 2) * rows, rows)
+        copies.append(start_rows(plan, from_pieces, where_ref, rows, wbuf.at[m], sems, 6 * m))
     wait_all(vec_copies)
     vec = vbuf[0:VEC_ROWS, :].astype(f32)
     for i in range(1, 4):
@@ -253,13 +288,13 @@
 
 
 def up_kernel(where_ref, low_ref, vec_ref, *refs):
-    pieces = refs[:6]
-    act_ref, own_ref, near_ref, across_ref, slope_ref, wbuf, sems = refs[6:]
+    pieces = refs[:8]
+    act_ref, own_ref, near_ref, across_ref, slope_ref, wbuf, sems = refs[8:]
     f = where_ref[0]
     hidden = wbuf.shape[1]
     rows = wbuf.shape[0] // 4
     block = hidden // 4
-    wait_all(start_rows(pieces, where_ref, 0, rows, hidden, wbuf, sems, 0))
+    wait_all(start_rows(up_plan(rows), pieces, where_ref, rows, wbuf, sems, 0))
     low = low_ref[...]
     for j in range(4):
         up = dot(low, wbuf[:, j * block : (j + 1) * block]) + vec_ref[BU + j : BU + j + 1, :]
@@ -274,11 +309,11 @@
 
 
 def down_kernel(where_ref, act_ref, n1_ref, vec_ref, cot_ref, *refs):
-    pieces = refs[:4]
-    out_ref, gsec_ref, glow_ref, sm_ref, wbuf, sems = refs[4:]
+    pieces = refs[:10]
+    out_ref, gsec_ref, glow_ref, sm_ref, wbuf, sems = refs[10:]
     rows = wbuf.shape[0] // 4
     width = wbuf.shape[1]
-    copies = start_rows(pieces, where_ref, 0, rows, width, wbuf, sems, 0)
+    copies = start_rows(down_plan(rows), pieces, where_ref, rows, wbuf, sems, 0)
     vec = vec_ref[...]
     wait_all(copies)
     branch = None
@@ -301,39 +336,45 @@
 
 
 def near_up_kernel(where_ref, own_ref, got_ref, *refs):
-    rights, got_rights, outs = refs[:4], refs[4:8], refs[8:]
+    rights, got_rights = refs[:4], refs[4:8]
+    send_x, keep_x, send_y, keep_y = refs[8:]
     block = rights[0].shape[1]
-    for slot, out in ((1, outs[0]), (0, outs[1])):
+    part = send_x.shape[1]
+    low_z = where_ref[2] == 0
+    for slot, out in ((1, send_x), (0, keep_x)):
         for j in range(4):
+            cols = slice(j * block, (j + 1) * block)
             total = dot_tn(own_ref[slot], rights[j][...]) + dot_tn(got_ref[slot], got_rights[j][...])
-            out[:, j * block : (j + 1) * block] = total.astype(bf16)
+            total = total.astype(bf16)
+            out[0, :, cols] = total[:part]
+            out[1, :, cols] = total[2 * part : 3 * part]
+            first, second = total[part : 2 * part], total[3 * part :]
+            send_y[slot, :, cols] = jnp.where(low_z, second, first)
+            keep_y[slot, :, cols] = jnp.where(low_z, first, second)
 
 
 def near_attn_kernel(where_ref, own_ref, got_ref, *refs):
     rights, got_rights = refs[:4], refs[4:8]
-    send_ref, keep_ref, send_y_ref, keep_y_ref = refs[8:]
-    y = where_ref[1]
-    rows = own_ref.shape[2]
+    send_x, keep_x, send_y, keep_y = refs[8:]
+    low_y = where_ref[1] == 0
 
     def block(left, n):
-        return dot_tn(own_ref[left], rights[n][...]) + dot_tn(got_ref[left], got_rights[n][...])
-
-    for slot, ref in ((1, send_ref), (0, keep_ref)):
-        ref[0:rows, :] = block(slot, 0).astype(bf16)
-        ref[rows : 2 * rows, :] = block(2 + slot, 1).astype(bf16)
-    for ref, first in ((send_y_ref, 1 - y), (keep_y_ref, y)):
-        right = jnp.where(first == 0, rights[2][...], rights[3][...])
-        got_right = jnp.where(first == 0, got_rights[2][...], got_rights[3][...])
-        for slot in (0, 1):
-            total = dot_tn(own_ref[2 + slot], right) + dot_tn(got_ref[2 + slot], got_right)
-            ref[slot] = total.astype(bf16)
+        total = dot_tn(own_ref[left], rights[n][...]) + dot_tn(got_ref[left], got_rights[n][...])
+        return total.astype(bf16)
+
+    for slot, ref in ((1, send_x), (0, keep_x)):
+        ref[0] = block(slot, 0)
+        ref[1] = block(2 + slot, 1)
+        query, key = block(2 + slot, 2), block(2 + slot, 3)
+        send_y[slot] = jnp.where(low_y, key, query)
+        keep_y[slot] = jnp.where(low_y, query, key)
 
 
 def down_grad_kernel(where_ref, *refs):
     lefts, rights, outs = refs[:4], refs[4:8], refs[8:]
-    z = where_ref[2]
+    y = where_ref[1]
     rows = outs[0].shape[0]
-    for half, out in ((1 - z, outs[0]), (z, outs[1])):
+    for half, out in ((1 - y, outs[0]), (y, outs[1])):
         cols = pl.ds(pl.multiple_of(half * rows, 128), rows)
         total = None
         for n, (left, right) in enumerate(zip(lefts, rights)):
@@ -343,11 +384,11 @@
 
 
 def hidden_back_kernel(where_ref, glow_ref, slope_ref, *refs):
-    pieces = refs[:4]
-    guis, sm_ref, wbuf, sems = refs[4:8], refs[8], refs[9], refs[10]
+    pieces = refs[:10]
+    guis, sm_ref, wbuf, sems = refs[10:14], refs[14], refs[15], refs[16]
     rows = wbuf.shape[0] // 4
     width = wbuf.shape[1]
-    wait_all(start_rows(pieces, where_ref, 0, rows, width, wbuf, sems, 0))
+    wait_all(start_rows(down_plan(rows), pieces, where_ref, rows, wbuf, sems, 0))
     glow = glow_ref[...]
     for j in range(4):
         grad = dot_nt(glow, wbuf[j * rows : (j + 1) * rows, :]) * slope_ref[j]
@@ -358,13 +399,13 @@
 
 
 def norm_back_kernel(where_ref, gsec_ref, n1_ref, inv_ref, vec_ref, *refs):
-    guis, pieces, attn_pieces = refs[:4], refs[4:10], refs[10:16]
-    gres_ref, gbr_ref, gatt_ref, sm_ref, wbuf, obuf, sems = refs[16:]
+    guis, pieces, attn_pieces = refs[:4], refs[4:12], refs[12:18]
+    gres_ref, gbr_ref, gatt_ref, sm_ref, wbuf, obuf, sems = refs[18:]
     rows = wbuf.shape[0] // 4
     hidden = wbuf.shape[1]
     width = obuf.shape[1]
-    copies = start_rows(pieces, where_ref, 0, rows, hidden, wbuf, sems, 0)
-    out_copies = start_rows(attn_pieces, where_ref, 3 * rows, rows, width, obuf, sems, 6)
+    copies = start_rows(up_plan(rows), pieces, where_ref, rows, wbuf, sems, 0)
+    out_copies = start_rows(attn_plan(rows, rows), attn_pieces, where_ref, rows, obuf, sems, 8)
     wait_all(copies)
     block = hidden // 4
     grad_normed = gsec_ref[...]
@@ -417,14 +458,15 @@
     where_ref, species_ref, gres_ref, gq_ref, gk_ref, gv_ref, sm2_ref, smu_ref, sm1_ref, *refs,
     length,
 ):
-    pieces = refs[:6]
-    gin_ref, sm_ref, wbuf, sems = refs[6:]
+    pieces, later_pieces = refs[:6], refs[6:12]
+    gin_ref, sm_ref, wbuf, sems = refs[12:]
     tokens, width = gres_ref.shape
     rows = width // 4
-    copies = [
-        start_rows(pieces, where_ref, m * rows, rows, width, wbuf.at[m], sems, 6 * m)
-        for m in range(3)
-    ]
+    copies = []
+    for m in range(3):
+        from_pieces = pieces if m < 2 else later_pieces
+        plan = attn_plan((m % 2) * rows, rows)
+        copies.append(start_rows(plan, from_pieces, where_ref, rows, wbuf.at[m], sems, 6 * m))
     sm_ref[BQ : BQ + 1, :] = column_sum(gq_ref[...].astype(f32))
     sm_ref[BV : BV + 1, :] = column_sum(gv_ref[...].astype(f32))
     sm_ref[BO : BO + 1, :] = sm1_ref[2:3, :]
@@ -455,32 +497,93 @@
     return (a.astype(f32) + b.astype(f32)).astype(bf16)
 
 
-def scatter_cells(keep, got, dp_index, steps):
-    for step in steps:
+def two_way_chain(send_x, keep_x, send_b, keep_b, dp_index, bits, steps):
+    p, q = [(dp_index >> bit) & 1 for bit in bits]
+    one, two = [1 << bit for bit in bits]
+    got_x = swap(send_x, "fsdp", 2)
+    got_b = swap(send_b, "dp", one)
+    got_x = yield got_x, send_b
+    give = jnp.where(p == 0, add(keep_x[1], got_x[1]), add(keep_x[0], got_x[0]))
+    take = jnp.where(p == 0, add(keep_x[0], got_x[0]), add(keep_x[1], got_x[1]))
+    got_give = swap(give, "dp", one)
+    got_b = yield got_b, give
+    give = add(keep_b[1], got_b[1])
+    rest = add(keep_b[0], got_b[0])
+    got_rest = swap(give, "fsdp", 2)
+    got_give = yield got_give, give
+    first = add(take, got_give)
+    got_rest = yield got_rest, first
+    second = add(rest, got_rest)
+    send = jnp.where(q == 0, second, first)
+    keep = jnp.where(q == 0, first, second)
+    got = yield swap(send, "dp", two), send
+    total = add(keep, got)
+    for step in steps[:-1]:
         bit = (dp_index >> step) & 1
-        sent = add(half_rows(keep, 1 - bit), half_rows(got, 1 - bit))
+        send = half_rows(total, 1 - bit)
+        got = yield swap(send, "dp", 1 << step), send
+        total = add(half_rows(total, bit), got)
+    got = yield swap(total, "dp", 1 << steps[-1]), total
+    total = add(total, got)
+    for step in reversed(steps[:-1]):
+        other = yield swap(total, "dp", 1 << step), total
+        total = join_rows(total, other, dp_index, step)
+    other = yield swap(total, "dp", two), total
+    mine = jnp.stack([jnp.where(q == 0, total, other), jnp.where(q == 0, other, total)])
+    other = yield swap(mine, "dp", one), mine
+    return jnp.where(p == 0, mine, other), jnp.where(p == 0, other, mine)
+
+
+def join_rows(total, other, dp_index, step):
+    return jnp.where(
+        (dp_index >> step) & 1 == 0,
+        jnp.concatenate([total, other], axis=0),
+        jnp.concatenate([other, total], axis=0),
+    )
+
+
+def halving_chain(send, keep, dp_index, steps):
+    got = yield swap(send, "dp", 1 << steps[0]), send
+    for step in steps[1:-1]:
+        bit = (dp_index >> step) & 1
+        send = add(half_rows(keep, 1 - bit), half_rows(got, 1 - bit))
         keep = add(half_rows(keep, bit), half_rows(got, bit))
-        got = swap(sent, "dp", 1 << step)
-    return keep, got
-
-
-def gather_cells(total, dp_index, order):
-    total = add(total, swap(total, "dp", 1 << order[-1]))
-    for step in reversed(order[:-1]):
-        bit = (dp_index >> step) & 1
-        other = swap(total, "dp", 1 << step)
-        total = jnp.where(
-            bit == 0,
-            jnp.concatenate([total, other], axis=0),
-            jnp.concatenate([other, total], axis=0),
-        )
+        got = yield swap(send, "dp", 1 << step), send
+    total = add(keep, got)
+    got = yield swap(total, "dp", 1 << steps[-1]), total
+    total = add(total, got)
+    for step in reversed(steps[:-1]):
+        other = yield swap(total, "dp", 1 << step), total
+        total = join_rows(total, other, dp_index, step)
     return total
 
 
-def reduce_cells(keep, got, dp_index, order, done=0):
-    return gather_cells(
-        add(*scatter_cells(keep, got, dp_index, order[done:-1])), dp_index, order
-    )
+def whole_chain(total, steps):
+    for axis, distance in (("fsdp", 1), ("fsdp", 2)) + tuple(("dp", 1 << step) for step in steps):
+        got = yield swap(total, axis, distance), total
+        total = total + got
+    return total
+
+
+def take_turns(chains, turns, token):
+    pending = {name: next(chain)[0] for name, chain in chains.items()}
+    results = {}
+
+    def turn(name, token):
+        try:
+            pending[name], token = chains[name].send(tie(pending[name], token))
+        except StopIteration as stop:
+            results[name] = stop.value
+            del pending[name]
+        return token
+
+    for name in turns:
+        if name in pending:
+            token = turn(name, token)
+    while pending:
+        for name in list(pending):
+            token = turn(name, token)
+    return results
 
 
 def local(
@@ -516,28 +619,29 @@
     y_bit = d & 1
     where = jnp.stack([f, y_bit, (d >> 1) & 1]).astype(jnp.int32)
     order = tuple(range((lax.axis_size("dp") - 1).bit_length()))
-    other_order = (1, 0) + order[2:]
-
-    packed_rows = shards * rows + VEC_ROWS
-    packed, half, half_up = call(
+
+    z_bit = (d >> 1) & 1
+    first_own, second_own, first_half, second_half = call(
         pack_kernel,
         (
-            sds((packed_rows, width), bf16),
-            sds((packed_rows, width // 2), bf16),
-            sds((rows, hidden // 2), bf16),
+            sds((2 * rows + VEC_ROWS, width), bf16),
+            sds((2 * rows, width), bf16),
+            sds((2 * rows + VEC_ROWS, width // 2), bf16),
+            sds((2 * rows, width // 2), bf16),
         ),
         1,
-        7 + TB,
+        6 + TB,
         0,
         [pltpu.VMEM((VEC_ROWS, width), f32)],
         "pack",
+        resident=False,
+        limit=LARGE_VMEM_LIMIT,
     )(
         where,
         w_query,
         w_key,
         w_value,
         w_out,
-        w_up,
         b_query,
         b_value,
         b_out,
@@ -549,26 +653,29 @@
         table,
         b_up,
     )
-    across = swap(half, "fsdp", 2)
-    relayed = swap(across, "dp", 1)
-    attn = (
-        packed,
-        swap(packed, "fsdp", 1),
-        across,
-        relayed,
-        swap(across, "fsdp", 1),
-        swap(relayed, "fsdp", 1),
-    )
-    across_up = swap(tie(half_up, across), "fsdp", 2)
-    relayed_up = swap(across_up, "dp", 1)
-    up = (
-        w_up,
-        swap(w_up, "fsdp", 1),
-        across_up,
-        relayed_up,
-        swap(across_up, "fsdp", 1),
-    )
-    across_down = swap(tie(w_down, across_up), "fsdp", 2)
+
+    def relays(half, axis_bit):
+        across = swap(half, "fsdp", 2)
+        return across, swap(across, "dp", axis_bit)
+
+    def with_core(across, relayed, when=None):
+        if when is not None:
+            across, relayed = tie(across, when), tie(relayed, when)
+        return across, relayed, swap(across, "fsdp", 1), swap(relayed, "fsdp", 1)
+
+    first = relays(first_half, 1)
+    second = relays(tie(second_half, first_half), 1)
+    up_top = relays(tie(half_columns(w_up[: rows // 2], z_bit), first[0]), 2)
+    up_rest = swap(tie(w_up[rows // 2 :], first[0]), "fsdp", 2)
+    attn_first = (first_own, swap(first_own, "fsdp", 1), *with_core(*first))
+    attn_second = (second_own, swap(second_own, "fsdp", 1), *with_core(*second))
+    attn_first = tuple(map(in_hbm, attn_first))
+    attn_second = tuple(map(in_hbm, attn_second))
+    down_core = swap(w_down, "fsdp", 1)
+    up_core = swap(w_up, "fsdp", 1)
+    top = shard_hidden // 2
+    down_top = swap(tie(half_columns(w_down[:top], y_bit), up_top[0]), "fsdp", 2)
+    down_rest = swap(tie(half_columns(w_down[top:], z_bit), up_top[0]), "fsdp", 2)
 
     x_rows = inputs.reshape(tokens, width)
     cot_rows = cotangent.reshape(tokens, width)
@@ -581,18 +688,18 @@
             flat_low,
             flat_low,
             flat_low,
-            sds((4, tokens, rows), bf16),
-            sds((4, tokens, rows), bf16),
+            pltpu.HBM((4, tokens, rows), bf16),
+            pltpu.HBM((4, tokens, rows), bf16),
             flat,
             sds((tokens, 128), f32),
             flat_low,
-            sds((2, tokens, rows), bf16),
-            sds((2, tokens, rows), bf16),
+            pltpu.HBM((2, tokens, rows), bf16),
+            pltpu.HBM((2, tokens, rows), bf16),
             sds((VEC_ROWS, width), f32),
         ),
         2,
         2,
-        6,
+        12,
         [
             pltpu.VMEM((4, width, width), bf16),
             pltpu.VMEM((4 * VEC_ROWS, width), bf16),
@@ -602,35 +709,35 @@
         ],
         "attend",
         ATTEND_COST,
-    )(where, species, x_rows, gene_ids, *attn)
-    up += (swap(tie(relayed_up, q), "fsdp", 1),)
+    )(where, species, x_rows, gene_ids, *attn_first, *attn_second)
+    up_late = tie(up_rest, q)
+    up = (w_up, up_core, *with_core(*up_top, q), up_late, swap(up_late, "fsdp", 1))
+    down_top = tie(down_top, q)
+    down_top = (down_top, swap(down_top, "dp", 1))
     act, act_own, act_near, act_across, slope = call(
         up_kernel,
         (
             sds((shards, tokens, shard_hidden), bf16),
-            *(sds((tokens, shard_hidden), bf16),) * 2,
-            sds((2, tokens, shard_hidden), bf16),
+            *(pltpu.HBM((tokens, shard_hidden), bf16),) * 2,
+            pltpu.HBM((2, tokens, shard_hidden), bf16),
             sds((shards, tokens, shard_hidden), f32),
         ),
         1,
         2,
-        6,
-        [pltpu.VMEM((width, hidden), bf16), pltpu.SemaphoreType.DMA((6,))],
+        8,
+        [pltpu.VMEM((width, hidden), bf16), pltpu.SemaphoreType.DMA((8,))],
         "up",
     )(where, low, vec, *up)
-    down = (
-        w_down,
-        swap(w_down, "fsdp", 1),
-        across_down,
-        swap(tie(across_down, act_own), "fsdp", 1),
-    )
+    down_rest = tie(down_rest, act_own)
+    down_rest = (down_rest, swap(down_rest, "dp", 2))
+    down = (w_down, down_core, *with_core(*down_top, act_own), *with_core(*down_rest))
     output, gsec, glow, sm2 = call(
         down_kernel,
         (flat_low, flat, flat_low, small),
         1,
         4,
-        4,
-        [pltpu.VMEM((hidden, width), bf16), pltpu.SemaphoreType.DMA((4,))],
+        10,
+        [pltpu.VMEM((hidden, width), bf16), pltpu.SemaphoreType.DMA((10,))],
         "down",
     )(where, act, n1, vec, cot_rows, *down)
     act_got = swap(act_across, "fsdp", 2)
@@ -640,46 +747,28 @@
         (*(sds((tokens, shard_hidden), bf16),) * 4, sds((8, shard_hidden), f32)),
         1,
         2,
-        4,
-        [pltpu.VMEM((hidden, width), bf16), pltpu.SemaphoreType.DMA((4,))],
+        10,
+        [pltpu.VMEM((hidden, width), bf16), pltpu.SemaphoreType.DMA((10,))],
         "hidden_back",
     )(where, glow, slope, *down)
     guis_got = [swap(part, "fsdp", 1) for part in guis]
     gres, gbr, gatt, sm1 = call(
         norm_back_kernel,
-        (flat, flat_low, flat_low, small),
+        (pltpu.HBM(flat.shape, f32), flat_low, flat_low, small),
         1,
         8,
-        12,
+        14,
         [
             pltpu.VMEM((width, hidden), bf16),
             pltpu.VMEM((width, width), bf16),
-            pltpu.SemaphoreType.DMA((12,)),
+            pltpu.SemaphoreType.DMA((14,)),
         ],
         "norm_back",
-    )(where, gsec, n1, inv1, vec, *guis, *up, *attn)
-    act_all = (
-        act_own,
-        swap(tie(act_near, gbr), "fsdp", 1),
-        act_got,
-        swap(tie(act_got, gbr)[1], "fsdp", 1),
-    )
-    glow_all = (
-        glow,
-        swap(tie(glow, gbr), "fsdp", 1),
-        glow_across,
-        swap(tie(glow_across, gbr), "fsdp", 1),
-    )
-    send_up, keep_up = call(
-        near_up_kernel, (sds((rows, hidden), bf16),) * 2, 1, 10, 0, [], "near_up"
-    )(tie(where, gbr), low_own, swap(low_share, "fsdp", 1), *guis, *guis_got)
-    got_up = swap(send_up, "fsdp", 2)
-    down_half = sds((shard_hidden // 2, width), bf16)
-    send_down, keep_down = call(down_grad_kernel, (down_half,) * 2, 1, 8, 0, [], "down_grad")(
-        tie(where, send_up), *act_all, *glow_all
-    )
-    got_down = swap(send_down, "dp", 2)
-    grad_down = reduce_cells(keep_down, got_down, d, other_order, 1)
+    )(where, gsec, n1, inv1, vec, *guis, *up, *attn_second)
+    part = pltpu.HBM((2, rows // 4, hidden), bf16)
+    up_parts = call(near_up_kernel, (part,) * 4, 1, 10, 0, [], "near_up", resident=False)(
+        tie(where, gbr), in_hbm(low_own), in_hbm(swap(low_share, "fsdp", 1)), *guis, *guis_got
+    )
     gq, gk, gv = call(
         partial(attend_back_kernel, length=length),
         (flat_low, flat_low, flat_low),
@@ -688,41 +777,66 @@
         0,
         [],
         "attend_back",
-    )(q, k, v, tie(gatt, keep_down), gene_ids)
-    grad_up = reduce_cells(keep_up, got_up, d, order)
+    )(q, k, v, tie(gatt, up_parts[0]), gene_ids)
+    act_all = (
+        act_own,
+        swap(tie(act_near, gbr), "fsdp", 1),
+        act_got,
+        swap(tie(act_got, gbr)[1], "fsdp", 1),
+    )
+    glow_all = (
+        glow,
+        swap(tie(glow, gbr), "fsdp", 1),
+        glow_across,
+        swap(tie(glow_across, gq), "fsdp", 1),
+    )
     rights = [gbr, gv, gq, gk]
     rights_got = [swap(right, "fsdp", 1) for right in rights]
+    down_half = pltpu.HBM((shard_hidden // 2, width), bf16)
+    send_down, keep_down = call(down_grad_kernel, (down_half,) * 2, 1, 8, 0, [], "down_grad", resident=False)(
+        tie(where, gq), *map(in_hbm, act_all), glow, *map(in_hbm, glow_all[1:])
+    )
+    pair = pltpu.HBM((2, rows, width), bf16)
+    attn_parts = call(near_attn_kernel, (pair,) * 4, 1, 10, 0, [], "near_attn", resident=False)(
+        tie(where, keep_down), in_hbm(own_attn), in_hbm(swap(share_attn, "fsdp", 1)), *rights, *map(in_hbm, rights_got)
+    )
     gin, sm = call(
         partial(input_back_kernel, length=length),
         (flat_low, sds((VEC_ROWS, width), f32)),
         2,
         7,
-        6,
+        12,
         [pltpu.VMEM((3, width, width), bf16), pltpu.SemaphoreType.DMA((18,))],
         "input_back",
-    )(where, species, gres, gq, gk, gv, sm2, smu, sm1, *attn)
-    pair = sds((2 * rows, width), bf16)
-    both = sds((2, rows, width), bf16)
-    send_ov, keep_ov, send_qk, keep_qk = call(
-        near_attn_kernel, (pair, pair, both, both), 1, 10, 0, [], "near_attn"
-    )(tie(where, gin, got_down), own_attn, swap(share_attn, "fsdp", 1), *rights, *rights_got)
-    got_ov = swap(tie(send_ov, got_up), "fsdp", 2)
-    grad_ov = reduce_cells(keep_ov, got_ov, d, order)
-    keep_qk, got_qk = scatter_cells(keep_qk, swap(send_qk, "dp", 1), d, order[1:-1])
-    sent_qk = add(keep_qk[1], got_qk[1])
-    grad_qk = gather_cells(
-        (
-            keep_qk[0].astype(f32) + got_qk[0].astype(f32) + swap(sent_qk, "fsdp", 2).astype(f32)
-        ).astype(bf16),
-        d,
-        order,
-    )
-
-    sm = tie(sm, got_ov)
-    sm = sm + swap(sm, "fsdp", 1)
-    sm = sm + swap(sm, "fsdp", 2)
-    for step in order:
-        sm = sm + swap(sm, "dp", 1 << step)
+        resident=False,
+    )(
+        tie(where, attn_parts[0]),
+        species,
+        gres,
+        gq,
+        gk,
+        gv,
+        sm2,
+        smu,
+        sm1,
+        *attn_first,
+        *attn_second,
+    )
+    done = take_turns(
+        {
+            "up": two_way_chain(*up_parts, d, (1, 0), order[2:]),
+            "down": halving_chain(send_down, keep_down, d, order),
+            "attn": two_way_chain(*attn_parts, d, (0, 1), order[2:]),
+            "small": whole_chain(sm, order),
+        },
+        [{"U": "up", "D": "down", "A": "attn", "S": "small"}[name] for name in TURNS],
+        attn_parts[0],
+    )
+    grad_up = jnp.stack(done["up"]).reshape(rows, hidden)
+    grad_down = done["down"]
+    low_attn, high_attn = done["attn"]
+    sm = done["small"]
+
     mine = lax.dynamic_slice_in_dim(sm, f * rows, rows, 1)
     b_up_grad = lax.dynamic_slice_in_dim(sm, BU + f, 1, 0)[0]
 
@@ -730,12 +844,12 @@
         output.reshape(inputs.shape),
         gin.reshape(inputs.shape),
         mine[TB : TB + 2],
-        grad_qk[:rows].astype(f32),
+        low_attn[1].astype(f32),
         mine[BQ],
-        grad_qk[rows:].astype(f32),
-        grad_ov[rows:].astype(f32),
+        high_attn[1].astype(f32),
+        high_attn[0].astype(f32),
         mine[BV],
-        grad_ov[:rows].astype(f32),
+        low_attn[0].astype(f32),
         mine[BO],
         mine[G1],
         mine[S1],

time: 247 us -> 213 us (0.86)
  Pallas kernels: 73.4 us -> 53.9 us
  waiting for transfers between devices: 101 us -> 85.2 us
    ppermute x57 -> x68, waiting for transfers between devices: 101 us -> 85.2 us  [swap(): return lax.ppermute(x, axis, [(i, i ^ distance) for i in range(count)])]
    pallas_call x7, Pallas kernels: 40.7 us -> 29.9 us  [the longest x1 6.1 us: local(): call(up_kernel, (sds((shards, tokens, shard_hidden), bf16), *(pltpu.HBM((...]
    unnamed x76 -> x69, local copies, waits for them, and re-layouts: 6.25 us -> 2.29 us
    pallas_call x1, Pallas kernels: 6.59 us -> 2.97 us  [local(): call(hidden_back_kernel, (*(sds((tokens, shard_hidden), bf16),) * 4, sds(...]
    ppermute x57 -> x68, starting transfers between devices: 53.8 us -> 54.6 us  [swap(): return lax.ppermute(x, axis, [(i, i ^ distance) for i in range(count)])]
  transfers between devices with their start and end apart: 57 -> 68, of which waited for: 20 -> 27; matrix products, arithmetic and copies ran while one was open for 4% -> 5% of each run, Pallas kernels for 28% -> 24%
where the time goes in v2:
time: 213 us; the launch traced here: 210 us
  waiting for transfers between devices  85.2 us (40%)
  starting transfers between devices  54.6 us (26%)
  Pallas kernels  53.9 us (25%)
  other arithmetic  8.72 us (4%)
  local copies, waits for them, and re-layouts  6.46 us (3%)
    ppermute x68, waiting for transfers between devices, swap(): return lax.ppermute(x, axis, [(i, i ^ distance) for i in range(count)])  85.2 us
    ppermute x68, starting transfers between devices, swap(): return lax.ppermute(x, axis, [(i, i ^ distance) for i in range(count)])  54.6 us
    pallas_call x1, Pallas kernels, local(): call(partial(attend_kernel, length=length), (flat_low, flat_low, flat_low...  10.1 us
    pallas_call x1, Pallas kernels, local(): call(partial(attend_back_kernel, length=length), (flat_low, flat_low, fla...  6.24 us
    pallas_call x1, Pallas kernels, local(): call(up_kernel, (sds((shards, tokens, shard_hidden), bf16), *(pltpu.HBM((...  6.1 us
    pallas_call x1, Pallas kernels, local(): call(norm_back_kernel, (pltpu.HBM(flat.shape, f32), flat_low, flat_low, s...  5.2 us
    pallas_call x1, Pallas kernels, local(): call(partial(input_back_kernel, length=length), (flat_low, sds((VEC_ROWS,...  4.66 us
    pallas_call x1, Pallas kernels, local(): call(down_grad_kernel, (down_half,) * 2, 1, 8, 0, [], 'down_grad', reside...  4.36 us
  transfers between devices with their start and end apart: 68, of which 27 were waited for; matrix products, arithmetic and copies ran while one was open for 5% of the time, Pallas kernels for 24%

profile of v2, /device:TPU:0, one launch (start us, length us, event | category | flops | bytes accessed | tf_op | source)
XLA Modules:
  0.0 210.2 jit_solution(10526294641219804637)
XLA Ops:
  1.3 2.7 %pack.1 = (bf16[400,768]{1,0:T(8,128)(2,1)}, bf16[384,768]{1,0:T(8,128)(2,1)}, bf16[400,384]{1,0:T(8,128)(2,1)}, bf16[384,384]{1,0:T(8,128)(2,1)}) custom-call(s32[3]{0:T(128)} %pad_add_fusion.where_ref, bf16[192,768]{1,0:T(8,128)(2,1)} %q_ref.1, bf16[192,768]{1,0:T(8,128)(2,1)} %k_ref.1, bf16[192,768]{1,0:T(8,128)(2,1)} %v_ref.1, bf16[192,768]{1,0:T(8,128)(2,1)} %o_ref.1, ...), custom_call_target="tpu_custom_call" | custom-call | flops 1024 | bytes 1024 | tf_op jit(solution)/shard_map/pack/pallas_call | solution.py:624
  4.0 3.0 %collective-permute-start.6 = (bf16[384,384]{1,0:T(8,128)(2,1)}, bf16[384,384]{1,0:T(8,128)(2,1)}, u32[]{:S(2)}, u32[]{:S(2)}) collective-permute-start(bf16[384,384]{1,0:T(8,128)(2,1)} %get-tuple-element.117), channel_id=1, source_target_pairs={{0,2},{1,3},{2,0},{3,1},{4,6},{5,7},{6,4},{7,5},{8,10},{9,11},{10,... | collective-permute-start | bytes 884744 | tf_op jit(solution)/shard_map/swap_fsdp2/ppermute | solution.py:40
  7.5 7.6 %collective-permute-done.6.refs_8_.refs_14_ = bf16[384,384]{1,0:T(8,128)(2,1)} collective-permute-done((bf16[384,384]{1,0:T(8,128)(2,1)}, bf16[384,384]{1,0:T(8,128)(2,1)}, u32[]{:S(2)}, u32[]{:S(2)}) %collective-permute-start.6) | collective-permute-done | bytes 294944 | tf_op jit(solution)/shard_map/swap_fsdp2/ppermute | solution.py:40
  15.1 2.1 collective-permute-start.7
  17.2 1.1 fusion.14
  18.3 1.0 constant_dynamic-slice_fusion.3
  19.2 1.7 collective-permute-done.1.refs_2_
  20.9 1.7 collective-permute-start.11
  22.9 1.5 collective-permute-start.2
  25.3 3.9 %collective-permute-done.11.refs_2_.refs_6_ = bf16[96,1536]{1,0:T(8,128)(2,1)S(1)} collective-permute-done((bf16[96,1536]{1,0:T(8,128)(2,1)S(1)}, bf16[96,1536]{1,0:T(8,128)(2,1)S(1)}, u32[]{:S(2)}, u32[]{:S(2)}) %collective-permute-start.11) | collective-permute-done | bytes 294944 | tf_op jit(solution)/shard_map/swap_fsdp2/ppermute | solution.py:40
  29.2 1.5 collective-permute-start.15
  30.6 2.3 %collective-permute-done.2.refs_3_ = bf16[400,384]{1,0:T(8,128)(2,1)} collective-permute-done((bf16[400,384]{1,0:T(8,128)(2,1)}, bf16[400,384]{1,0:T(8,128)(2,1)}, u32[]{:S(2)}, u32[]{:S(2)}) %collective-permute-start.2) | collective-permute-done | bytes 307232 | tf_op jit(solution)/shard_map/swap_dp1/ppermute | solution.py:40
  33.7 2.5 %collective-permute-done.9.refs_11_.refs_17_ = bf16[384,384]{1,0:T(8,128)(2,1)S(1)} collective-permute-done((bf16[384,384]{1,0:T(8,128)(2,1)}, bf16[384,384]{1,0:T(8,128)(2,1)S(1)}, u32[]{:S(2)}, u32[]{:S(2)}) %collective-permute-start.9) | collective-permute-done | bytes 294944 | tf_op jit(solution)/shard_map/swap_fsdp1/ppermute | solution.py:40
  36.2 1.5 collective-permute-start.18
  37.6 1.6 collective-permute-start.12
  39.2 10.1 %attend.1 = (bf16[256,768]{1,0:T(8,128)(2,1)S(1)}, bf16[256,768]{1,0:T(8,128)(2,1)S(1)}, bf16[256,768]{1,0:T(8,128)(2,1)S(1)}, bf16[4,256,192]{2,1,0:T(8,128)(2,...) custom-call(s32[3]{0:T(128)S(1)} %copy-done.9, ...), custom_call_target="tpu_custom_call" | custom-call | flops 1024 | bytes 1024 | tf_op jit(solution)/shard_map/attend/pallas_call | solution.py:685
  50.7 1.1 collective-permute-done.14.refs_5_.refs_9_
  51.8 1.5 collective-permute-start.19
  53.4 6.1 %up.1 = (bf16[4,256,768]{2,1,0:T(8,128)(2,1)S(1)}, bf16[256,768]{1,0:T(8,128)(2,1)}, bf16[256,768]{1,0:T(8,128)(2,1)}, bf16[2,256,768]{2,1,0:T(8,128)(2,1)}, f32[4,256,768]{2,1,0:T(8,128)S(1)}) custom-call(s32[3]{0:T(128)S(1)} %copy-done.9, bf16[256,768]{1,0:T(8,128)(2,1)S(1)} %get-tuple-element.118.low_ref, f32[16,768]{1,0:T(8,128)S(1)} %get-tuple-element.119.vec_ref, ...), custom_call_target="tpu_custom_call" | custom-call | flops 1024 | bytes 1024 | tf_op jit(solution)/shard_map/up/pallas_call | solution.py:717
  60.3 1.4 collective-permute-start.32
  62.3 6.1 %collective-permute-done.23.refs_7_ = bf16[384,384]{1,0:T(8,128)(2,1)S(1)} collective-permute-done((bf16[384,384]{1,0:T(8,128)(2,1)S(1)}, bf16[384,384]{1,0:T(8,128)(2,1)S(1)}, u32[]{:S(2)}, u32[]{:S(2)}) %collective-permute-start.23) | collective-permute-done | bytes 294944 | tf_op jit(solution)/shard_map/swap_dp2/ppermute | solution.py:40
  68.3 1.6 collective-permute-done.25.refs_9_
  69.9 3.5 %down.1 = (bf16[256,768]{1,0:T(8,128)(2,1)S(1)}, f32[256,768]{1,0:T(8,128)S(1)}, bf16[256,768]{1,0:T(8,128)(2,1)S(1)}, f32[8,768]{1,0:T(8,128)S(1)}) custom-call(s32[3]{0:T(128)S(1)} %copy-done.9, bf16[4,256,768]{2,1,0:T(8,128)(2,1)S(1)} %get-tuple-element.126.act_ref, f32[256,768]{1,0:T(8,128)S(1)} %get-tuple-element.127.n1_ref, ...), custom_call_target="tpu_custom_call" | custom-call | flops 1024 | bytes 1024 | tf_op jit(solution)/shard_map/down/pallas_call | solution.py:734
  73.5 3.0 %hidden_back.1 = (bf16[256,768]{1,0:T(8,128)(2,1)S(1)}, bf16[256,768]{1,0:T(8,128)(2,1)S(1)}, bf16[256,768]{1,0:T(8,128)(2,1)S(1)}, bf16[256,768]{1,0:T(8,128)(2,1)S(1)}, f32[8,768]{1,0:T(8,128)S(1)}) custom-call(s32[3]{0:T(128)S(1)} %copy-done.9, bf16[256,768]{1,0:T(8,128)(2,1)S(1)} %get-tuple-element.159.glow_ref.refs_4_, ...), custom_call_target="tpu_custom_call" | custom-call | flops 1024 | bytes 1024 | tf_op jit(solution)/shard_map/hidden_back/pallas_call | solution.py:745
  77.5 1.1 collective-permute-done.26.got_ref
  79.5 1.2 collective-permute-start.35
  80.7 5.2 %norm_back.1 = (f32[256,768]{1,0:T(8,128)}, bf16[256,768]{1,0:T(8,128)(2,1)S(1)}, bf16[256,768]{1,0:T(8,128)(2,1)S(1)}, f32[8,768]{1,0:T(8,128)S(1)}) custom-call(s32[3]{0:T(128)S(1)} %copy-done.9, f32[256,768]{1,0:T(8,128)S(1)} %get-tuple-element.138.gsec_ref, f32[256,768]{1,0:T(8,128)S(1)} %get-tuple-element.127.n1_ref, ...), custom_call_target="tpu_custom_call" | custom-call | flops 1024 | bytes 1024 | tf_op jit(solution)/shard_map/norm_back/pallas_call | solution.py:755
  87.2 3.7 %near_up.1 = (bf16[2,48,3072]{2,1,0:T(8,128)(2,1)}, bf16[2,48,3072]{2,1,0:T(8,128)(2,1)}, bf16[2,48,3072]{2,1,0:T(8,128)(2,1)}, bf16[2,48,3072]{2,1,0:T(8,128)(2,1)}) custom-call(s32[3]{0:T(128)S(1)} %copy-done.9, bf16[2,256,192]{2,1,0:T(8,128)(2,1)} %get-tuple-element.149.own_ref, bf16[2,256,192]{2,1,0:T(8,128)(2,1)} %copy-done.27, ...), custom_call_target="tpu_custom_call" | custom-call | flops 1024 | bytes 1024 | tf_op jit(solution)/shard_map/near_up/pallas_call | solution.py:769
  90.9 6.2 %attend_back.1 = (bf16[256,768]{1,0:T(8,128)(2,1)S(1)}, bf16[256,768]{1,0:T(8,128)(2,1)S(1)}, bf16[256,768]{1,0:T(8,128)(2,1)S(1)}) custom-call(bf16[256,768]{1,0:T(8,128)(2,1)S(1)} %get-tuple-element.121.q_ref, bf16[256,768]{1,0:T(8,128)(2,1)S(1)} %get-tuple-element.136.k_ref, bf16[256,768]{1,0:T(8,128)(2,1)S(1)} %get-tuple-element.137.v_ref, ...), custom_call_target="tpu_custom_call" | custom-call | flops 1024 | bytes 1024 | tf_op jit(solution)/shard_map/attend_back/pallas_call | solution.py:772
  100.0 4.4 %down_grad.1 = (bf16[384,768]{1,0:T(8,128)(2,1)}, bf16[384,768]{1,0:T(8,128)(2,1)}) custom-call(s32[3]{0:T(128)S(1)} %copy-done.9, bf16[256,768]{1,0:T(8,128)(2,1)} %get-tuple-element.130.refs_0_, bf16[256,768]{1,0:T(8,128)(2,1)} %copy-done.24, bf16[2,256,768]{2,1,0:T(8,128)(2,1)} %copy-done.17, bf16[256,768]{1,0:T(8,128)(2,1)} %copy-done.25, ...), custom_call_target="tpu_custom_call" | custom-call | flops 1024 | bytes 1024 | tf_op jit(solution)/shard_map/down_grad/pallas_call | solution.py:796
  104.3 1.4 collective-permute-start.44
  105.7 4.3 %near_attn.1 = (bf16[2,192,768]{2,1,0:T(8,128)(2,1)}, bf16[2,192,768]{2,1,0:T(8,128)(2,1)}, bf16[2,192,768]{2,1,0:T(8,128)(2,1)}, bf16[2,192,768]{2,1,0:T(8,128)(2,1)}) custom-call(s32[3]{0:T(128)S(1)} %copy-done.9, bf16[4,256,192]{2,1,0:T(8,128)(2,1)} %get-tuple-element.163.own_ref, bf16[4,256,192]{2,1,0:T(8,128)(2,1)} %collective-permute-done.37.got_ref, ...), custom_call_target="tpu_custom_call" | custom-call | flops 1024 | bytes 1024 | tf_op jit(solution)/shard_map/near_attn/pallas_call | solution.py:800
  110.8 1.3 collective-permute-start.43
  112.1 4.7 %input_back.1 = (bf16[256,768]{1,0:T(8,128)(2,1)}, f32[16,768]{1,0:T(8,128)S(1)}) custom-call(s32[3]{0:T(128)S(1)} %copy-done.9, s32[2]{0:T(128)S(1)} %copy-done.11, f32[256,768]{1,0:T(8,128)S(1)} %copy-done.6, bf16[256,768]{1,0:T(8,128)(2,1)S(1)} %get-tuple-element.153.refs_2_.gq_ref, bf16[256,768]{1,0:T(8,128)(2,1)S(1)} %get-tuple-element.166.refs_3_.gk_ref, ...), custom_call_target="tpu_custom_call" | custom-call | flops 1024 | bytes 1024 | tf_op jit(solution)/shard_map/input_back/pallas_call | solution.py:803
  117.9 2.0 collective-permute-done.44
  119.9 1.2 collective-permute-start.51
  121.1 5.9 %collective-permute-done.43 = bf16[384,768]{1,0:T(8,128)(2,1)S(1)} collective-permute-done((bf16[384,768]{1,0:T(8,128)(2,1)S(1)}, bf16[384,768]{1,0:T(8,128)(2,1)S(1)}, u32[]{:S(2)}, u32[]{:S(2)}) %collective-permute-start.43) | collective-permute-done | bytes 589856 | tf_op jit(solution)/shard_map/swap_dp1/ppermute | solution.py:40
  127.0 1.3 collective-permute-start.50
  129.2 1.3 collective-permute-start.46
  130.6 4.1 %collective-permute-done.46 = f32[16,768]{1,0:T(8,128)S(1)} collective-permute-done((f32[16,768]{1,0:T(8,128)S(1)}, f32[16,768]{1,0:T(8,128)S(1)}, u32[]{:S(2)}, u32[]{:S(2)}) %collective-permute-start.46) | collective-permute-done | bytes 49184 | tf_op jit(solution)/shard_map/swap_fsdp2/ppermute | solution.py:40
  134.8 1.4 collective-permute-start.53
  137.2 1.5 collective-permute-start.58
  139.7 1.4 collective-permute-start.52
  141.2 2.6 %collective-permute-start.57 = (bf16[192,768]{1,0:T(8,128)(2,1)S(1)}, bf16[192,768]{1,0:T(8,128)(2,1)S(1)}, u32[]{:S(2)}, u32[]{:S(2)}) collective-permute-start(bf16[192,768]{1,0:T(8,128)(2,1)S(1)} %add_convert_fusion.5), channel_id=1, source_target_pairs={{0,16},{4,20},{8,24},{12,28},{16,0},{20,4},{24,8},{28,12},{1,17},{... | collective-permute-start | bytes 884744 | tf_op jit(solution)/shard_map/swap_dp4/ppermute | solution.py:40
  143.9 2.1 collective-permute-done.53
  146.7 1.3 collective-permute-start.56
  147.9 4.2 %collective-permute-done.58 = bf16[48,3072]{1,0:T(8,128)(2,1)S(1)} collective-permute-done((bf16[48,3072]{1,0:T(8,128)(2,1)S(1)}, bf16[48,3072]{1,0:T(8,128)(2,1)S(1)}, u32[]{:S(2)}, u32[]{:S(2)}) %collective-permute-start.58) | collective-permute-done | bytes 294944 | tf_op jit(solution)/shard_map/swap_dp1/ppermute | solution.py:40
  152.4 2.2 %collective-permute-done.57 = bf16[192,768]{1,0:T(8,128)(2,1)S(1)} collective-permute-done((bf16[192,768]{1,0:T(8,128)(2,1)S(1)}, bf16[192,768]{1,0:T(8,128)(2,1)S(1)}, u32[]{:S(2)}, u32[]{:S(2)}) %collective-permute-start.57) | collective-permute-done | bytes 294944 | tf_op jit(solution)/shard_map/swap_dp4/ppermute | solution.py:40
  154.9 1.8 collective-permute-start.55
  156.7 1.7 collective-permute-start.60
  158.4 8.7 %collective-permute-done.56 = bf16[192,768]{1,0:T(8,128)(2,1)S(1)} collective-permute-done((bf16[192,768]{1,0:T(8,128)(2,1)S(1)}, bf16[192,768]{1,0:T(8,128)(2,1)S(1)}, u32[]{:S(2)}, u32[]{:S(2)}) %collective-permute-start.56) | collective-permute-done | bytes 294944 | tf_op jit(solution)/shard_map/swap_dp2/ppermute | solution.py:40
  167.3 5.2 %collective-permute-done.55 = f32[16,768]{1,0:T(8,128)S(1)} collective-permute-done((f32[16,768]{1,0:T(8,128)S(1)}, f32[16,768]{1,0:T(8,128)S(1)}, u32[]{:S(2)}, u32[]{:S(2)}) %collective-permute-start.55) | collective-permute-done | bytes 49184 | tf_op jit(solution)/shard_map/swap_dp2/ppermute | solution.py:40
  172.8 8.4 %collective-permute-done.60 = bf16[48,3072]{1,0:T(8,128)(2,1)S(1)} collective-permute-done((bf16[48,3072]{1,0:T(8,128)(2,1)S(1)}, bf16[48,3072]{1,0:T(8,128)(2,1)S(1)}, u32[]{:S(2)}, u32[]{:S(2)}) %collective-permute-start.60) | collective-permute-done | bytes 294944 | tf_op jit(solution)/shard_map/swap_dp4/ppermute | solution.py:40
  181.3 1.5 collective-permute-start.64
  184.1 2.3 %collective-permute-done.59 = f32[16,768]{1,0:T(8,128)S(1)} collective-permute-done((f32[16,768]{1,0:T(8,128)S(1)}, f32[16,768]{1,0:T(8,128)S(1)}, u32[]{:S(2)}, u32[]{:S(2)}) %collective-permute-start.59) | collective-permute-done | bytes 49184 | tf_op jit(solution)/shard_map/swap_dp4/ppermute | solution.py:40
  187.1 1.0 collective-permute-done.64
  188.2 3.5 %collective-permute-start.66 = (bf16[2,48,3072]{2,1,0:T(8,128)(2,1)S(1)}, bf16[2,48,3072]{2,1,0:T(8,128)(2,1)S(1)}, u32[]{:S(2)}, u32[]{:S(2)}) collective-permute-start(bf16[2,48,3072]{2,1,0:T(8,128)(2,1)S(1)} %pad_maximum_fusion.1), channel_id=1, source_target_pairs={{0,8},{4,12},{8,0},{12,4},{16,24},{20,28},{24,16},{28,20},{1,9},{5... | collective-permute-start | bytes 1769480 | tf_op jit(solution)/shard_map/swap_dp2/ppermute | solution.py:40
  193.6 2.8 %collective-permute-done.63 = bf16[192,768]{1,0:T(8,128)(2,1)S(1)} collective-permute-done((bf16[192,768]{1,0:T(8,128)(2,1)S(1)}, bf16[192,768]{1,0:T(8,128)(2,1)S(1)}, u32[]{:S(2)}, u32[]{:S(2)}) %collective-permute-start.63) | collective-permute-done | bytes 294944 | tf_op jit(solution)/shard_map/swap_dp2/ppermute | solution.py:40
  196.5 1.7 collective-permute-start.65
  198.1 1.7 fusion
  199.8 6.2 %collective-permute-done.66 = bf16[2,48,3072]{2,1,0:T(8,128)(2,1)S(1)} collective-permute-done((bf16[2,48,3072]{2,1,0:T(8,128)(2,1)S(1)}, bf16[2,48,3072]{2,1,0:T(8,128)(2,1)S(1)}, u32[]{:S(2)}, u32[]{:S(2)}) %collective-permute-start.66) | collective-permute-done | bytes 589856 | tf_op jit(solution)/shard_map/swap_dp2/ppermute | solution.py:40
  206.2 1.7 bitcast_convert_fusion
  208.0 1.1 fusion.9
  209.1 1.1 fusion.10
  (193 shorter events, 23.0 us)
Async XLA Ops:
  4.0 11.1 %collective-permute-start.6 = (bf16[384,384]{1,0:T(8,128)(2,1)}, bf16[384,384]{1,0:T(8,128)(2,1)}, u32[]{:S(2)}, u32[]{:S(2)}) collective-permute-start(bf16[384,384]{1,0:T(8,128)(2,1)} %get-tuple-element.117), channel_id=1, source_target_pairs={{0,2},{1,3},{2,0},{3,1},{4,6},{5,7},{6,4},{7,5},{8,10},{9,11},{10,... | collective-permute-start | bytes 884744 | tf_op jit(solution)/shard_map/swap_fsdp2/ppermute | solution.py:40
  6.9 14.0 %collective-permute-start.1 = (bf16[400,384]{1,0:T(8,128)(2,1)}, bf16[400,384]{1,0:T(8,128)(2,1)}, u32[]{:S(2)}, u32[]{:S(2)}) collective-permute-start(bf16[400,384]{1,0:T(8,128)(2,1)} %get-tuple-element.114), channel_id=1, source_target_pairs={{0,2},{1,3},{2,0},{3,1},{4,6},{5,7},{6,4},{7,5},{8,10},{9,11},{10,... | collective-permute-start | bytes 921608 | tf_op jit(solution)/shard_map/swap_fsdp2/ppermute | solution.py:40
  7.0 17.4 %collective-permute-start.5 = (bf16[384,768]{1,0:T(8,128)(2,1)}, bf16[384,768]{1,0:T(8,128)(2,1)S(1)}, u32[]{:S(2)}, u32[]{:S(2)}) collective-permute-start(bf16[384,768]{1,0:T(8,128)(2,1)} %get-tuple-element.115.refs_6_.refs_12_), channel_id=1, source_target_pairs={{0,1},{1,0},{2,3},{3,2},{4,5},{5,4},{6,7},{7,6},{8,9},{9,8},{10,11... | collective-permute-start | bytes 1769480 | tf_op jit(solution)/shard_map/swap_fsdp1/ppermute | solution.py:40
  7.0 26.4 %collective-permute-start = (bf16[400,768]{1,0:T(8,128)(2,1)}, bf16[400,768]{1,0:T(8,128)(2,1)}, u32[]{:S(2)}, u32[]{:S(2)}) collective-permute-start(bf16[400,768]{1,0:T(8,128)(2,1)} %get-tuple-element.113.refs_0_), channel_id=1, source_target_pairs={{0,1},{1,0},{2,3},{3,2},{4,5},{5,4},{6,7},{7,6},{8,9},{9,8},{10,11... | collective-permute-start | bytes 1843208 | tf_op jit(solution)/shard_map/swap_fsdp1/ppermute | solution.py:40
  15.1 7.8 %collective-permute-start.7 = (bf16[384,384]{1,0:T(8,128)(2,1)}, bf16[384,384]{1,0:T(8,128)(2,1)}, u32[]{:S(2)}, u32[]{:S(2)}) collective-permute-start(bf16[384,384]{1,0:T(8,128)(2,1)} %collective-permute-done.6.refs_8_.refs_14_), channel_id=1, source_target_pairs={{0,4},{4,0},{8,12},{12,8},{16,20},{20,16},{24,28},{28,24},{1,5},{5... | collective-permute-start | bytes 884744 | tf_op jit(solution)/shard_map/swap_dp1/ppermute | solution.py:40
  18.3 4.6 %collective-permute-start.8 = (bf16[384,384]{1,0:T(8,128)(2,1)}, bf16[384,384]{1,0:T(8,128)(2,1)S(1)}, u32[]{:S(2)}, u32[]{:S(2)}) collective-permute-start(bf16[384,384]{1,0:T(8,128)(2,1)} %collective-permute-done.6.refs_8_.refs_14_), channel_id=1, source_target_pairs={{0,1},{1,0},{2,3},{3,2},{4,5},{5,4},{6,7},{7,6},{8,9},{9,8},{10,11... | collective-permute-start | bytes 884744 | tf_op jit(solution)/shard_map/swap_fsdp1/ppermute | solution.py:40
  20.9 8.2 %collective-permute-start.11 = (bf16[96,1536]{1,0:T(8,128)(2,1)S(1)}, bf16[96,1536]{1,0:T(8,128)(2,1)S(1)}, u32[]{:S(2)}, u32[]{:S(2)}) collective-permute-start(bf16[96,1536]{1,0:T(8,128)(2,1)S(1)} %constant_dynamic-slice_fusion.3), channel_id=1, source_target_pairs={{0,2},{1,3},{2,0},{3,1},{4,6},{5,7},{6,4},{7,5},{8,10},{9,11},{10,... | collective-permute-start | bytes 884744 | tf_op jit(solution)/shard_map/swap_fsdp2/ppermute | solution.py:40
  22.9 27.1 %collective-permute-start.10 = (bf16[192,3072]{1,0:T(8,128)(2,1)S(1)}, bf16[192,3072]{1,0:T(8,128)(2,1)}, u32[]{:S(2)}, u32[]{:S(2)}) collective-permute-start(bf16[192,3072]{1,0:T(8,128)(2,1)S(1)} %copy-done), channel_id=1, source_target_pairs={{0,1},{1,0},{2,3},{3,2},{4,5},{5,4},{6,7},{7,6},{8,9},{9,8},{10,11... | collective-permute-start | bytes 3538952 | tf_op jit(solution)/shard_map/swap_fsdp1/ppermute | solution.py:40
  22.9 10.0 %collective-permute-start.2 = (bf16[400,384]{1,0:T(8,128)(2,1)}, bf16[400,384]{1,0:T(8,128)(2,1)}, u32[]{:S(2)}, u32[]{:S(2)}) collective-permute-start(bf16[400,384]{1,0:T(8,128)(2,1)} %collective-permute-done.1.refs_2_), channel_id=1, source_target_pairs={{0,4},{4,0},{8,12},{12,8},{16,20},{20,16},{24,28},{28,24},{1,5},{5... | collective-permute-start | bytes 921608 | tf_op jit(solution)/shard_map/swap_dp1/ppermute | solution.py:40
  24.4 8.5 %collective-permute-start.3 = (bf16[400,384]{1,0:T(8,128)(2,1)}, bf16[400,384]{1,0:T(8,128)(2,1)}, u32[]{:S(2)}, u32[]{:S(2)}) collective-permute-start(bf16[400,384]{1,0:T(8,128)(2,1)} %collective-permute-done.1.refs_2_), channel_id=1, source_target_pairs={{0,1},{1,0},{2,3},{3,2},{4,5},{5,4},{6,7},{7,6},{8,9},{9,8},{10,11... | collective-permute-start | bytes 921608 | tf_op jit(solution)/shard_map/swap_fsdp1/ppermute | solution.py:40
  29.2 20.2 %collective-permute-start.15 = (bf16[96,3072]{1,0:T(8,128)(2,1)}, bf16[96,3072]{1,0:T(8,128)(2,1)S(1)}, u32[]{:S(2)}, u32[]{:S(2)}) collective-permute-start(bf16[96,3072]{1,0:T(8,128)(2,1)} %get-tuple-element.124), channel_id=1, source_target_pairs={{0,2},{1,3},{2,0},{3,1},{4,6},{5,7},{6,4},{7,5},{8,10},{9,11},{10,... | collective-permute-start | bytes 1769480 | tf_op jit(solution)/shard_map/swap_fsdp2/ppermute | solution.py:40
  32.9 29.3 %collective-permute-start.17 = (bf16[768,768]{1,0:T(8,128)(2,1)S(1)}, bf16[768,768]{1,0:T(8,128)(2,1)S(1)}, u32[]{:S(2)}, u32[]{:S(2)}) collective-permute-start(bf16[768,768]{1,0:T(8,128)(2,1)S(1)} %copy-done.1), channel_id=1, source_target_pairs={{0,1},{1,0},{2,3},{3,2},{4,5},{5,4},{6,7},{7,6},{8,9},{9,8},{10,11... | collective-permute-start | bytes 3538952 | tf_op jit(solution)/shard_map/swap_fsdp1/ppermute | solution.py:40
  32.9 3.3 %collective-permute-start.9 = (bf16[384,384]{1,0:T(8,128)(2,1)}, bf16[384,384]{1,0:T(8,128)(2,1)S(1)}, u32[]{:S(2)}, u32[]{:S(2)}) collective-permute-start(bf16[384,384]{1,0:T(8,128)(2,1)} %collective-permute-done.7.refs_9_.refs_15_), channel_id=1, source_target_pairs={{0,1},{1,0},{2,3},{3,2},{4,5},{5,4},{6,7},{7,6},{8,9},{9,8},{10,11... | collective-permute-start | bytes 884744 | tf_op jit(solution)/shard_map/swap_fsdp1/ppermute | solution.py:40
  33.4 4.2 %collective-permute-start.4 = (bf16[400,384]{1,0:T(8,128)(2,1)}, bf16[400,384]{1,0:T(8,128)(2,1)S(1)}, u32[]{:S(2)}, u32[]{:S(2)}) collective-permute-start(bf16[400,384]{1,0:T(8,128)(2,1)} %collective-permute-done.2.refs_3_), channel_id=1, source_target_pairs={{0,1},{1,0},{2,3},{3,2},{4,5},{5,4},{6,7},{7,6},{8,9},{9,8},{10,11... | collective-permute-start | bytes 921608 | tf_op jit(solution)/shard_map/swap_fsdp1/ppermute | solution.py:40
  36.2 13.8 %collective-permute-start.18 = (bf16[384,384]{1,0:T(8,128)(2,1)S(1)}, bf16[384,384]{1,0:T(8,128)(2,1)S(1)}, u32[]{:S(2)}, u32[]{:S(2)}) collective-permute-start(bf16[384,384]{1,0:T(8,128)(2,1)S(1)} %get-tuple-element.128), channel_id=1, source_target_pairs={{0,2},{1,3},{2,0},{3,1},{4,6},{5,7},{6,4},{7,5},{8,10},{9,11},{10,... | collective-permute-start | bytes 884744 | tf_op jit(solution)/shard_map/swap_fsdp2/ppermute | solution.py:40
  37.6 11.8 %collective-permute-start.12 = (bf16[96,1536]{1,0:T(8,128)(2,1)S(1)}, bf16[96,1536]{1,0:T(8,128)(2,1)S(1)}, u32[]{:S(2)}, u32[]{:S(2)}) collective-permute-start(bf16[96,1536]{1,0:T(8,128)(2,1)S(1)} %collective-permute-done.11.refs_2_.refs_6_), channel_id=1, source_target_pairs={{0,8},{4,12},{8,0},{12,4},{16,24},{20,28},{24,16},{28,20},{1,9},{5... | collective-permute-start | bytes 884744 | tf_op jit(solution)/shard_map/swap_dp2/ppermute | solution.py:40
  49.3 4.0 %collective-permute-start.16 = (bf16[96,3072]{1,0:T(8,128)(2,1)S(1)}, bf16[96,3072]{1,0:T(8,128)(2,1)S(1)}, u32[]{:S(2)}, u32[]{:S(2)}) collective-permute-start(bf16[96,3072]{1,0:T(8,128)(2,1)S(1)} %collective-permute-done.15.refs_6_.refs_10_), channel_id=1, source_target_pairs={{0,1},{1,0},{2,3},{3,2},{4,5},{5,4},{6,7},{7,6},{8,9},{9,8},{10,11... | collective-permute-start | bytes 1769480 | tf_op jit(solution)/shard_map/swap_fsdp1/ppermute | solution.py:40
  49.9 3.4 %collective-permute-start.13 = (bf16[96,1536]{1,0:T(8,128)(2,1)S(1)}, bf16[96,1536]{1,0:T(8,128)(2,1)S(1)}, u32[]{:S(2)}, u32[]{:S(2)}) collective-permute-start(bf16[96,1536]{1,0:T(8,128)(2,1)S(1)} %collective-permute-done.11.refs_2_.refs_6_), channel_id=1, source_target_pairs={{0,1},{1,0},{2,3},{3,2},{4,5},{5,4},{6,7},{7,6},{8,9},{9,8},{10,11... | collective-permute-start | bytes 884744 | tf_op jit(solution)/shard_map/swap_fsdp1/ppermute | solution.py:40
  50.0 9.5 %collective-permute-start.22 = (bf16[384,384]{1,0:T(8,128)(2,1)S(1)}, bf16[384,384]{1,0:T(8,128)(2,1)S(1)}, u32[]{:S(2)}, u32[]{:S(2)}) collective-permute-start(bf16[384,384]{1,0:T(8,128)(2,1)S(1)} %get-tuple-element.133), channel_id=1, source_target_pairs={{0,2},{1,3},{2,0},{3,1},{4,6},{5,7},{6,4},{7,5},{8,10},{9,11},{10,... | collective-permute-start | bytes 884744 | tf_op jit(solution)/shard_map/swap_fsdp2/ppermute | solution.py:40
  51.8 9.9 %collective-permute-start.19 = (bf16[384,384]{1,0:T(8,128)(2,1)S(1)}, bf16[384,384]{1,0:T(8,128)(2,1)S(1)}, u32[]{:S(2)}, u32[]{:S(2)}) collective-permute-start(bf16[384,384]{1,0:T(8,128)(2,1)S(1)} %collective-permute-done.18.refs_2_), channel_id=1, source_target_pairs={{0,4},{4,0},{8,12},{12,8},{16,20},{20,16},{24,28},{28,24},{1,5},{5... | collective-permute-start | bytes 884744 | tf_op jit(solution)/shard_map/swap_dp1/ppermute | solution.py:40
  59.5 8.8 %collective-permute-start.23 = (bf16[384,384]{1,0:T(8,128)(2,1)S(1)}, bf16[384,384]{1,0:T(8,128)(2,1)S(1)}, u32[]{:S(2)}, u32[]{:S(2)}) collective-permute-start(bf16[384,384]{1,0:T(8,128)(2,1)S(1)} %collective-permute-done.22.refs_6_), channel_id=1, source_target_pairs={{0,8},{4,12},{8,0},{12,4},{16,24},{20,28},{24,16},{28,20},{1,9},{5... | collective-permute-start | bytes 884744 | tf_op jit(solution)/shard_map/swap_dp2/ppermute | solution.py:40
  60.3 19.2 %collective-permute-start.32 = (bf16[2,256,768]{2,1,0:T(8,128)(2,1)}, bf16[2,256,768]{2,1,0:T(8,128)(2,1)S(1)}, u32[]{:S(2)}, u32[]{:S(2)}) collective-permute-start(bf16[2,256,768]{2,1,0:T(8,128)(2,1)} %get-tuple-element.157), channel_id=1, source_target_pairs={{0,2},{1,3},{2,0},{3,1},{4,6},{5,7},{6,4},{7,5},{8,10},{9,11},{10,... | collective-permute-start | bytes 2359304 | tf_op jit(solution)/shard_map/swap_fsdp2/ppermute | solution.py:40
  61.7 6.7 %collective-permute-start.24 = (bf16[384,384]{1,0:T(8,128)(2,1)S(1)}, bf16[384,384]{1,0:T(8,128)(2,1)S(1)}, u32[]{:S(2)}, u32[]{:S(2)}) collective-permute-start(bf16[384,384]{1,0:T(8,128)(2,1)S(1)} %collective-permute-done.22.refs_6_), channel_id=1, source_target_pairs={{0,1},{1,0},{2,3},{3,2},{4,5},{5,4},{6,7},{7,6},{8,9},{9,8},{10,11... | collective-permute-start | bytes 884744 | tf_op jit(solution)/shard_map/swap_fsdp1/ppermute | solution.py:40
  61.7 6.6 %collective-permute-start.21 = (bf16[384,384]{1,0:T(8,128)(2,1)S(1)}, bf16[384,384]{1,0:T(8,128)(2,1)S(1)}, u32[]{:S(2)}, u32[]{:S(2)}) collective-permute-start(bf16[384,384]{1,0:T(8,128)(2,1)S(1)} %collective-permute-done.19.refs_3_), channel_id=1, source_target_pairs={{0,1},{1,0},{2,3},{3,2},{4,5},{5,4},{6,7},{7,6},{8,9},{9,8},{10,11... | collective-permute-start | bytes 884744 | tf_op jit(solution)/shard_map/swap_fsdp1/ppermute | solution.py:40
  62.2 6.1 %collective-permute-start.20 = (bf16[384,384]{1,0:T(8,128)(2,1)S(1)}, bf16[384,384]{1,0:T(8,128)(2,1)S(1)}, u32[]{:S(2)}, u32[]{:S(2)}) collective-permute-start(bf16[384,384]{1,0:T(8,128)(2,1)S(1)} %collective-permute-done.18.refs_2_), channel_id=1, source_target_pairs={{0,1},{1,0},{2,3},{3,2},{4,5},{5,4},{6,7},{7,6},{8,9},{9,8},{10,11... | collective-permute-start | bytes 884744 | tf_op jit(solution)/shard_map/swap_fsdp1/ppermute | solution.py:40
  76.5 9.5 %collective-permute-start.27 = (bf16[256,768]{1,0:T(8,128)(2,1)S(1)}, bf16[256,768]{1,0:T(8,128)(2,1)S(1)}, u32[]{:S(2)}, u32[]{:S(2)}) collective-permute-start(bf16[256,768]{1,0:T(8,128)(2,1)S(1)} %get-tuple-element.142.refs_0_), channel_id=1, source_target_pairs={{0,1},{1,0},{2,3},{3,2},{4,5},{5,4},{6,7},{7,6},{8,9},{9,8},{10,11... | collective-permute-start | bytes 1179656 | tf_op jit(solution)/shard_map/swap_fsdp1/ppermute | solution.py:40
  77.0 9.1 %collective-permute-start.28 = (bf16[256,768]{1,0:T(8,128)(2,1)S(1)}, bf16[256,768]{1,0:T(8,128)(2,1)S(1)}, u32[]{:S(2)}, u32[]{:S(2)}) collective-permute-start(bf16[256,768]{1,0:T(8,128)(2,1)S(1)} %get-tuple-element.143.refs_1_), channel_id=1, source_target_pairs={{0,1},{1,0},{2,3},{3,2},{4,5},{5,4},{6,7},{7,6},{8,9},{9,8},{10,11... | collective-permute-start | bytes 1179656 | tf_op jit(solution)/shard_map/swap_fsdp1/ppermute | solution.py:40
  77.2 9.5 %collective-permute-start.29 = (bf16[256,768]{1,0:T(8,128)(2,1)S(1)}, bf16[256,768]{1,0:T(8,128)(2,1)S(1)}, u32[]{:S(2)}, u32[]{:S(2)}) collective-permute-start(bf16[256,768]{1,0:T(8,128)(2,1)S(1)} %get-tuple-element.144.refs_2_), channel_id=1, source_target_pairs={{0,1},{1,0},{2,3},{3,2},{4,5},{5,4},{6,7},{7,6},{8,9},{9,8},{10,11... | collective-permute-start | bytes 1179656 | tf_op jit(solution)/shard_map/swap_fsdp1/ppermute | solution.py:40
  78.6 8.1 %collective-permute-start.30 = (bf16[256,768]{1,0:T(8,128)(2,1)S(1)}, bf16[256,768]{1,0:T(8,128)(2,1)S(1)}, u32[]{:S(2)}, u32[]{:S(2)}) collective-permute-start(bf16[256,768]{1,0:T(8,128)(2,1)S(1)} %get-tuple-element.145.refs_3_), channel_id=1, source_target_pairs={{0,1},{1,0},{2,3},{3,2},{4,5},{5,4},{6,7},{7,6},{8,9},{9,8},{10,11... | collective-permute-start | bytes 1179656 | tf_op jit(solution)/shard_map/swap_fsdp1/ppermute | solution.py:40
  79.5 17.6 %collective-permute-start.35 = (bf16[256,768]{1,0:T(8,128)(2,1)S(1)}, bf16[256,768]{1,0:T(8,128)(2,1)S(1)}, u32[]{:S(2)}, u32[]{:S(2)}) collective-permute-start(bf16[256,768]{1,0:T(8,128)(2,1)S(1)} %get-tuple-element.159.glow_ref.refs_4_), channel_id=1, source_target_pairs={{0,2},{1,3},{2,0},{3,1},{4,6},{5,7},{6,4},{7,5},{8,10},{9,11},{10,... | collective-permute-start | bytes 1179656 | tf_op jit(solution)/shard_map/swap_fsdp2/ppermute | solution.py:40
  86.0 11.3 %collective-permute-start.37 = (bf16[4,256,192]{2,1,0:T(8,128)(2,1)S(1)}, bf16[4,256,192]{2,1,0:T(8,128)(2,1)}, u32[]{:S(2)}, u32[]{:S(2)}) collective-permute-start(bf16[4,256,192]{2,1,0:T(8,128)(2,1)S(1)} %copy-done.31), channel_id=1, source_target_pairs={{0,1},{1,0},{2,3},{3,2},{4,5},{5,4},{6,7},{7,6},{8,9},{9,8},{10,11... | collective-permute-start | bytes 1179656 | tf_op jit(solution)/shard_map/swap_fsdp1/ppermute | solution.py:40
  86.1 12.0 %collective-permute-start.34 = (bf16[256,768]{1,0:T(8,128)(2,1)S(1)}, bf16[256,768]{1,0:T(8,128)(2,1)}, u32[]{:S(2)}, u32[]{:S(2)}) collective-permute-start(bf16[256,768]{1,0:T(8,128)(2,1)S(1)} %get-tuple-element.159.glow_ref.refs_4_), channel_id=1, source_target_pairs={{0,1},{1,0},{2,3},{3,2},{4,5},{5,4},{6,7},{7,6},{8,9},{9,8},{10,11... | collective-permute-start | bytes 1179656 | tf_op jit(solution)/shard_map/swap_fsdp1/ppermute | solution.py:40
  86.7 11.6 %collective-permute-start.31 = (bf16[256,768]{1,0:T(8,128)(2,1)S(1)}, bf16[256,768]{1,0:T(8,128)(2,1)S(1)}, u32[]{:S(2)}, u32[]{:S(2)}) collective-permute-start(bf16[256,768]{1,0:T(8,128)(2,1)S(1)} %copy-done.32), channel_id=1, source_target_pairs={{0,1},{1,0},{2,3},{3,2},{4,5},{5,4},{6,7},{7,6},{8,9},{9,8},{10,11... | collective-permute-start | bytes 1179656 | tf_op jit(solution)/shard_map/swap_fsdp1/ppermute | solution.py:40
  86.8 11.9 %collective-permute-start.33 = (bf16[256,768]{1,0:T(8,128)(2,1)S(1)}, bf16[256,768]{1,0:T(8,128)(2,1)S(1)}, u32[]{:S(2)}, u32[]{:S(2)}) collective-permute-start(bf16[256,768]{1,0:T(8,128)(2,1)S(1)} %slice_bitcast_fusion), channel_id=1, source_target_pairs={{0,1},{1,0},{2,3},{3,2},{4,5},{5,4},{6,7},{7,6},{8,9},{9,8},{10,11... | collective-permute-start | bytes 1179656 | tf_op jit(solution)/shard_map/swap_fsdp1/ppermute | solution.py:40
  97.3 19.6 %collective-permute-start.45 = (bf16[2,48,3072]{2,1,0:T(8,128)(2,1)}, bf16[2,48,3072]{2,1,0:T(8,128)(2,1)S(1)}, u32[]{:S(2)}, u32[]{:S(2)}) collective-permute-start(bf16[2,48,3072]{2,1,0:T(8,128)(2,1)} %get-tuple-element.151), channel_id=1, source_target_pairs={{0,2},{1,3},{2,0},{3,1},{4,6},{5,7},{6,4},{7,5},{8,10},{9,11},{10,... | collective-permute-start | bytes 1769480 | tf_op jit(solution)/shard_map/swap_fsdp2/ppermute | solution.py:40
  98.1 6.2 %collective-permute-start.38 = (bf16[256,768]{1,0:T(8,128)(2,1)S(1)}, bf16[256,768]{1,0:T(8,128)(2,1)S(1)}, u32[]{:S(2)}, u32[]{:S(2)}) collective-permute-start(bf16[256,768]{1,0:T(8,128)(2,1)S(1)} %get-tuple-element.147.refs_0_), channel_id=1, source_target_pairs={{0,1},{1,0},{2,3},{3,2},{4,5},{5,4},{6,7},{7,6},{8,9},{9,8},{10,11... | collective-permute-start | bytes 1179656 | tf_op jit(solution)/shard_map/swap_fsdp1/ppermute | solution.py:40
  98.3 7.4 %collective-permute-start.40 = (bf16[256,768]{1,0:T(8,128)(2,1)S(1)}, bf16[256,768]{1,0:T(8,128)(2,1)}, u32[]{:S(2)}, u32[]{:S(2)}) collective-permute-start(bf16[256,768]{1,0:T(8,128)(2,1)S(1)} %get-tuple-element.153.refs_2_.gq_ref), channel_id=1, source_target_pairs={{0,1},{1,0},{2,3},{3,2},{4,5},{5,4},{6,7},{7,6},{8,9},{9,8},{10,11... | collective-permute-start | bytes 1179656 | tf_op jit(solution)/shard_map/swap_fsdp1/ppermute | solution.py:40
  98.7 7.0 %collective-permute-start.39 = (bf16[256,768]{1,0:T(8,128)(2,1)S(1)}, bf16[256,768]{1,0:T(8,128)(2,1)}, u32[]{:S(2)}, u32[]{:S(2)}) collective-permute-start(bf16[256,768]{1,0:T(8,128)(2,1)S(1)} %get-tuple-element.165.refs_1_.gv_ref), channel_id=1, source_target_pairs={{0,1},{1,0},{2,3},{3,2},{4,5},{5,4},{6,7},{7,6},{8,9},{9,8},{10,11... | collective-permute-start | bytes 1179656 | tf_op jit(solution)/shard_map/swap_fsdp1/ppermute | solution.py:40
  99.7 6.0 %collective-permute-start.41 = (bf16[256,768]{1,0:T(8,128)(2,1)S(1)}, bf16[256,768]{1,0:T(8,128)(2,1)}, u32[]{:S(2)}, u32[]{:S(2)}) collective-permute-start(bf16[256,768]{1,0:T(8,128)(2,1)S(1)} %get-tuple-element.166.refs_3_.gk_ref), channel_id=1, source_target_pairs={{0,1},{1,0},{2,3},{3,2},{4,5},{5,4},{6,7},{7,6},{8,9},{9,8},{10,11... | collective-permute-start | bytes 1179656 | tf_op jit(solution)/shard_map/swap_fsdp1/ppermute | solution.py:40
  104.3 15.6 %collective-permute-start.44 = (bf16[2,48,3072]{2,1,0:T(8,128)(2,1)S(1)}, bf16[2,48,3072]{2,1,0:T(8,128)(2,1)S(1)}, u32[]{:S(2)}, u32[]{:S(2)}) collective-permute-start(bf16[2,48,3072]{2,1,0:T(8,128)(2,1)S(1)} %copy-done.28), channel_id=1, source_target_pairs={{0,8},{4,12},{8,0},{12,4},{16,24},{20,28},{24,16},{28,20},{1,9},{5... | collective-permute-start | bytes 1769480 | tf_op jit(solution)/shard_map/swap_dp2/ppermute | solution.py:40
  110.1 19.1 %collective-permute-start.47 = (bf16[2,192,768]{2,1,0:T(8,128)(2,1)}, bf16[2,192,768]{2,1,0:T(8,128)(2,1)S(1)}, u32[]{:S(2)}, u32[]{:S(2)}) collective-permute-start(bf16[2,192,768]{2,1,0:T(8,128)(2,1)} %get-tuple-element.167), channel_id=1, source_target_pairs={{0,2},{1,3},{2,0},{3,1},{4,6},{5,7},{6,4},{7,5},{8,10},{9,11},{10,... | collective-permute-start | bytes 1769480 | tf_op jit(solution)/shard_map/swap_fsdp2/ppermute | solution.py:40
  110.8 16.2 %collective-permute-start.43 = (bf16[384,768]{1,0:T(8,128)(2,1)S(1)}, bf16[384,768]{1,0:T(8,128)(2,1)S(1)}, u32[]{:S(2)}, u32[]{:S(2)}) collective-permute-start(bf16[384,768]{1,0:T(8,128)(2,1)S(1)} %copy-done.30), channel_id=1, source_target_pairs={{0,4},{4,0},{8,12},{12,8},{16,20},{20,16},{24,28},{28,24},{1,5},{5... | collective-permute-start | bytes 1769480 | tf_op jit(solution)/shard_map/swap_dp1/ppermute | solution.py:40
  116.8 11.6 %collective-permute-start.42 = (f32[16,768]{1,0:T(8,128)S(1)}, f32[16,768]{1,0:T(8,128)S(1)}, u32[]{:S(2)}, u32[]{:S(2)}) collective-permute-start(f32[16,768]{1,0:T(8,128)S(1)} %get-tuple-element.174), channel_id=1, source_target_pairs={{0,1},{1,0},{2,3},{3,2},{4,5},{5,4},{6,7},{7,6},{8,9},{9,8},{10,11... | collective-permute-start | bytes 147464 | tf_op jit(solution)/shard_map/swap_fsdp1/ppermute | solution.py:40
  116.9 22.7 %collective-permute-start.49 = (bf16[2,192,768]{2,1,0:T(8,128)(2,1)S(1)}, bf16[2,192,768]{2,1,0:T(8,128)(2,1)S(1)}, u32[]{:S(2)}, u32[]{:S(2)}) collective-permute-start(bf16[2,192,768]{2,1,0:T(8,128)(2,1)S(1)} %copy-done.29), channel_id=1, source_target_pairs={{0,4},{4,0},{8,12},{12,8},{16,20},{20,16},{24,28},{28,24},{1,5},{5... | collective-permute-start | bytes 1769480 | tf_op jit(solution)/shard_map/swap_dp1/ppermute | solution.py:40
  119.9 16.3 %collective-permute-start.51 = (bf16[48,3072]{1,0:T(8,128)(2,1)S(1)}, bf16[48,3072]{1,0:T(8,128)(2,1)S(1)}, u32[]{:S(2)}, u32[]{:S(2)}) collective-permute-start(bf16[48,3072]{1,0:T(8,128)(2,1)S(1)} %select_bitcast_fusion.7), channel_id=1, source_target_pairs={{0,8},{4,12},{8,0},{12,4},{16,24},{20,28},{24,16},{28,20},{1,9},{5... | collective-permute-start | bytes 884744 | tf_op jit(solution)/shard_map/swap_dp2/ppermute | solution.py:40
  127.0 10.1 %collective-permute-start.50 = (bf16[48,3072]{1,0:T(8,128)(2,1)S(1)}, bf16[48,3072]{1,0:T(8,128)(2,1)S(1)}, u32[]{:S(2)}, u32[]{:S(2)}) collective-permute-start(bf16[48,3072]{1,0:T(8,128)(2,1)S(1)} %fusion.5), channel_id=1, source_target_pairs={{0,2},{1,3},{2,0},{3,1},{4,6},{5,7},{6,4},{7,5},{8,10},{9,11},{10,... | collective-permute-start | bytes 884744 | tf_op jit(solution)/shard_map/swap_fsdp2/ppermute | solution.py:40
  128.4 12.7 %collective-permute-start.54 = (bf16[192,768]{1,0:T(8,128)(2,1)S(1)}, bf16[192,768]{1,0:T(8,128)(2,1)S(1)}, u32[]{:S(2)}, u32[]{:S(2)}) collective-permute-start(bf16[192,768]{1,0:T(8,128)(2,1)S(1)} %add_convert_fusion.12), channel_id=1, source_target_pairs={{0,8},{4,12},{8,0},{12,4},{16,24},{20,28},{24,16},{28,20},{1,9},{5... | collective-permute-start | bytes 884744 | tf_op jit(solution)/shard_map/swap_dp2/ppermute | solution.py:40
  129.2 5.6 %collective-permute-start.46 = (f32[16,768]{1,0:T(8,128)S(1)}, f32[16,768]{1,0:T(8,128)S(1)}, u32[]{:S(2)}, u32[]{:S(2)}) collective-permute-start(f32[16,768]{1,0:T(8,128)S(1)} %add.120), channel_id=1, source_target_pairs={{0,2},{1,3},{2,0},{3,1},{4,6},{5,7},{6,4},{7,5},{8,10},{9,11},{10,... | collective-permute-start | bytes 147464 | tf_op jit(solution)/shard_map/swap_fsdp2/ppermute | solution.py:40
  134.8 11.2 %collective-permute-start.53 = (bf16[192,768]{1,0:T(8,128)(2,1)S(1)}, bf16[192,768]{1,0:T(8,128)(2,1)S(1)}, u32[]{:S(2)}, u32[]{:S(2)}) collective-permute-start(bf16[192,768]{1,0:T(8,128)(2,1)S(1)} %select_bitcast_fusion.6), channel_id=1, source_target_pairs={{0,4},{4,0},{8,12},{12,8},{16,20},{20,16},{24,28},{28,24},{1,5},{5... | collective-permute-start | bytes 884744 | tf_op jit(solution)/shard_map/swap_dp1/ppermute | solution.py:40
  136.2 11.7 %collective-permute-start.48 = (f32[16,768]{1,0:T(8,128)S(1)}, f32[16,768]{1,0:T(8,128)S(1)}, u32[]{:S(2)}, u32[]{:S(2)}) collective-permute-start(f32[16,768]{1,0:T(8,128)S(1)} %add.123), channel_id=1, source_target_pairs={{0,4},{4,0},{8,12},{12,8},{16,20},{20,16},{24,28},{28,24},{1,5},{5... | collective-permute-start | bytes 147464 | tf_op jit(solution)/shard_map/swap_dp1/ppermute | solution.py:40
  137.2 14.9 %collective-permute-start.58 = (bf16[48,3072]{1,0:T(8,128)(2,1)S(1)}, bf16[48,3072]{1,0:T(8,128)(2,1)S(1)}, u32[]{:S(2)}, u32[]{:S(2)}) collective-permute-start(bf16[48,3072]{1,0:T(8,128)(2,1)S(1)} %broadcast_select_fusion.2), channel_id=1, source_target_pairs={{0,4},{4,0},{8,12},{12,8},{16,20},{20,16},{24,28},{28,24},{1,5},{5... | collective-permute-start | bytes 884744 | tf_op jit(solution)/shard_map/swap_dp1/ppermute | solution.py:40
  139.7 6.8 %collective-permute-start.52 = (bf16[192,768]{1,0:T(8,128)(2,1)S(1)}, bf16[192,768]{1,0:T(8,128)(2,1)S(1)}, u32[]{:S(2)}, u32[]{:S(2)}) collective-permute-start(bf16[192,768]{1,0:T(8,128)(2,1)S(1)} %fusion.8), channel_id=1, source_target_pairs={{0,2},{1,3},{2,0},{3,1},{4,6},{5,7},{6,4},{7,5},{8,10},{9,11},{10,... | collective-permute-start | bytes 884744 | tf_op jit(solution)/shard_map/swap_fsdp2/ppermute | solution.py:40
  141.2 13.3 %collective-permute-start.57 = (bf16[192,768]{1,0:T(8,128)(2,1)S(1)}, bf16[192,768]{1,0:T(8,128)(2,1)S(1)}, u32[]{:S(2)}, u32[]{:S(2)}) collective-permute-start(bf16[192,768]{1,0:T(8,128)(2,1)S(1)} %add_convert_fusion.5), channel_id=1, source_target_pairs={{0,16},{4,20},{8,24},{12,28},{16,0},{20,4},{24,8},{28,12},{1,17},{... | collective-permute-start | bytes 884744 | tf_op jit(solution)/shard_map/swap_dp4/ppermute | solution.py:40
  146.7 20.4 %collective-permute-start.56 = (bf16[192,768]{1,0:T(8,128)(2,1)S(1)}, bf16[192,768]{1,0:T(8,128)(2,1)S(1)}, u32[]{:S(2)}, u32[]{:S(2)}) collective-permute-start(bf16[192,768]{1,0:T(8,128)(2,1)S(1)} %broadcast_select_fusion.3), channel_id=1, source_target_pairs={{0,8},{4,12},{8,0},{12,4},{16,24},{20,28},{24,16},{28,20},{1,9},{5... | collective-permute-start | bytes 884744 | tf_op jit(solution)/shard_map/swap_dp2/ppermute | solution.py:40
  154.6 18.0 %collective-permute-start.61 = (bf16[192,768]{1,0:T(8,128)(2,1)S(1)}, bf16[192,768]{1,0:T(8,128)(2,1)S(1)}, u32[]{:S(2)}, u32[]{:S(2)}) collective-permute-start(bf16[192,768]{1,0:T(8,128)(2,1)S(1)} %add_convert_fusion.3), channel_id=1, source_target_pairs={{0,8},{4,12},{8,0},{12,4},{16,24},{20,28},{24,16},{28,20},{1,9},{5... | collective-permute-start | bytes 884744 | tf_op jit(solution)/shard_map/swap_dp2/ppermute | solution.py:40
  154.9 17.6 %collective-permute-start.55 = (f32[16,768]{1,0:T(8,128)S(1)}, f32[16,768]{1,0:T(8,128)S(1)}, u32[]{:S(2)}, u32[]{:S(2)}) collective-permute-start(f32[16,768]{1,0:T(8,128)S(1)} %add.134), channel_id=1, source_target_pairs={{0,8},{4,12},{8,0},{12,4},{16,24},{20,28},{24,16},{28,20},{1,9},{5... | collective-permute-start | bytes 147464 | tf_op jit(solution)/shard_map/swap_dp2/ppermute | solution.py:40
  156.7 24.5 %collective-permute-start.60 = (bf16[48,3072]{1,0:T(8,128)(2,1)S(1)}, bf16[48,3072]{1,0:T(8,128)(2,1)S(1)}, u32[]{:S(2)}, u32[]{:S(2)}) collective-permute-start(bf16[48,3072]{1,0:T(8,128)(2,1)S(1)} %add_convert_fusion.4), channel_id=1, source_target_pairs={{0,16},{4,20},{8,24},{12,28},{16,0},{20,4},{24,8},{28,12},{1,17},{... | collective-permute-start | bytes 884744 | tf_op jit(solution)/shard_map/swap_dp4/ppermute | solution.py:40
  167.3 19.1 %collective-permute-start.62 = (bf16[192,768]{1,0:T(8,128)(2,1)S(1)}, bf16[192,768]{1,0:T(8,128)(2,1)S(1)}, u32[]{:S(2)}, u32[]{:S(2)}) collective-permute-start(bf16[192,768]{1,0:T(8,128)(2,1)S(1)} %add_convert_fusion.2), channel_id=1, source_target_pairs={{0,16},{4,20},{8,24},{12,28},{16,0},{20,4},{24,8},{28,12},{1,17},{... | collective-permute-start | bytes 884744 | tf_op jit(solution)/shard_map/swap_dp4/ppermute | solution.py:40
  172.6 13.8 %collective-permute-start.59 = (f32[16,768]{1,0:T(8,128)S(1)}, f32[16,768]{1,0:T(8,128)S(1)}, u32[]{:S(2)}, u32[]{:S(2)}) collective-permute-start(f32[16,768]{1,0:T(8,128)S(1)} %add.138), channel_id=1, source_target_pairs={{0,16},{4,20},{8,24},{12,28},{16,0},{20,4},{24,8},{28,12},{1,17},{... | collective-permute-start | bytes 147464 | tf_op jit(solution)/shard_map/swap_dp4/ppermute | solution.py:40
  181.3 6.8 %collective-permute-start.64 = (bf16[48,3072]{1,0:T(8,128)(2,1)S(1)}, bf16[48,3072]{1,0:T(8,128)(2,1)S(1)}, u32[]{:S(2)}, u32[]{:S(2)}) collective-permute-start(bf16[48,3072]{1,0:T(8,128)(2,1)S(1)} %add_convert_fusion.1), channel_id=1, source_target_pairs={{0,4},{4,0},{8,12},{12,8},{16,20},{20,16},{24,28},{28,24},{1,5},{5... | collective-permute-start | bytes 884744 | tf_op jit(solution)/shard_map/swap_dp1/ppermute | solution.py:40
  183.5 14.6 %collective-permute-start.67 = (bf16[384,768]{1,0:T(8,128)(2,1)S(1)}, bf16[384,768]{1,0:T(8,128)(2,1)S(1)}, u32[]{:S(2)}, u32[]{:S(2)}) collective-permute-start(bf16[384,768]{1,0:T(8,128)(2,1)S(1)} %maximum_select_fusion.1), channel_id=1, source_target_pairs={{0,4},{4,0},{8,12},{12,8},{16,20},{20,16},{24,28},{28,24},{1,5},{5... | collective-permute-start | bytes 1769480 | tf_op jit(solution)/shard_map/swap_dp1/ppermute | solution.py:40
  186.4 9.9 %collective-permute-start.63 = (bf16[192,768]{1,0:T(8,128)(2,1)S(1)}, bf16[192,768]{1,0:T(8,128)(2,1)S(1)}, u32[]{:S(2)}, u32[]{:S(2)}) collective-permute-start(bf16[192,768]{1,0:T(8,128)(2,1)S(1)} %add_convert_fusion), channel_id=1, source_target_pairs={{0,8},{4,12},{8,0},{12,4},{16,24},{20,28},{24,16},{28,20},{1,9},{5... | collective-permute-start | bytes 884744 | tf_op jit(solution)/shard_map/swap_dp2/ppermute | solution.py:40
  188.2 17.8 %collective-permute-start.66 = (bf16[2,48,3072]{2,1,0:T(8,128)(2,1)S(1)}, bf16[2,48,3072]{2,1,0:T(8,128)(2,1)S(1)}, u32[]{:S(2)}, u32[]{:S(2)}) collective-permute-start(bf16[2,48,3072]{2,1,0:T(8,128)(2,1)S(1)} %pad_maximum_fusion.1), channel_id=1, source_target_pairs={{0,8},{4,12},{8,0},{12,4},{16,24},{20,28},{24,16},{28,20},{1,9},{5... | collective-permute-start | bytes 1769480 | tf_op jit(solution)/shard_map/swap_dp2/ppermute | solution.py:40
  196.5 11.4 %collective-permute-start.65 = (bf16[2,192,768]{2,1,0:T(8,128)(2,1)S(1)}, bf16[2,192,768]{2,1,0:T(8,128)(2,1)S(1)}, u32[]{:S(2)}, u32[]{:S(2)}) collective-permute-start(bf16[2,192,768]{2,1,0:T(8,128)(2,1)S(1)} %pad_maximum_fusion.2), channel_id=1, source_target_pairs={{0,4},{4,0},{8,12},{12,8},{16,20},{20,16},{24,28},{28,24},{1,5},{5... | collective-permute-start | bytes 1769480 | tf_op jit(solution)/shard_map/swap_dp1/ppermute | solution.py:40
  (38 other events, 244.1 us)

commit v3 on v2

--- a/solution.py
+++ b/solution.py
@@ -15,7 +15,12 @@
 
 BQ, BV, BO, G1, S1, BD, G2, S2, TB, BU = 0, 1, 2, 3, 4, 5, 6, 7, 8, 10
 VEC_ROWS = 16
-TURNS = "UUDSASUUADAASUDASDUSAUADUA"
+EARLY_TURNS = ""
+MIDDLE_TURNS = "UU"
+UP_STRIPS_FIRST = False
+TURNS = "DSUASUADAASUDASUDASUUADA"
+UP_BITS = (1, 0)
+DOWN_BITS = (0, 1)
 COST = 1024
 ATTEND_COST = 1024
 VMEM_LIMIT = 16 * 1024 * 1024
@@ -340,7 +345,7 @@
     send_x, keep_x, send_y, keep_y = refs[8:]
     block = rights[0].shape[1]
     part = send_x.shape[1]
-    low_z = where_ref[2] == 0
+    low_first = where_ref[1 + UP_BITS[0]] == 0
     for slot, out in ((1, send_x), (0, keep_x)):
         for j in range(4):
             cols = slice(j * block, (j + 1) * block)
@@ -349,8 +354,8 @@
             out[0, :, cols] = total[:part]
             out[1, :, cols] = total[2 * part : 3 * part]
             first, second = total[part : 2 * part], total[3 * part :]
-            send_y[slot, :, cols] = jnp.where(low_z, second, first)
-            keep_y[slot, :, cols] = jnp.where(low_z, first, second)
+            send_y[slot, :, cols] = jnp.where(low_first, second, first)
+            keep_y[slot, :, cols] = jnp.where(low_first, first, second)
 
 
 def near_attn_kernel(where_ref, own_ref, got_ref, *refs):
@@ -372,9 +377,9 @@
 
 def down_grad_kernel(where_ref, *refs):
     lefts, rights, outs = refs[:4], refs[4:8], refs[8:]
-    y = where_ref[1]
+    mine = where_ref[1 + DOWN_BITS[0]]
     rows = outs[0].shape[0]
-    for half, out in ((1 - y, outs[0]), (y, outs[1])):
+    for half, out in ((1 - mine, outs[0]), (mine, outs[1])):
         cols = pl.ds(pl.multiple_of(half * rows, 128), rows)
         total = None
         for n, (left, right) in enumerate(zip(lefts, rights)):
@@ -497,21 +502,25 @@
     return (a.astype(f32) + b.astype(f32)).astype(bf16)
 
 
-def two_way_chain(send_x, keep_x, send_b, keep_b, dp_index, bits, steps):
+def two_way_chain(send_x, keep_x, send_b, keep_b, dp_index, bits, steps, b_first):
     p, q = [(dp_index >> bit) & 1 for bit in bits]
     one, two = [1 << bit for bit in bits]
     got_x = swap(send_x, "fsdp", 2)
     got_b = swap(send_b, "dp", one)
-    got_x = yield got_x, send_b
-    give = jnp.where(p == 0, add(keep_x[1], got_x[1]), add(keep_x[0], got_x[0]))
-    take = jnp.where(p == 0, add(keep_x[0], got_x[0]), add(keep_x[1], got_x[1]))
-    got_give = swap(give, "dp", one)
-    got_b = yield got_b, give
-    give = add(keep_b[1], got_b[1])
-    rest = add(keep_b[0], got_b[0])
-    got_rest = swap(give, "fsdp", 2)
-    got_give = yield got_give, give
-    first = add(take, got_give)
+    last = send_b
+    for over_x in (False, True) if b_first else (True, False):
+        if over_x:
+            got_x = yield got_x, last
+            last = jnp.where(p == 0, add(keep_x[1], got_x[1]), add(keep_x[0], got_x[0]))
+            take = jnp.where(p == 0, add(keep_x[0], got_x[0]), add(keep_x[1], got_x[1]))
+            got_take = swap(last, "dp", one)
+        else:
+            got_b = yield got_b, last
+            last = add(keep_b[1], got_b[1])
+            rest = add(keep_b[0], got_b[0])
+            got_rest = swap(last, "fsdp", 2)
+    got_take = yield got_take, last
+    first = add(take, got_take)
     got_rest = yield got_rest, first
     second = add(rest, got_rest)
     send = jnp.where(q == 0, second, first)
@@ -565,25 +574,24 @@
     return total
 
 
-def take_turns(chains, turns, token):
-    pending = {name: next(chain)[0] for name, chain in chains.items()}
-    results = {}
-
-    def turn(name, token):
-        try:
-            pending[name], token = chains[name].send(tie(pending[name], token))
-        except StopIteration as stop:
-            results[name] = stop.value
-            del pending[name]
+class Turns:
+    def __init__(self):
+        self.pending, self.done = {}, {}
+
+    def add(self, name, chain):
+        self.pending[name] = next(chain)[0], chain
+
+    def take(self, names, token):
+        for name in names:
+            if name in self.pending:
+                value, chain = self.pending[name]
+                try:
+                    value, token = chain.send(tie(value, token))
+                    self.pending[name] = value, chain
+                except StopIteration as stop:
+                    self.done[name] = stop.value
+                    del self.pending[name]
         return token
-
-    for name in turns:
-        if name in pending:
-            token = turn(name, token)
-    while pending:
-        for name in list(pending):
-            token = turn(name, token)
-    return results
 
 
 def local(
@@ -790,16 +798,22 @@
         glow_across,
         swap(tie(glow_across, gq), "fsdp", 1),
     )
+    turns = Turns()
+    turns.add("U", two_way_chain(*up_parts, d, UP_BITS, order[2:], UP_STRIPS_FIRST))
     rights = [gbr, gv, gq, gk]
     rights_got = [swap(right, "fsdp", 1) for right in rights]
     down_half = pltpu.HBM((shard_hidden // 2, width), bf16)
     send_down, keep_down = call(down_grad_kernel, (down_half,) * 2, 1, 8, 0, [], "down_grad", resident=False)(
         tie(where, gq), *map(in_hbm, act_all), glow, *map(in_hbm, glow_all[1:])
     )
+    turns.add("D", halving_chain(send_down, keep_down, d, DOWN_BITS + order[2:]))
+    token = turns.take(EARLY_TURNS, keep_down)
     pair = pltpu.HBM((2, rows, width), bf16)
     attn_parts = call(near_attn_kernel, (pair,) * 4, 1, 10, 0, [], "near_attn", resident=False)(
-        tie(where, keep_down), in_hbm(own_attn), in_hbm(swap(share_attn, "fsdp", 1)), *rights, *map(in_hbm, rights_got)
-    )
+        tie(where, keep_down, token), in_hbm(own_attn), in_hbm(swap(share_attn, "fsdp", 1)), *rights, *map(in_hbm, rights_got)
+    )
+    turns.add("A", two_way_chain(*attn_parts, d, (0, 1), order[2:], False))
+    token = turns.take(MIDDLE_TURNS, attn_parts[0])
     gin, sm = call(
         partial(input_back_kernel, length=length),
         (flat_low, sds((VEC_ROWS, width), f32)),
@@ -810,7 +824,7 @@
         "input_back",
         resident=False,
     )(
-        tie(where, attn_parts[0]),
+        tie(where, token),
         species,
         gres,
         gq,
@@ -822,20 +836,14 @@
         *attn_first,
         *attn_second,
     )
-    done = take_turns(
-        {
-            "up": two_way_chain(*up_parts, d, (1, 0), order[2:]),
-            "down": halving_chain(send_down, keep_down, d, order),
-            "attn": two_way_chain(*attn_parts, d, (0, 1), order[2:]),
-            "small": whole_chain(sm, order),
-        },
-        [{"U": "up", "D": "down", "A": "attn", "S": "small"}[name] for name in TURNS],
-        attn_parts[0],
-    )
-    grad_up = jnp.stack(done["up"]).reshape(rows, hidden)
-    grad_down = done["down"]
-    low_attn, high_attn = done["attn"]
-    sm = done["small"]
+    turns.add("S", whole_chain(sm, order))
+    token = turns.take(TURNS, token)
+    while turns.pending:
+        token = turns.take(tuple(turns.pending), token)
+    grad_up = jnp.stack(turns.done["U"]).reshape(rows, hidden)
+    grad_down = turns.done["D"]
+    low_attn, high_attn = turns.done["A"]
+    sm = turns.done["S"]
 
     mine = lax.dynamic_slice_in_dim(sm, f * rows, rows, 1)
     b_up_grad = lax.dynamic_slice_in_dim(sm, BU + f, 1, 0)[0]

time: 213 us -> 206 us (0.967); the launches traced: 210 us -> 205 us
  waiting for transfers between devices: 85.2 us -> 78.4 us
  other arithmetic: 8.72 us -> 10.9 us
    ppermute x68, waiting for transfers between devices: 85.2 us -> 78.4 us  [swap(): return lax.ppermute(x, axis, [(i, i ^ distance) for i in range(count)])]
  transfers between devices with their start and end apart: 68 -> 68, of which waited for: 27 -> 27; matrix products, arithmetic and copies ran while one was open for 5% -> 6% of each run, Pallas kernels for 24% -> 25%
where the time goes in v3:
time: 206 us; the launch traced here: 205 us
  waiting for transfers between devices  78.4 us (38%)
  starting transfers between devices  54.6 us (27%)
  Pallas kernels  53.9 us (26%)
  other arithmetic  10.9 us (5%)
  local copies, waits for them, and re-layouts  6.49 us (3%)
    ppermute x68, waiting for transfers between devices, swap(): return lax.ppermute(x, axis, [(i, i ^ distance) for i in range(count)])  78.4 us
    ppermute x68, starting transfers between devices, swap(): return lax.ppermute(x, axis, [(i, i ^ distance) for i in range(count)])  54.6 us
    pallas_call x1, Pallas kernels, local(): call(partial(attend_kernel, length=length), (flat_low, flat_low, flat_low...  10.1 us
    pallas_call x1, Pallas kernels, local(): call(partial(attend_back_kernel, length=length), (flat_low, flat_low, fla...  6.24 us
    pallas_call x1, Pallas kernels, local(): call(up_kernel, (sds((shards, tokens, shard_hidden), bf16), *(pltpu.HBM((...  6.1 us
    pallas_call x1, Pallas kernels, local(): call(norm_back_kernel, (pltpu.HBM(flat.shape, f32), flat_low, flat_low, s...  5.19 us
    pallas_call x1, Pallas kernels, local(): call(partial(input_back_kernel, length=length), (flat_low, sds((VEC_ROWS,...  4.67 us
    pallas_call x1, Pallas kernels, local(): call(down_grad_kernel, (down_half,) * 2, 1, 8, 0, [], 'down_grad', reside...  4.4 us
  transfers between devices with their start and end apart: 68, of which 27 were waited for; matrix products, arithmetic and copies ran while one was open for 6% of the time, Pallas kernels for 25%

profile of v3, /device:TPU:0, one launch (start us, length us, event | category | flops | bytes accessed | tf_op | source)
XLA Modules:
  0.0 205.5 jit_solution(5207018808872669413)
XLA Ops:
  1.3 2.7 %pack.1 = (bf16[400,768]{1,0:T(8,128)(2,1)}, bf16[384,768]{1,0:T(8,128)(2,1)}, bf16[400,384]{1,0:T(8,128)(2,1)}, bf16[384,384]{1,0:T(8,128)(2,1)}) custom-call(s32[3]{0:T(128)} %pad_add_fusion.where_ref, bf16[192,768]{1,0:T(8,128)(2,1)} %q_ref.1, bf16[192,768]{1,0:T(8,128)(2,1)} %k_ref.1, bf16[192,768]{1,0:T(8,128)(2,1)} %v_ref.1, bf16[192,768]{1,0:T(8,128)(2,1)} %o_ref.1, ...), custom_call_target="tpu_custom_call" | custom-call | flops 1024 | bytes 1024 | tf_op jit(solution)/shard_map/pack/pallas_call | solution.py:632
  4.0 3.0 %collective-permute-start.6 = (bf16[384,384]{1,0:T(8,128)(2,1)}, bf16[384,384]{1,0:T(8,128)(2,1)}, u32[]{:S(2)}, u32[]{:S(2)}) collective-permute-start(bf16[384,384]{1,0:T(8,128)(2,1)} %get-tuple-element.117), channel_id=1, source_target_pairs={{0,2},{1,3},{2,0},{3,1},{4,6},{5,7},{6,4},{7,5},{8,10},{9,11},{10,... | collective-permute-start | bytes 884744 | tf_op jit(solution)/shard_map/swap_fsdp2/ppermute | solution.py:45
  7.5 7.6 %collective-permute-done.6.refs_8_.refs_14_ = bf16[384,384]{1,0:T(8,128)(2,1)} collective-permute-done((bf16[384,384]{1,0:T(8,128)(2,1)}, bf16[384,384]{1,0:T(8,128)(2,1)}, u32[]{:S(2)}, u32[]{:S(2)}) %collective-permute-start.6) | collective-permute-done | bytes 294944 | tf_op jit(solution)/shard_map/swap_fsdp2/ppermute | solution.py:45
  15.1 2.1 collective-permute-start.7
  17.2 1.1 fusion.14
  19.2 1.7 collective-permute-done.1.refs_2_
  20.9 1.7 collective-permute-start.11
  22.9 1.5 collective-permute-start.2
  25.3 3.9 %collective-permute-done.11.refs_2_.refs_6_ = bf16[96,1536]{1,0:T(8,128)(2,1)S(1)} collective-permute-done((bf16[96,1536]{1,0:T(8,128)(2,1)S(1)}, bf16[96,1536]{1,0:T(8,128)(2,1)S(1)}, u32[]{:S(2)}, u32[]{:S(2)}) %collective-permute-start.11) | collective-permute-done | bytes 294944 | tf_op jit(solution)/shard_map/swap_fsdp2/ppermute | solution.py:45
  29.2 1.5 collective-permute-start.15
  30.6 2.3 %collective-permute-done.2.refs_3_ = bf16[400,384]{1,0:T(8,128)(2,1)} collective-permute-done((bf16[400,384]{1,0:T(8,128)(2,1)}, bf16[400,384]{1,0:T(8,128)(2,1)}, u32[]{:S(2)}, u32[]{:S(2)}) %collective-permute-start.2) | collective-permute-done | bytes 307232 | tf_op jit(solution)/shard_map/swap_dp1/ppermute | solution.py:45
  33.7 2.5 %collective-permute-done.9.refs_11_.refs_17_ = bf16[384,384]{1,0:T(8,128)(2,1)S(1)} collective-permute-done((bf16[384,384]{1,0:T(8,128)(2,1)}, bf16[384,384]{1,0:T(8,128)(2,1)S(1)}, u32[]{:S(2)}, u32[]{:S(2)}) %collective-permute-start.9) | collective-permute-done | bytes 294944 | tf_op jit(solution)/shard_map/swap_fsdp1/ppermute | solution.py:45
  36.2 1.5 collective-permute-start.18
  37.6 1.6 collective-permute-start.12
  39.2 10.1 %attend.1 = (bf16[256,768]{1,0:T(8,128)(2,1)S(1)}, bf16[256,768]{1,0:T(8,128)(2,1)S(1)}, bf16[256,768]{1,0:T(8,128)(2,1)S(1)}, bf16[4,256,192]{2,1,0:T(8,128)(2,...) custom-call(s32[3]{0:T(128)S(1)} %copy-done.9, ...), custom_call_target="tpu_custom_call" | custom-call | flops 1024 | bytes 1024 | tf_op jit(solution)/shard_map/attend/pallas_call | solution.py:693
  50.7 1.1 collective-permute-done.14.refs_5_.refs_9_
  51.8 1.5 collective-permute-start.19
  53.4 6.1 %up.1 = (bf16[4,256,768]{2,1,0:T(8,128)(2,1)S(1)}, bf16[256,768]{1,0:T(8,128)(2,1)}, bf16[256,768]{1,0:T(8,128)(2,1)}, bf16[2,256,768]{2,1,0:T(8,128)(2,1)}, f32[4,256,768]{2,1,0:T(8,128)S(1)}) custom-call(s32[3]{0:T(128)S(1)} %copy-done.9, bf16[256,768]{1,0:T(8,128)(2,1)S(1)} %get-tuple-element.118.low_ref, f32[16,768]{1,0:T(8,128)S(1)} %get-tuple-element.119.vec_ref, ...), custom_call_target="tpu_custom_call" | custom-call | flops 1024 | bytes 1024 | tf_op jit(solution)/shard_map/up/pallas_call | solution.py:725
  60.3 1.4 collective-permute-start.34
  62.3 6.1 %collective-permute-done.23.refs_7_ = bf16[384,384]{1,0:T(8,128)(2,1)S(1)} collective-permute-done((bf16[384,384]{1,0:T(8,128)(2,1)S(1)}, bf16[384,384]{1,0:T(8,128)(2,1)S(1)}, u32[]{:S(2)}, u32[]{:S(2)}) %collective-permute-start.23) | collective-permute-done | bytes 294944 | tf_op jit(solution)/shard_map/swap_dp2/ppermute | solution.py:45
  68.3 1.6 collective-permute-done.25.refs_9_
  69.9 3.5 %down.1 = (bf16[256,768]{1,0:T(8,128)(2,1)S(1)}, f32[256,768]{1,0:T(8,128)S(1)}, bf16[256,768]{1,0:T(8,128)(2,1)S(1)}, f32[8,768]{1,0:T(8,128)S(1)}) custom-call(s32[3]{0:T(128)S(1)} %copy-done.9, bf16[4,256,768]{2,1,0:T(8,128)(2,1)S(1)} %get-tuple-element.126.act_ref, f32[256,768]{1,0:T(8,128)S(1)} %get-tuple-element.127.n1_ref, ...), custom_call_target="tpu_custom_call" | custom-call | flops 1024 | bytes 1024 | tf_op jit(solution)/shard_map/down/pallas_call | solution.py:742
  73.5 3.0 %hidden_back.1 = (bf16[256,768]{1,0:T(8,128)(2,1)S(1)}, bf16[256,768]{1,0:T(8,128)(2,1)S(1)}, bf16[256,768]{1,0:T(8,128)(2,1)S(1)}, bf16[256,768]{1,0:T(8,128)(2,1)S(1)}, f32[8,768]{1,0:T(8,128)S(1)}) custom-call(s32[3]{0:T(128)S(1)} %copy-done.9, bf16[256,768]{1,0:T(8,128)(2,1)S(1)} %get-tuple-element.162.glow_ref.refs_4_, ...), custom_call_target="tpu_custom_call" | custom-call | flops 1024 | bytes 1024 | tf_op jit(solution)/shard_map/hidden_back/pallas_call | solution.py:753
  77.5 1.1 collective-permute-done.26.got_ref
  79.5 1.2 collective-permute-start.37
  80.7 5.2 %norm_back.1 = (f32[256,768]{1,0:T(8,128)}, bf16[256,768]{1,0:T(8,128)(2,1)S(1)}, bf16[256,768]{1,0:T(8,128)(2,1)S(1)}, f32[8,768]{1,0:T(8,128)S(1)}) custom-call(s32[3]{0:T(128)S(1)} %copy-done.9, f32[256,768]{1,0:T(8,128)S(1)} %get-tuple-element.136.gsec_ref, f32[256,768]{1,0:T(8,128)S(1)} %get-tuple-element.127.n1_ref, ...), custom_call_target="tpu_custom_call" | custom-call | flops 1024 | bytes 1024 | tf_op jit(solution)/shard_map/norm_back/pallas_call | solution.py:763
  87.2 3.7 %near_up.1 = (bf16[2,48,3072]{2,1,0:T(8,128)(2,1)}, bf16[2,48,3072]{2,1,0:T(8,128)(2,1)}, bf16[2,48,3072]{2,1,0:T(8,128)(2,1)}, bf16[2,48,3072]{2,1,0:T(8,128)(2,1)}) custom-call(s32[3]{0:T(128)S(1)} %copy-done.9, bf16[2,256,192]{2,1,0:T(8,128)(2,1)} %get-tuple-element.146.own_ref, bf16[2,256,192]{2,1,0:T(8,128)(2,1)} %copy-done.28, ...), custom_call_target="tpu_custom_call" | custom-call | flops 1024 | bytes 1024 | tf_op jit(solution)/shard_map/near_up/pallas_call | solution.py:777
  90.9 6.2 %attend_back.1 = (bf16[256,768]{1,0:T(8,128)(2,1)S(1)}, bf16[256,768]{1,0:T(8,128)(2,1)S(1)}, bf16[256,768]{1,0:T(8,128)(2,1)S(1)}) custom-call(bf16[256,768]{1,0:T(8,128)(2,1)S(1)} %get-tuple-element.121.q_ref, bf16[256,768]{1,0:T(8,128)(2,1)S(1)} %get-tuple-element.152.k_ref, bf16[256,768]{1,0:T(8,128)(2,1)S(1)} %get-tuple-element.153.v_ref, ...), custom_call_target="tpu_custom_call" | custom-call | flops 1024 | bytes 1024 | tf_op jit(solution)/shard_map/attend_back/pallas_call | solution.py:780
  100.7 4.4 %down_grad.1 = (bf16[384,768]{1,0:T(8,128)(2,1)}, bf16[384,768]{1,0:T(8,128)(2,1)}) custom-call(s32[3]{0:T(128)S(1)} %copy-done.9, bf16[256,768]{1,0:T(8,128)(2,1)} %get-tuple-element.130.refs_0_, bf16[256,768]{1,0:T(8,128)(2,1)} %copy-done.25, bf16[2,256,768]{2,1,0:T(8,128)(2,1)} %copy-done.17, bf16[256,768]{1,0:T(8,128)(2,1)} %copy-done.26, ...), custom_call_target="tpu_custom_call" | custom-call | flops 1024 | bytes 1024 | tf_op jit(solution)/shard_map/down_grad/pallas_call | solution.py:806
  105.1 1.4 collective-permute-start.31
  107.5 4.3 %near_attn.1 = (bf16[2,192,768]{2,1,0:T(8,128)(2,1)}, bf16[2,192,768]{2,1,0:T(8,128)(2,1)}, bf16[2,192,768]{2,1,0:T(8,128)(2,1)}, bf16[2,192,768]{2,1,0:T(8,128)(2,1)}) custom-call(s32[3]{0:T(128)S(1)} %copy-done.9, bf16[4,256,192]{2,1,0:T(8,128)(2,1)} %get-tuple-element.166.own_ref, bf16[4,256,192]{2,1,0:T(8,128)(2,1)} %copy-done.22, ...), custom_call_target="tpu_custom_call" | custom-call | flops 1024 | bytes 1024 | tf_op jit(solution)/shard_map/near_attn/pallas_call | solution.py:812
  113.6 1.3 select_bitcast_fusion.7
  114.8 1.3 collective-permute-start.48
  116.1 5.2 %collective-permute-done.31 = bf16[2,48,3072]{2,1,0:T(8,128)(2,1)S(1)} collective-permute-done((bf16[2,48,3072]{2,1,0:T(8,128)(2,1)S(1)}, bf16[2,48,3072]{2,1,0:T(8,128)(2,1)S(1)}, u32[]{:S(2)}, u32[]{:S(2)}) %collective-permute-start.31) | collective-permute-done | bytes 589856 | tf_op jit(solution)/shard_map/swap_dp2/ppermute | solution.py:45
  121.4 1.3 collective-permute-start.51
  122.7 4.7 %input_back.1 = (bf16[256,768]{1,0:T(8,128)(2,1)}, f32[16,768]{1,0:T(8,128)S(1)}) custom-call(s32[3]{0:T(128)S(1)} %copy-done.9, s32[2]{0:T(128)S(1)} %copy-done.11, f32[256,768]{1,0:T(8,128)S(1)} %copy-done.6, bf16[256,768]{1,0:T(8,128)(2,1)S(1)} %get-tuple-element.156.refs_2_.gq_ref, bf16[256,768]{1,0:T(8,128)(2,1)S(1)} %get-tuple-element.169.refs_3_.gk_ref, ...), custom_call_target="tpu_custom_call" | custom-call | flops 1024 | bytes 1024 | tf_op jit(solution)/shard_map/input_back/pallas_call | solution.py:817
  127.6 1.1 collective-permute-done.44
  129.5 1.4 collective-permute-start.46
  130.9 1.2 fusion.4
  132.4 1.1 collective-permute-start.53
  134.2 1.1 collective-permute-start.49
  135.5 1.1 collective-permute-start.58
  137.9 2.7 %collective-permute-start.57 = (bf16[192,768]{1,0:T(8,128)(2,1)S(1)}, bf16[192,768]{1,0:T(8,128)(2,1)S(1)}, u32[]{:S(2)}, u32[]{:S(2)}) collective-permute-start(bf16[192,768]{1,0:T(8,128)(2,1)S(1)} %add_convert_fusion.5), channel_id=1, source_target_pairs={{0,16},{4,20},{8,24},{12,28},{16,0},{20,4},{24,8},{28,12},{1,17},{... | collective-permute-start | bytes 884744 | tf_op jit(solution)/shard_map/swap_dp4/ppermute | solution.py:45
  140.6 1.7 collective-permute-done.53
  142.5 1.6 collective-permute-done.52
  144.2 1.3 collective-permute-start.56
  146.4 1.9 collective-permute-done.58
  148.5 2.7 %collective-permute-start.62 = (bf16[48,3072]{1,0:T(8,128)(2,1)S(1)}, bf16[48,3072]{1,0:T(8,128)(2,1)S(1)}, u32[]{:S(2)}, u32[]{:S(2)}) collective-permute-start(bf16[48,3072]{1,0:T(8,128)(2,1)S(1)} %add_convert_fusion.4), channel_id=1, source_target_pairs={{0,16},{4,20},{8,24},{12,28},{16,0},{20,4},{24,8},{28,12},{1,17},{... | collective-permute-start | bytes 884744 | tf_op jit(solution)/shard_map/swap_dp4/ppermute | solution.py:45
  151.2 4.2 %collective-permute-done.57 = bf16[192,768]{1,0:T(8,128)(2,1)S(1)} collective-permute-done((bf16[192,768]{1,0:T(8,128)(2,1)S(1)}, bf16[192,768]{1,0:T(8,128)(2,1)S(1)}, u32[]{:S(2)}, u32[]{:S(2)}) %collective-permute-start.57) | collective-permute-done | bytes 294944 | tf_op jit(solution)/shard_map/swap_dp4/ppermute | solution.py:45
  155.5 6.4 %collective-permute-done.56 = bf16[192,768]{1,0:T(8,128)(2,1)S(1)} collective-permute-done((bf16[192,768]{1,0:T(8,128)(2,1)S(1)}, bf16[192,768]{1,0:T(8,128)(2,1)S(1)}, u32[]{:S(2)}, u32[]{:S(2)}) %collective-permute-start.56) | collective-permute-done | bytes 294944 | tf_op jit(solution)/shard_map/swap_dp2/ppermute | solution.py:45
  162.6 2.6 %collective-permute-done.55 = f32[16,768]{1,0:T(8,128)S(1)} collective-permute-done((f32[16,768]{1,0:T(8,128)S(1)}, f32[16,768]{1,0:T(8,128)S(1)}, u32[]{:S(2)}, u32[]{:S(2)}) %collective-permute-start.55) | collective-permute-done | bytes 49184 | tf_op jit(solution)/shard_map/swap_dp2/ppermute | solution.py:45
  165.2 2.2 %collective-permute-start.59 = (f32[16,768]{1,0:T(8,128)S(1)}, f32[16,768]{1,0:T(8,128)S(1)}, u32[]{:S(2)}, u32[]{:S(2)}) collective-permute-start(f32[16,768]{1,0:T(8,128)S(1)} %add.138), channel_id=1, source_target_pairs={{0,16},{4,20},{8,24},{12,28},{16,0},{20,4},{24,8},{28,12},{1,17},{... | collective-permute-start | bytes 147464 | tf_op jit(solution)/shard_map/swap_dp4/ppermute | solution.py:45
  168.1 1.2 collective-permute-start.64
  169.3 2.6 %collective-permute-done.61 = bf16[192,768]{1,0:T(8,128)(2,1)S(1)} collective-permute-done((bf16[192,768]{1,0:T(8,128)(2,1)S(1)}, bf16[192,768]{1,0:T(8,128)(2,1)S(1)}, u32[]{:S(2)}, u32[]{:S(2)}) %collective-permute-start.61) | collective-permute-done | bytes 294944 | tf_op jit(solution)/shard_map/swap_dp2/ppermute | solution.py:45
  172.1 1.3 collective-permute-start.67
  173.4 6.8 %collective-permute-done.60 = bf16[192,768]{1,0:T(8,128)(2,1)S(1)} collective-permute-done((bf16[192,768]{1,0:T(8,128)(2,1)S(1)}, bf16[192,768]{1,0:T(8,128)(2,1)S(1)}, u32[]{:S(2)}, u32[]{:S(2)}) %collective-permute-start.60) | collective-permute-done | bytes 294944 | tf_op jit(solution)/shard_map/swap_dp4/ppermute | solution.py:45
  180.7 1.9 collective-permute-start.66
  184.5 5.7 %collective-permute-done.63 = bf16[192,768]{1,0:T(8,128)(2,1)S(1)} collective-permute-done((bf16[192,768]{1,0:T(8,128)(2,1)S(1)}, bf16[192,768]{1,0:T(8,128)(2,1)S(1)}, u32[]{:S(2)}, u32[]{:S(2)}) %collective-permute-start.63) | collective-permute-done | bytes 294944 | tf_op jit(solution)/shard_map/swap_dp2/ppermute | solution.py:45
  190.3 1.2 collective-permute-start.65
  191.5 1.6 fusion
  193.1 8.1 %collective-permute-done.66 = bf16[2,48,3072]{2,1,0:T(8,128)(2,1)S(1)} collective-permute-done((bf16[2,48,3072]{2,1,0:T(8,128)(2,1)S(1)}, bf16[2,48,3072]{2,1,0:T(8,128)(2,1)S(1)}, u32[]{:S(2)}, u32[]{:S(2)}) %collective-permute-start.66) | collective-permute-done | bytes 589856 | tf_op jit(solution)/shard_map/swap_dp2/ppermute | solution.py:45
  201.5 1.7 bitcast_convert_fusion
  203.3 1.1 fusion.9
  204.4 1.1 fusion.10
  (191 shorter events, 25.5 us)
Async XLA Ops:
  4.0 11.1 %collective-permute-start.6 = (bf16[384,384]{1,0:T(8,128)(2,1)}, bf16[384,384]{1,0:T(8,128)(2,1)}, u32[]{:S(2)}, u32[]{:S(2)}) collective-permute-start(bf16[384,384]{1,0:T(8,128)(2,1)} %get-tuple-element.117), channel_id=1, source_target_pairs={{0,2},{1,3},{2,0},{3,1},{4,6},{5,7},{6,4},{7,5},{8,10},{9,11},{10,... | collective-permute-start | bytes 884744 | tf_op jit(solution)/shard_map/swap_fsdp2/ppermute | solution.py:45
  6.9 14.0 %collective-permute-start.1 = (bf16[400,384]{1,0:T(8,128)(2,1)}, bf16[400,384]{1,0:T(8,128)(2,1)}, u32[]{:S(2)}, u32[]{:S(2)}) collective-permute-start(bf16[400,384]{1,0:T(8,128)(2,1)} %get-tuple-element.114), channel_id=1, source_target_pairs={{0,2},{1,3},{2,0},{3,1},{4,6},{5,7},{6,4},{7,5},{8,10},{9,11},{10,... | collective-permute-start | bytes 921608 | tf_op jit(solution)/shard_map/swap_fsdp2/ppermute | solution.py:45
  7.0 17.4 %collective-permute-start.5 = (bf16[384,768]{1,0:T(8,128)(2,1)}, bf16[384,768]{1,0:T(8,128)(2,1)S(1)}, u32[]{:S(2)}, u32[]{:S(2)}) collective-permute-start(bf16[384,768]{1,0:T(8,128)(2,1)} %get-tuple-element.115.refs_6_.refs_12_), channel_id=1, source_target_pairs={{0,1},{1,0},{2,3},{3,2},{4,5},{5,4},{6,7},{7,6},{8,9},{9,8},{10,11... | collective-permute-start | bytes 1769480 | tf_op jit(solution)/shard_map/swap_fsdp1/ppermute | solution.py:45
  7.0 26.4 %collective-permute-start = (bf16[400,768]{1,0:T(8,128)(2,1)}, bf16[400,768]{1,0:T(8,128)(2,1)}, u32[]{:S(2)}, u32[]{:S(2)}) collective-permute-start(bf16[400,768]{1,0:T(8,128)(2,1)} %get-tuple-element.113.refs_0_), channel_id=1, source_target_pairs={{0,1},{1,0},{2,3},{3,2},{4,5},{5,4},{6,7},{7,6},{8,9},{9,8},{10,11... | collective-permute-start | bytes 1843208 | tf_op jit(solution)/shard_map/swap_fsdp1/ppermute | solution.py:45
  15.1 7.8 %collective-permute-start.7 = (bf16[384,384]{1,0:T(8,128)(2,1)}, bf16[384,384]{1,0:T(8,128)(2,1)}, u32[]{:S(2)}, u32[]{:S(2)}) collective-permute-start(bf16[384,384]{1,0:T(8,128)(2,1)} %collective-permute-done.6.refs_8_.refs_14_), channel_id=1, source_target_pairs={{0,4},{4,0},{8,12},{12,8},{16,20},{20,16},{24,28},{28,24},{1,5},{5... | collective-permute-start | bytes 884744 | tf_op jit(solution)/shard_map/swap_dp1/ppermute | solution.py:45
  18.3 4.6 %collective-permute-start.8 = (bf16[384,384]{1,0:T(8,128)(2,1)}, bf16[384,384]{1,0:T(8,128)(2,1)S(1)}, u32[]{:S(2)}, u32[]{:S(2)}) collective-permute-start(bf16[384,384]{1,0:T(8,128)(2,1)} %collective-permute-done.6.refs_8_.refs_14_), channel_id=1, source_target_pairs={{0,1},{1,0},{2,3},{3,2},{4,5},{5,4},{6,7},{7,6},{8,9},{9,8},{10,11... | collective-permute-start | bytes 884744 | tf_op jit(solution)/shard_map/swap_fsdp1/ppermute | solution.py:45
  20.9 8.2 %collective-permute-start.11 = (bf16[96,1536]{1,0:T(8,128)(2,1)S(1)}, bf16[96,1536]{1,0:T(8,128)(2,1)S(1)}, u32[]{:S(2)}, u32[]{:S(2)}) collective-permute-start(bf16[96,1536]{1,0:T(8,128)(2,1)S(1)} %constant_dynamic-slice_fusion.3), channel_id=1, source_target_pairs={{0,2},{1,3},{2,0},{3,1},{4,6},{5,7},{6,4},{7,5},{8,10},{9,11},{10,... | collective-permute-start | bytes 884744 | tf_op jit(solution)/shard_map/swap_fsdp2/ppermute | solution.py:45
  22.9 27.1 %collective-permute-start.10 = (bf16[192,3072]{1,0:T(8,128)(2,1)S(1)}, bf16[192,3072]{1,0:T(8,128)(2,1)}, u32[]{:S(2)}, u32[]{:S(2)}) collective-permute-start(bf16[192,3072]{1,0:T(8,128)(2,1)S(1)} %copy-done), channel_id=1, source_target_pairs={{0,1},{1,0},{2,3},{3,2},{4,5},{5,4},{6,7},{7,6},{8,9},{9,8},{10,11... | collective-permute-start | bytes 3538952 | tf_op jit(solution)/shard_map/swap_fsdp1/ppermute | solution.py:45
  22.9 10.0 %collective-permute-start.2 = (bf16[400,384]{1,0:T(8,128)(2,1)}, bf16[400,384]{1,0:T(8,128)(2,1)}, u32[]{:S(2)}, u32[]{:S(2)}) collective-permute-start(bf16[400,384]{1,0:T(8,128)(2,1)} %collective-permute-done.1.refs_2_), channel_id=1, source_target_pairs={{0,4},{4,0},{8,12},{12,8},{16,20},{20,16},{24,28},{28,24},{1,5},{5... | collective-permute-start | bytes 921608 | tf_op jit(solution)/shard_map/swap_dp1/ppermute | solution.py:45
  24.4 8.5 %collective-permute-start.3 = (bf16[400,384]{1,0:T(8,128)(2,1)}, bf16[400,384]{1,0:T(8,128)(2,1)}, u32[]{:S(2)}, u32[]{:S(2)}) collective-permute-start(bf16[400,384]{1,0:T(8,128)(2,1)} %collective-permute-done.1.refs_2_), channel_id=1, source_target_pairs={{0,1},{1,0},{2,3},{3,2},{4,5},{5,4},{6,7},{7,6},{8,9},{9,8},{10,11... | collective-permute-start | bytes 921608 | tf_op jit(solution)/shard_map/swap_fsdp1/ppermute | solution.py:45
  29.2 20.2 %collective-permute-start.15 = (bf16[96,3072]{1,0:T(8,128)(2,1)}, bf16[96,3072]{1,0:T(8,128)(2,1)S(1)}, u32[]{:S(2)}, u32[]{:S(2)}) collective-permute-start(bf16[96,3072]{1,0:T(8,128)(2,1)} %get-tuple-element.124), channel_id=1, source_target_pairs={{0,2},{1,3},{2,0},{3,1},{4,6},{5,7},{6,4},{7,5},{8,10},{9,11},{10,... | collective-permute-start | bytes 1769480 | tf_op jit(solution)/shard_map/swap_fsdp2/ppermute | solution.py:45
  32.9 29.3 %collective-permute-start.17 = (bf16[768,768]{1,0:T(8,128)(2,1)S(1)}, bf16[768,768]{1,0:T(8,128)(2,1)S(1)}, u32[]{:S(2)}, u32[]{:S(2)}) collective-permute-start(bf16[768,768]{1,0:T(8,128)(2,1)S(1)} %copy-done.1), channel_id=1, source_target_pairs={{0,1},{1,0},{2,3},{3,2},{4,5},{5,4},{6,7},{7,6},{8,9},{9,8},{10,11... | collective-permute-start | bytes 3538952 | tf_op jit(solution)/shard_map/swap_fsdp1/ppermute | solution.py:45
  32.9 3.3 %collective-permute-start.9 = (bf16[384,384]{1,0:T(8,128)(2,1)}, bf16[384,384]{1,0:T(8,128)(2,1)S(1)}, u32[]{:S(2)}, u32[]{:S(2)}) collective-permute-start(bf16[384,384]{1,0:T(8,128)(2,1)} %collective-permute-done.7.refs_9_.refs_15_), channel_id=1, source_target_pairs={{0,1},{1,0},{2,3},{3,2},{4,5},{5,4},{6,7},{7,6},{8,9},{9,8},{10,11... | collective-permute-start | bytes 884744 | tf_op jit(solution)/shard_map/swap_fsdp1/ppermute | solution.py:45
  33.4 4.2 %collective-permute-start.4 = (bf16[400,384]{1,0:T(8,128)(2,1)}, bf16[400,384]{1,0:T(8,128)(2,1)S(1)}, u32[]{:S(2)}, u32[]{:S(2)}) collective-permute-start(bf16[400,384]{1,0:T(8,128)(2,1)} %collective-permute-done.2.refs_3_), channel_id=1, source_target_pairs={{0,1},{1,0},{2,3},{3,2},{4,5},{5,4},{6,7},{7,6},{8,9},{9,8},{10,11... | collective-permute-start | bytes 921608 | tf_op jit(solution)/shard_map/swap_fsdp1/ppermute | solution.py:45
  36.2 13.8 %collective-permute-start.18 = (bf16[384,384]{1,0:T(8,128)(2,1)S(1)}, bf16[384,384]{1,0:T(8,128)(2,1)S(1)}, u32[]{:S(2)}, u32[]{:S(2)}) collective-permute-start(bf16[384,384]{1,0:T(8,128)(2,1)S(1)} %get-tuple-element.128), channel_id=1, source_target_pairs={{0,2},{1,3},{2,0},{3,1},{4,6},{5,7},{6,4},{7,5},{8,10},{9,11},{10,... | collective-permute-start | bytes 884744 | tf_op jit(solution)/shard_map/swap_fsdp2/ppermute | solution.py:45
  37.6 11.8 %collective-permute-start.12 = (bf16[96,1536]{1,0:T(8,128)(2,1)S(1)}, bf16[96,1536]{1,0:T(8,128)(2,1)S(1)}, u32[]{:S(2)}, u32[]{:S(2)}) collective-permute-start(bf16[96,1536]{1,0:T(8,128)(2,1)S(1)} %collective-permute-done.11.refs_2_.refs_6_), channel_id=1, source_target_pairs={{0,8},{4,12},{8,0},{12,4},{16,24},{20,28},{24,16},{28,20},{1,9},{5... | collective-permute-start | bytes 884744 | tf_op jit(solution)/shard_map/swap_dp2/ppermute | solution.py:45
  49.3 4.0 %collective-permute-start.16 = (bf16[96,3072]{1,0:T(8,128)(2,1)S(1)}, bf16[96,3072]{1,0:T(8,128)(2,1)S(1)}, u32[]{:S(2)}, u32[]{:S(2)}) collective-permute-start(bf16[96,3072]{1,0:T(8,128)(2,1)S(1)} %collective-permute-done.15.refs_6_.refs_10_), channel_id=1, source_target_pairs={{0,1},{1,0},{2,3},{3,2},{4,5},{5,4},{6,7},{7,6},{8,9},{9,8},{10,11... | collective-permute-start | bytes 1769480 | tf_op jit(solution)/shard_map/swap_fsdp1/ppermute | solution.py:45
  49.4 2.4 %collective-permute-start.14 = (bf16[96,1536]{1,0:T(8,128)(2,1)S(1)}, bf16[96,1536]{1,0:T(8,128)(2,1)S(1)}, u32[]{:S(2)}, u32[]{:S(2)}) collective-permute-start(bf16[96,1536]{1,0:T(8,128)(2,1)S(1)} %collective-permute-done.12.refs_3_.refs_7_), channel_id=1, source_target_pairs={{0,1},{1,0},{2,3},{3,2},{4,5},{5,4},{6,7},{7,6},{8,9},{9,8},{10,11... | collective-permute-start | bytes 884744 | tf_op jit(solution)/shard_map/swap_fsdp1/ppermute | solution.py:45
  49.9 3.4 %collective-permute-start.13 = (bf16[96,1536]{1,0:T(8,128)(2,1)S(1)}, bf16[96,1536]{1,0:T(8,128)(2,1)S(1)}, u32[]{:S(2)}, u32[]{:S(2)}) collective-permute-start(bf16[96,1536]{1,0:T(8,128)(2,1)S(1)} %collective-permute-done.11.refs_2_.refs_6_), channel_id=1, source_target_pairs={{0,1},{1,0},{2,3},{3,2},{4,5},{5,4},{6,7},{7,6},{8,9},{9,8},{10,11... | collective-permute-start | bytes 884744 | tf_op jit(solution)/shard_map/swap_fsdp1/ppermute | solution.py:45
  50.0 9.5 %collective-permute-start.22 = (bf16[384,384]{1,0:T(8,128)(2,1)S(1)}, bf16[384,384]{1,0:T(8,128)(2,1)S(1)}, u32[]{:S(2)}, u32[]{:S(2)}) collective-permute-start(bf16[384,384]{1,0:T(8,128)(2,1)S(1)} %get-tuple-element.133), channel_id=1, source_target_pairs={{0,2},{1,3},{2,0},{3,1},{4,6},{5,7},{6,4},{7,5},{8,10},{9,11},{10,... | collective-permute-start | bytes 884744 | tf_op jit(solution)/shard_map/swap_fsdp2/ppermute | solution.py:45
  51.8 9.9 %collective-permute-start.19 = (bf16[384,384]{1,0:T(8,128)(2,1)S(1)}, bf16[384,384]{1,0:T(8,128)(2,1)S(1)}, u32[]{:S(2)}, u32[]{:S(2)}) collective-permute-start(bf16[384,384]{1,0:T(8,128)(2,1)S(1)} %collective-permute-done.18.refs_2_), channel_id=1, source_target_pairs={{0,4},{4,0},{8,12},{12,8},{16,20},{20,16},{24,28},{28,24},{1,5},{5... | collective-permute-start | bytes 884744 | tf_op jit(solution)/shard_map/swap_dp1/ppermute | solution.py:45
  59.5 8.8 %collective-permute-start.23 = (bf16[384,384]{1,0:T(8,128)(2,1)S(1)}, bf16[384,384]{1,0:T(8,128)(2,1)S(1)}, u32[]{:S(2)}, u32[]{:S(2)}) collective-permute-start(bf16[384,384]{1,0:T(8,128)(2,1)S(1)} %collective-permute-done.22.refs_6_), channel_id=1, source_target_pairs={{0,8},{4,12},{8,0},{12,4},{16,24},{20,28},{24,16},{28,20},{1,9},{5... | collective-permute-start | bytes 884744 | tf_op jit(solution)/shard_map/swap_dp2/ppermute | solution.py:45
  60.3 19.2 %collective-permute-start.34 = (bf16[2,256,768]{2,1,0:T(8,128)(2,1)}, bf16[2,256,768]{2,1,0:T(8,128)(2,1)S(1)}, u32[]{:S(2)}, u32[]{:S(2)}) collective-permute-start(bf16[2,256,768]{2,1,0:T(8,128)(2,1)} %get-tuple-element.160), channel_id=1, source_target_pairs={{0,2},{1,3},{2,0},{3,1},{4,6},{5,7},{6,4},{7,5},{8,10},{9,11},{10,... | collective-permute-start | bytes 2359304 | tf_op jit(solution)/shard_map/swap_fsdp2/ppermute | solution.py:45
  61.7 6.6 %collective-permute-start.24 = (bf16[384,384]{1,0:T(8,128)(2,1)S(1)}, bf16[384,384]{1,0:T(8,128)(2,1)S(1)}, u32[]{:S(2)}, u32[]{:S(2)}) collective-permute-start(bf16[384,384]{1,0:T(8,128)(2,1)S(1)} %collective-permute-done.22.refs_6_), channel_id=1, source_target_pairs={{0,1},{1,0},{2,3},{3,2},{4,5},{5,4},{6,7},{7,6},{8,9},{9,8},{10,11... | collective-permute-start | bytes 884744 | tf_op jit(solution)/shard_map/swap_fsdp1/ppermute | solution.py:45
  61.7 6.6 %collective-permute-start.21 = (bf16[384,384]{1,0:T(8,128)(2,1)S(1)}, bf16[384,384]{1,0:T(8,128)(2,1)S(1)}, u32[]{:S(2)}, u32[]{:S(2)}) collective-permute-start(bf16[384,384]{1,0:T(8,128)(2,1)S(1)} %collective-permute-done.19.refs_3_), channel_id=1, source_target_pairs={{0,1},{1,0},{2,3},{3,2},{4,5},{5,4},{6,7},{7,6},{8,9},{9,8},{10,11... | collective-permute-start | bytes 884744 | tf_op jit(solution)/shard_map/swap_fsdp1/ppermute | solution.py:45
  62.2 6.1 %collective-permute-start.20 = (bf16[384,384]{1,0:T(8,128)(2,1)S(1)}, bf16[384,384]{1,0:T(8,128)(2,1)S(1)}, u32[]{:S(2)}, u32[]{:S(2)}) collective-permute-start(bf16[384,384]{1,0:T(8,128)(2,1)S(1)} %collective-permute-done.18.refs_2_), channel_id=1, source_target_pairs={{0,1},{1,0},{2,3},{3,2},{4,5},{5,4},{6,7},{7,6},{8,9},{9,8},{10,11... | collective-permute-start | bytes 884744 | tf_op jit(solution)/shard_map/swap_fsdp1/ppermute | solution.py:45
  76.5 9.5 %collective-permute-start.27 = (bf16[256,768]{1,0:T(8,128)(2,1)S(1)}, bf16[256,768]{1,0:T(8,128)(2,1)S(1)}, u32[]{:S(2)}, u32[]{:S(2)}) collective-permute-start(bf16[256,768]{1,0:T(8,128)(2,1)S(1)} %get-tuple-element.140.refs_0_), channel_id=1, source_target_pairs={{0,1},{1,0},{2,3},{3,2},{4,5},{5,4},{6,7},{7,6},{8,9},{9,8},{10,11... | collective-permute-start | bytes 1179656 | tf_op jit(solution)/shard_map/swap_fsdp1/ppermute | solution.py:45
  77.0 9.0 %collective-permute-start.28 = (bf16[256,768]{1,0:T(8,128)(2,1)S(1)}, bf16[256,768]{1,0:T(8,128)(2,1)S(1)}, u32[]{:S(2)}, u32[]{:S(2)}) collective-permute-start(bf16[256,768]{1,0:T(8,128)(2,1)S(1)} %get-tuple-element.141.refs_1_), channel_id=1, source_target_pairs={{0,1},{1,0},{2,3},{3,2},{4,5},{5,4},{6,7},{7,6},{8,9},{9,8},{10,11... | collective-permute-start | bytes 1179656 | tf_op jit(solution)/shard_map/swap_fsdp1/ppermute | solution.py:45
  77.2 9.5 %collective-permute-start.29 = (bf16[256,768]{1,0:T(8,128)(2,1)S(1)}, bf16[256,768]{1,0:T(8,128)(2,1)S(1)}, u32[]{:S(2)}, u32[]{:S(2)}) collective-permute-start(bf16[256,768]{1,0:T(8,128)(2,1)S(1)} %get-tuple-element.142.refs_2_), channel_id=1, source_target_pairs={{0,1},{1,0},{2,3},{3,2},{4,5},{5,4},{6,7},{7,6},{8,9},{9,8},{10,11... | collective-permute-start | bytes 1179656 | tf_op jit(solution)/shard_map/swap_fsdp1/ppermute | solution.py:45
  78.6 8.1 %collective-permute-start.30 = (bf16[256,768]{1,0:T(8,128)(2,1)S(1)}, bf16[256,768]{1,0:T(8,128)(2,1)S(1)}, u32[]{:S(2)}, u32[]{:S(2)}) collective-permute-start(bf16[256,768]{1,0:T(8,128)(2,1)S(1)} %get-tuple-element.143.refs_3_), channel_id=1, source_target_pairs={{0,1},{1,0},{2,3},{3,2},{4,5},{5,4},{6,7},{7,6},{8,9},{9,8},{10,11... | collective-permute-start | bytes 1179656 | tf_op jit(solution)/shard_map/swap_fsdp1/ppermute | solution.py:45
  79.5 17.6 %collective-permute-start.37 = (bf16[256,768]{1,0:T(8,128)(2,1)S(1)}, bf16[256,768]{1,0:T(8,128)(2,1)S(1)}, u32[]{:S(2)}, u32[]{:S(2)}) collective-permute-start(bf16[256,768]{1,0:T(8,128)(2,1)S(1)} %get-tuple-element.162.glow_ref.refs_4_), channel_id=1, source_target_pairs={{0,2},{1,3},{2,0},{3,1},{4,6},{5,7},{6,4},{7,5},{8,10},{9,11},{10,... | collective-permute-start | bytes 1179656 | tf_op jit(solution)/shard_map/swap_fsdp2/ppermute | solution.py:45
  85.9 11.3 %collective-permute-start.39 = (bf16[4,256,192]{2,1,0:T(8,128)(2,1)S(1)}, bf16[4,256,192]{2,1,0:T(8,128)(2,1)S(1)}, u32[]{:S(2)}, u32[]{:S(2)}) collective-permute-start(bf16[4,256,192]{2,1,0:T(8,128)(2,1)S(1)} %copy-done.30), channel_id=1, source_target_pairs={{0,1},{1,0},{2,3},{3,2},{4,5},{5,4},{6,7},{7,6},{8,9},{9,8},{10,11... | collective-permute-start | bytes 1179656 | tf_op jit(solution)/shard_map/swap_fsdp1/ppermute | solution.py:45
  86.1 12.0 %collective-permute-start.36 = (bf16[256,768]{1,0:T(8,128)(2,1)S(1)}, bf16[256,768]{1,0:T(8,128)(2,1)S(1)}, u32[]{:S(2)}, u32[]{:S(2)}) collective-permute-start(bf16[256,768]{1,0:T(8,128)(2,1)S(1)} %get-tuple-element.162.glow_ref.refs_4_), channel_id=1, source_target_pairs={{0,1},{1,0},{2,3},{3,2},{4,5},{5,4},{6,7},{7,6},{8,9},{9,8},{10,11... | collective-permute-start | bytes 1179656 | tf_op jit(solution)/shard_map/swap_fsdp1/ppermute | solution.py:45
  86.7 11.6 %collective-permute-start.33 = (bf16[256,768]{1,0:T(8,128)(2,1)S(1)}, bf16[256,768]{1,0:T(8,128)(2,1)S(1)}, u32[]{:S(2)}, u32[]{:S(2)}) collective-permute-start(bf16[256,768]{1,0:T(8,128)(2,1)S(1)} %copy-done.31), channel_id=1, source_target_pairs={{0,1},{1,0},{2,3},{3,2},{4,5},{5,4},{6,7},{7,6},{8,9},{9,8},{10,11... | collective-permute-start | bytes 1179656 | tf_op jit(solution)/shard_map/swap_fsdp1/ppermute | solution.py:45
  86.7 11.9 %collective-permute-start.35 = (bf16[256,768]{1,0:T(8,128)(2,1)S(1)}, bf16[256,768]{1,0:T(8,128)(2,1)S(1)}, u32[]{:S(2)}, u32[]{:S(2)}) collective-permute-start(bf16[256,768]{1,0:T(8,128)(2,1)S(1)} %slice_bitcast_fusion), channel_id=1, source_target_pairs={{0,1},{1,0},{2,3},{3,2},{4,5},{5,4},{6,7},{7,6},{8,9},{9,8},{10,11... | collective-permute-start | bytes 1179656 | tf_op jit(solution)/shard_map/swap_fsdp1/ppermute | solution.py:45
  97.3 16.3 %collective-permute-start.32 = (bf16[2,48,3072]{2,1,0:T(8,128)(2,1)}, bf16[2,48,3072]{2,1,0:T(8,128)(2,1)}, u32[]{:S(2)}, u32[]{:S(2)}) collective-permute-start(bf16[2,48,3072]{2,1,0:T(8,128)(2,1)} %get-tuple-element.151), channel_id=1, source_target_pairs={{0,2},{1,3},{2,0},{3,1},{4,6},{5,7},{6,4},{7,5},{8,10},{9,11},{10,... | collective-permute-start | bytes 1769480 | tf_op jit(solution)/shard_map/swap_fsdp2/ppermute | solution.py:45
  98.1 7.0 %collective-permute-start.40 = (bf16[256,768]{1,0:T(8,128)(2,1)S(1)}, bf16[256,768]{1,0:T(8,128)(2,1)}, u32[]{:S(2)}, u32[]{:S(2)}) collective-permute-start(bf16[256,768]{1,0:T(8,128)(2,1)S(1)} %get-tuple-element.144.refs_0_), channel_id=1, source_target_pairs={{0,1},{1,0},{2,3},{3,2},{4,5},{5,4},{6,7},{7,6},{8,9},{9,8},{10,11... | collective-permute-start | bytes 1179656 | tf_op jit(solution)/shard_map/swap_fsdp1/ppermute | solution.py:45
  98.2 8.2 %collective-permute-start.41 = (bf16[256,768]{1,0:T(8,128)(2,1)S(1)}, bf16[256,768]{1,0:T(8,128)(2,1)}, u32[]{:S(2)}, u32[]{:S(2)}) collective-permute-start(bf16[256,768]{1,0:T(8,128)(2,1)S(1)} %get-tuple-element.168.refs_1_.gv_ref), channel_id=1, source_target_pairs={{0,1},{1,0},{2,3},{3,2},{4,5},{5,4},{6,7},{7,6},{8,9},{9,8},{10,11... | collective-permute-start | bytes 1179656 | tf_op jit(solution)/shard_map/swap_fsdp1/ppermute | solution.py:45
  98.6 8.9 %collective-permute-start.42 = (bf16[256,768]{1,0:T(8,128)(2,1)S(1)}, bf16[256,768]{1,0:T(8,128)(2,1)}, u32[]{:S(2)}, u32[]{:S(2)}) collective-permute-start(bf16[256,768]{1,0:T(8,128)(2,1)S(1)} %get-tuple-element.156.refs_2_.gq_ref), channel_id=1, source_target_pairs={{0,1},{1,0},{2,3},{3,2},{4,5},{5,4},{6,7},{7,6},{8,9},{9,8},{10,11... | collective-permute-start | bytes 1179656 | tf_op jit(solution)/shard_map/swap_fsdp1/ppermute | solution.py:45
  99.7 7.8 %collective-permute-start.43 = (bf16[256,768]{1,0:T(8,128)(2,1)S(1)}, bf16[256,768]{1,0:T(8,128)(2,1)}, u32[]{:S(2)}, u32[]{:S(2)}) collective-permute-start(bf16[256,768]{1,0:T(8,128)(2,1)S(1)} %get-tuple-element.169.refs_3_.gk_ref), channel_id=1, source_target_pairs={{0,1},{1,0},{2,3},{3,2},{4,5},{5,4},{6,7},{7,6},{8,9},{9,8},{10,11... | collective-permute-start | bytes 1179656 | tf_op jit(solution)/shard_map/swap_fsdp1/ppermute | solution.py:45
  105.1 16.3 %collective-permute-start.31 = (bf16[2,48,3072]{2,1,0:T(8,128)(2,1)S(1)}, bf16[2,48,3072]{2,1,0:T(8,128)(2,1)S(1)}, u32[]{:S(2)}, u32[]{:S(2)}) collective-permute-start(bf16[2,48,3072]{2,1,0:T(8,128)(2,1)S(1)} %copy-done.29), channel_id=1, source_target_pairs={{0,8},{4,12},{8,0},{12,4},{16,24},{20,28},{24,16},{28,20},{1,9},{5... | collective-permute-start | bytes 1769480 | tf_op jit(solution)/shard_map/swap_dp2/ppermute | solution.py:45
  106.5 20.9 %collective-permute-start.45 = (bf16[384,768]{1,0:T(8,128)(2,1)}, bf16[384,768]{1,0:T(8,128)(2,1)S(1)}, u32[]{:S(2)}, u32[]{:S(2)}) collective-permute-start(bf16[384,768]{1,0:T(8,128)(2,1)} %get-tuple-element.180), channel_id=1, source_target_pairs={{0,4},{4,0},{8,12},{12,8},{16,20},{20,16},{24,28},{28,24},{1,5},{5... | collective-permute-start | bytes 1769480 | tf_op jit(solution)/shard_map/swap_dp1/ppermute | solution.py:45
  111.8 20.3 %collective-permute-start.47 = (bf16[2,192,768]{2,1,0:T(8,128)(2,1)}, bf16[2,192,768]{2,1,0:T(8,128)(2,1)S(1)}, u32[]{:S(2)}, u32[]{:S(2)}) collective-permute-start(bf16[2,192,768]{2,1,0:T(8,128)(2,1)} %get-tuple-element.170), channel_id=1, source_target_pairs={{0,2},{1,3},{2,0},{3,1},{4,6},{5,7},{6,4},{7,5},{8,10},{9,11},{10,... | collective-permute-start | bytes 1769480 | tf_op jit(solution)/shard_map/swap_fsdp2/ppermute | solution.py:45
  112.7 23.9 %collective-permute-start.50 = (bf16[2,192,768]{2,1,0:T(8,128)(2,1)}, bf16[2,192,768]{2,1,0:T(8,128)(2,1)S(1)}, u32[]{:S(2)}, u32[]{:S(2)}) collective-permute-start(bf16[2,192,768]{2,1,0:T(8,128)(2,1)} %get-tuple-element.188), channel_id=1, source_target_pairs={{0,4},{4,0},{8,12},{12,8},{16,20},{20,16},{24,28},{28,24},{1,5},{5... | collective-permute-start | bytes 1769480 | tf_op jit(solution)/shard_map/swap_dp1/ppermute | solution.py:45
  114.8 14.7 %collective-permute-start.48 = (bf16[48,3072]{1,0:T(8,128)(2,1)S(1)}, bf16[48,3072]{1,0:T(8,128)(2,1)S(1)}, u32[]{:S(2)}, u32[]{:S(2)}) collective-permute-start(bf16[48,3072]{1,0:T(8,128)(2,1)S(1)} %select_bitcast_fusion.7), channel_id=1, source_target_pairs={{0,8},{4,12},{8,0},{12,4},{16,24},{20,28},{24,16},{28,20},{1,9},{5... | collective-permute-start | bytes 884744 | tf_op jit(solution)/shard_map/swap_dp2/ppermute | solution.py:45
  121.4 13.9 %collective-permute-start.51 = (bf16[48,3072]{1,0:T(8,128)(2,1)S(1)}, bf16[48,3072]{1,0:T(8,128)(2,1)S(1)}, u32[]{:S(2)}, u32[]{:S(2)}) collective-permute-start(bf16[48,3072]{1,0:T(8,128)(2,1)S(1)} %fusion.5), channel_id=1, source_target_pairs={{0,2},{1,3},{2,0},{3,1},{4,6},{5,7},{6,4},{7,5},{8,10},{9,11},{10,... | collective-permute-start | bytes 884744 | tf_op jit(solution)/shard_map/swap_fsdp2/ppermute | solution.py:45
  128.7 9.1 %collective-permute-start.54 = (bf16[192,768]{1,0:T(8,128)(2,1)S(1)}, bf16[192,768]{1,0:T(8,128)(2,1)S(1)}, u32[]{:S(2)}, u32[]{:S(2)}) collective-permute-start(bf16[192,768]{1,0:T(8,128)(2,1)S(1)} %add_convert_fusion.12), channel_id=1, source_target_pairs={{0,8},{4,12},{8,0},{12,4},{16,24},{20,28},{24,16},{28,20},{1,9},{5... | collective-permute-start | bytes 884744 | tf_op jit(solution)/shard_map/swap_dp2/ppermute | solution.py:45
  129.5 4.7 %collective-permute-start.46 = (f32[16,768]{1,0:T(8,128)S(1)}, f32[16,768]{1,0:T(8,128)S(1)}, u32[]{:S(2)}, u32[]{:S(2)}) collective-permute-start(f32[16,768]{1,0:T(8,128)S(1)} %add.120), channel_id=1, source_target_pairs={{0,2},{1,3},{2,0},{3,1},{4,6},{5,7},{6,4},{7,5},{8,10},{9,11},{10,... | collective-permute-start | bytes 147464 | tf_op jit(solution)/shard_map/swap_fsdp2/ppermute | solution.py:45
  132.4 9.9 %collective-permute-start.53 = (bf16[192,768]{1,0:T(8,128)(2,1)S(1)}, bf16[192,768]{1,0:T(8,128)(2,1)S(1)}, u32[]{:S(2)}, u32[]{:S(2)}) collective-permute-start(bf16[192,768]{1,0:T(8,128)(2,1)S(1)} %select_bitcast_fusion.6), channel_id=1, source_target_pairs={{0,4},{4,0},{8,12},{12,8},{16,20},{20,16},{24,28},{28,24},{1,5},{5... | collective-permute-start | bytes 884744 | tf_op jit(solution)/shard_map/swap_dp1/ppermute | solution.py:45
  134.2 11.3 %collective-permute-start.49 = (f32[16,768]{1,0:T(8,128)S(1)}, f32[16,768]{1,0:T(8,128)S(1)}, u32[]{:S(2)}, u32[]{:S(2)}) collective-permute-start(f32[16,768]{1,0:T(8,128)S(1)} %add.124), channel_id=1, source_target_pairs={{0,4},{4,0},{8,12},{12,8},{16,20},{20,16},{24,28},{28,24},{1,5},{5... | collective-permute-start | bytes 147464 | tf_op jit(solution)/shard_map/swap_dp1/ppermute | solution.py:45
  135.5 12.8 %collective-permute-start.58 = (bf16[48,3072]{1,0:T(8,128)(2,1)S(1)}, bf16[48,3072]{1,0:T(8,128)(2,1)S(1)}, u32[]{:S(2)}, u32[]{:S(2)}) collective-permute-start(bf16[48,3072]{1,0:T(8,128)(2,1)S(1)} %broadcast_select_fusion.2), channel_id=1, source_target_pairs={{0,4},{4,0},{8,12},{12,8},{16,20},{20,16},{24,28},{28,24},{1,5},{5... | collective-permute-start | bytes 884744 | tf_op jit(solution)/shard_map/swap_dp1/ppermute | solution.py:45
  136.6 7.4 %collective-permute-start.52 = (bf16[192,768]{1,0:T(8,128)(2,1)S(1)}, bf16[192,768]{1,0:T(8,128)(2,1)S(1)}, u32[]{:S(2)}, u32[]{:S(2)}) collective-permute-start(bf16[192,768]{1,0:T(8,128)(2,1)S(1)} %fusion.8), channel_id=1, source_target_pairs={{0,2},{1,3},{2,0},{3,1},{4,6},{5,7},{6,4},{7,5},{8,10},{9,11},{10,... | collective-permute-start | bytes 884744 | tf_op jit(solution)/shard_map/swap_fsdp2/ppermute | solution.py:45
  137.9 17.4 %collective-permute-start.57 = (bf16[192,768]{1,0:T(8,128)(2,1)S(1)}, bf16[192,768]{1,0:T(8,128)(2,1)S(1)}, u32[]{:S(2)}, u32[]{:S(2)}) collective-permute-start(bf16[192,768]{1,0:T(8,128)(2,1)S(1)} %add_convert_fusion.5), channel_id=1, source_target_pairs={{0,16},{4,20},{8,24},{12,28},{16,0},{20,4},{24,8},{28,12},{1,17},{... | collective-permute-start | bytes 884744 | tf_op jit(solution)/shard_map/swap_dp4/ppermute | solution.py:45
  144.2 17.7 %collective-permute-start.56 = (bf16[192,768]{1,0:T(8,128)(2,1)S(1)}, bf16[192,768]{1,0:T(8,128)(2,1)S(1)}, u32[]{:S(2)}, u32[]{:S(2)}) collective-permute-start(bf16[192,768]{1,0:T(8,128)(2,1)S(1)} %broadcast_select_fusion.3), channel_id=1, source_target_pairs={{0,8},{4,12},{8,0},{12,4},{16,24},{20,28},{24,16},{28,20},{1,9},{5... | collective-permute-start | bytes 884744 | tf_op jit(solution)/shard_map/swap_dp2/ppermute | solution.py:45
  145.6 19.7 %collective-permute-start.55 = (f32[16,768]{1,0:T(8,128)S(1)}, f32[16,768]{1,0:T(8,128)S(1)}, u32[]{:S(2)}, u32[]{:S(2)}) collective-permute-start(f32[16,768]{1,0:T(8,128)S(1)} %add.134), channel_id=1, source_target_pairs={{0,8},{4,12},{8,0},{12,4},{16,24},{20,28},{24,16},{28,20},{1,9},{5... | collective-permute-start | bytes 147464 | tf_op jit(solution)/shard_map/swap_dp2/ppermute | solution.py:45
  148.5 19.5 %collective-permute-start.62 = (bf16[48,3072]{1,0:T(8,128)(2,1)S(1)}, bf16[48,3072]{1,0:T(8,128)(2,1)S(1)}, u32[]{:S(2)}, u32[]{:S(2)}) collective-permute-start(bf16[48,3072]{1,0:T(8,128)(2,1)S(1)} %add_convert_fusion.4), channel_id=1, source_target_pairs={{0,16},{4,20},{8,24},{12,28},{16,0},{20,4},{24,8},{28,12},{1,17},{... | collective-permute-start | bytes 884744 | tf_op jit(solution)/shard_map/swap_dp4/ppermute | solution.py:45
  155.4 16.5 %collective-permute-start.61 = (bf16[192,768]{1,0:T(8,128)(2,1)S(1)}, bf16[192,768]{1,0:T(8,128)(2,1)S(1)}, u32[]{:S(2)}, u32[]{:S(2)}) collective-permute-start(bf16[192,768]{1,0:T(8,128)(2,1)S(1)} %add_convert_fusion.3), channel_id=1, source_target_pairs={{0,8},{4,12},{8,0},{12,4},{16,24},{20,28},{24,16},{28,20},{1,9},{5... | collective-permute-start | bytes 884744 | tf_op jit(solution)/shard_map/swap_dp2/ppermute | solution.py:45
  162.1 18.1 %collective-permute-start.60 = (bf16[192,768]{1,0:T(8,128)(2,1)S(1)}, bf16[192,768]{1,0:T(8,128)(2,1)S(1)}, u32[]{:S(2)}, u32[]{:S(2)}) collective-permute-start(bf16[192,768]{1,0:T(8,128)(2,1)S(1)} %add_convert_fusion.2), channel_id=1, source_target_pairs={{0,16},{4,20},{8,24},{12,28},{16,0},{20,4},{24,8},{28,12},{1,17},{... | collective-permute-start | bytes 884744 | tf_op jit(solution)/shard_map/swap_dp4/ppermute | solution.py:45
  165.2 17.3 %collective-permute-start.59 = (f32[16,768]{1,0:T(8,128)S(1)}, f32[16,768]{1,0:T(8,128)S(1)}, u32[]{:S(2)}, u32[]{:S(2)}) collective-permute-start(f32[16,768]{1,0:T(8,128)S(1)} %add.138), channel_id=1, source_target_pairs={{0,16},{4,20},{8,24},{12,28},{16,0},{20,4},{24,8},{28,12},{1,17},{... | collective-permute-start | bytes 147464 | tf_op jit(solution)/shard_map/swap_dp4/ppermute | solution.py:45
  168.1 12.4 %collective-permute-start.64 = (bf16[48,3072]{1,0:T(8,128)(2,1)S(1)}, bf16[48,3072]{1,0:T(8,128)(2,1)S(1)}, u32[]{:S(2)}, u32[]{:S(2)}) collective-permute-start(bf16[48,3072]{1,0:T(8,128)(2,1)S(1)} %add_convert_fusion.1), channel_id=1, source_target_pairs={{0,4},{4,0},{8,12},{12,8},{16,20},{20,16},{24,28},{28,24},{1,5},{5... | collective-permute-start | bytes 884744 | tf_op jit(solution)/shard_map/swap_dp1/ppermute | solution.py:45
  172.1 19.5 %collective-permute-start.67 = (bf16[384,768]{1,0:T(8,128)(2,1)S(1)}, bf16[384,768]{1,0:T(8,128)(2,1)S(1)}, u32[]{:S(2)}, u32[]{:S(2)}) collective-permute-start(bf16[384,768]{1,0:T(8,128)(2,1)S(1)} %maximum_select_fusion.1), channel_id=1, source_target_pairs={{0,4},{4,0},{8,12},{12,8},{16,20},{20,16},{24,28},{28,24},{1,5},{5... | collective-permute-start | bytes 1769480 | tf_op jit(solution)/shard_map/swap_dp1/ppermute | solution.py:45
  180.3 9.9 %collective-permute-start.63 = (bf16[192,768]{1,0:T(8,128)(2,1)S(1)}, bf16[192,768]{1,0:T(8,128)(2,1)S(1)}, u32[]{:S(2)}, u32[]{:S(2)}) collective-permute-start(bf16[192,768]{1,0:T(8,128)(2,1)S(1)} %add_convert_fusion), channel_id=1, source_target_pairs={{0,8},{4,12},{8,0},{12,4},{16,24},{20,28},{24,16},{28,20},{1,9},{5... | collective-permute-start | bytes 884744 | tf_op jit(solution)/shard_map/swap_dp2/ppermute | solution.py:45
  180.7 20.6 %collective-permute-start.66 = (bf16[2,48,3072]{2,1,0:T(8,128)(2,1)S(1)}, bf16[2,48,3072]{2,1,0:T(8,128)(2,1)S(1)}, u32[]{:S(2)}, u32[]{:S(2)}) collective-permute-start(bf16[2,48,3072]{2,1,0:T(8,128)(2,1)S(1)} %pad_maximum_fusion.1), channel_id=1, source_target_pairs={{0,8},{4,12},{8,0},{12,4},{16,24},{20,28},{24,16},{28,20},{1,9},{5... | collective-permute-start | bytes 1769480 | tf_op jit(solution)/shard_map/swap_dp2/ppermute | solution.py:45
  190.3 12.9 %collective-permute-start.65 = (bf16[2,192,768]{2,1,0:T(8,128)(2,1)S(1)}, bf16[2,192,768]{2,1,0:T(8,128)(2,1)S(1)}, u32[]{:S(2)}, u32[]{:S(2)}) collective-permute-start(bf16[2,192,768]{2,1,0:T(8,128)(2,1)S(1)} %pad_maximum_fusion.2), channel_id=1, source_target_pairs={{0,4},{4,0},{8,12},{12,8},{16,20},{20,16},{24,28},{28,24},{1,5},{5... | collective-permute-start | bytes 1769480 | tf_op jit(solution)/shard_map/swap_dp1/ppermute | solution.py:45
  (37 other events, 237.4 us)

commit v4 on v3

--- a/solution.py
+++ b/solution.py
@@ -18,7 +18,7 @@
 EARLY_TURNS = ""
 MIDDLE_TURNS = "UU"
 UP_STRIPS_FIRST = False
-TURNS = "DSUASUADAASUDASUDASUUADA"
+TURNS = "DUSASUADAASUDASUDASUUADA"
 UP_BITS = (1, 0)
 DOWN_BITS = (0, 1)
 COST = 1024

time: 206 us -> 205 us (level)
  transfers between devices with their start and end apart: 68 -> 68, of which waited for: 27 -> 24; matrix products, arithmetic and copies ran while one was open for 6% -> 6% of each run, Pallas kernels for 25% -> 25%
where the time goes in v4:
time: 205 us; the launch traced here: 204 us
  waiting for transfers between devices  78.3 us (38%)
  Pallas kernels  53.9 us (26%)
  starting transfers between devices  53.5 us (26%)
  other arithmetic  10.9 us (5%)
  local copies, waits for them, and re-layouts  6.49 us (3%)
    ppermute x68, waiting for transfers between devices, swap(): return lax.ppermute(x, axis, [(i, i ^ distance) for i in range(count)])  78.3 us
    ppermute x68, starting transfers between devices, swap(): return lax.ppermute(x, axis, [(i, i ^ distance) for i in range(count)])  53.5 us
    pallas_call x1, Pallas kernels, local(): call(partial(attend_kernel, length=length), (flat_low, flat_low, flat_low...  10.1 us
    pallas_call x1, Pallas kernels, local(): call(partial(attend_back_kernel, length=length), (flat_low, flat_low, fla...  6.24 us
    pallas_call x1, Pallas kernels, local(): call(up_kernel, (sds((shards, tokens, shard_hidden), bf16), *(pltpu.HBM((...  6.1 us
    pallas_call x1, Pallas kernels, local(): call(norm_back_kernel, (pltpu.HBM(flat.shape, f32), flat_low, flat_low, s...  5.19 us
    pallas_call x1, Pallas kernels, local(): call(partial(input_back_kernel, length=length), (flat_low, sds((VEC_ROWS,...  4.67 us
    pallas_call x1, Pallas kernels, local(): call(down_grad_kernel, (down_half,) * 2, 1, 8, 0, [], 'down_grad', reside...  4.4 us
  transfers between devices with their start and end apart: 68, of which 24 were waited for; matrix products, arithmetic and copies ran while one was open for 6% of the time, Pallas kernels for 25%

profile of v4, /device:TPU:0, one launch (start us, length us, event | category | flops | bytes accessed | tf_op | source)
XLA Modules:
  0.0 204.2 jit_solution(8100856010016801761)
XLA Ops:
  1.3 2.7 %pack.1 = (bf16[400,768]{1,0:T(8,128)(2,1)}, bf16[384,768]{1,0:T(8,128)(2,1)}, bf16[400,384]{1,0:T(8,128)(2,1)}, bf16[384,384]{1,0:T(8,128)(2,1)}) custom-call(s32[3]{0:T(128)} %pad_add_fusion.where_ref, bf16[192,768]{1,0:T(8,128)(2,1)} %q_ref.1, bf16[192,768]{1,0:T(8,128)(2,1)} %k_ref.1, bf16[192,768]{1,0:T(8,128)(2,1)} %v_ref.1, bf16[192,768]{1,0:T(8,128)(2,1)} %o_ref.1, ...), custom_call_target="tpu_custom_call" | custom-call | flops 1024 | bytes 1024 | tf_op jit(solution)/shard_map/pack/pallas_call | solution.py:632
  4.0 3.0 %collective-permute-start.6 = (bf16[384,384]{1,0:T(8,128)(2,1)}, bf16[384,384]{1,0:T(8,128)(2,1)}, u32[]{:S(2)}, u32[]{:S(2)}) collective-permute-start(bf16[384,384]{1,0:T(8,128)(2,1)} %get-tuple-element.117), channel_id=1, source_target_pairs={{0,2},{1,3},{2,0},{3,1},{4,6},{5,7},{6,4},{7,5},{8,10},{9,11},{10,... | collective-permute-start | bytes 884744 | tf_op jit(solution)/shard_map/swap_fsdp2/ppermute | solution.py:45
  7.5 7.6 %collective-permute-done.6.refs_8_.refs_14_ = bf16[384,384]{1,0:T(8,128)(2,1)} collective-permute-done((bf16[384,384]{1,0:T(8,128)(2,1)}, bf16[384,384]{1,0:T(8,128)(2,1)}, u32[]{:S(2)}, u32[]{:S(2)}) %collective-permute-start.6) | collective-permute-done | bytes 294944 | tf_op jit(solution)/shard_map/swap_fsdp2/ppermute | solution.py:45
  15.1 2.1 %collective-permute-start.7 = (bf16[384,384]{1,0:T(8,128)(2,1)}, bf16[384,384]{1,0:T(8,128)(2,1)}, u32[]{:S(2)}, u32[]{:S(2)}) collective-permute-start(bf16[384,384]{1,0:T(8,128)(2,1)} %collective-permute-done.6.refs_8_.refs_14_), channel_id=1, source_target_pairs={{0,4},{4,0},{8,12},{12,8},{16,20},{20,16},{24,28},{28,24},{1,5},{5... | collective-permute-start | bytes 884744 | tf_op jit(solution)/shard_map/swap_dp1/ppermute | solution.py:45
  17.2 1.1 fusion.14
  19.2 1.7 collective-permute-done.1.refs_2_
  20.9 1.7 collective-permute-start.11
  22.9 1.5 collective-permute-start.2
  25.3 3.9 %collective-permute-done.11.refs_2_.refs_6_ = bf16[96,1536]{1,0:T(8,128)(2,1)S(1)} collective-permute-done((bf16[96,1536]{1,0:T(8,128)(2,1)S(1)}, bf16[96,1536]{1,0:T(8,128)(2,1)S(1)}, u32[]{:S(2)}, u32[]{:S(2)}) %collective-permute-start.11) | collective-permute-done | bytes 294944 | tf_op jit(solution)/shard_map/swap_fsdp2/ppermute | solution.py:45
  29.2 1.5 collective-permute-start.15
  30.6 2.3 %collective-permute-done.2.refs_3_ = bf16[400,384]{1,0:T(8,128)(2,1)} collective-permute-done((bf16[400,384]{1,0:T(8,128)(2,1)}, bf16[400,384]{1,0:T(8,128)(2,1)}, u32[]{:S(2)}, u32[]{:S(2)}) %collective-permute-start.2) | collective-permute-done | bytes 307232 | tf_op jit(solution)/shard_map/swap_dp1/ppermute | solution.py:45
  33.7 2.5 %collective-permute-done.9.refs_11_.refs_17_ = bf16[384,384]{1,0:T(8,128)(2,1)S(1)} collective-permute-done((bf16[384,384]{1,0:T(8,128)(2,1)}, bf16[384,384]{1,0:T(8,128)(2,1)S(1)}, u32[]{:S(2)}, u32[]{:S(2)}) %collective-permute-start.9) | collective-permute-done | bytes 294944 | tf_op jit(solution)/shard_map/swap_fsdp1/ppermute | solution.py:45
  36.2 1.5 collective-permute-start.18
  37.6 1.6 collective-permute-start.12
  39.2 10.1 %attend.1 = (bf16[256,768]{1,0:T(8,128)(2,1)S(1)}, bf16[256,768]{1,0:T(8,128)(2,1)S(1)}, bf16[256,768]{1,0:T(8,128)(2,1)S(1)}, bf16[4,256,192]{2,1,0:T(8,128)(2,...) custom-call(s32[3]{0:T(128)S(1)} %copy-done.9, ...), custom_call_target="tpu_custom_call" | custom-call | flops 1024 | bytes 1024 | tf_op jit(solution)/shard_map/attend/pallas_call | solution.py:693
  50.7 1.1 collective-permute-done.14.refs_5_.refs_9_
  51.8 1.5 collective-permute-start.19
  53.4 6.1 %up.1 = (bf16[4,256,768]{2,1,0:T(8,128)(2,1)S(1)}, bf16[256,768]{1,0:T(8,128)(2,1)}, bf16[256,768]{1,0:T(8,128)(2,1)}, bf16[2,256,768]{2,1,0:T(8,128)(2,1)}, f32[4,256,768]{2,1,0:T(8,128)S(1)}) custom-call(s32[3]{0:T(128)S(1)} %copy-done.9, bf16[256,768]{1,0:T(8,128)(2,1)S(1)} %get-tuple-element.118.low_ref, f32[16,768]{1,0:T(8,128)S(1)} %get-tuple-element.119.vec_ref, ...), custom_call_target="tpu_custom_call" | custom-call | flops 1024 | bytes 1024 | tf_op jit(solution)/shard_map/up/pallas_call | solution.py:725
  60.3 1.4 collective-permute-start.34
  62.3 6.1 %collective-permute-done.23.refs_7_ = bf16[384,384]{1,0:T(8,128)(2,1)S(1)} collective-permute-done((bf16[384,384]{1,0:T(8,128)(2,1)S(1)}, bf16[384,384]{1,0:T(8,128)(2,1)S(1)}, u32[]{:S(2)}, u32[]{:S(2)}) %collective-permute-start.23) | collective-permute-done | bytes 294944 | tf_op jit(solution)/shard_map/swap_dp2/ppermute | solution.py:45
  68.3 1.6 collective-permute-done.25.refs_9_
  69.9 3.5 %down.1 = (bf16[256,768]{1,0:T(8,128)(2,1)S(1)}, f32[256,768]{1,0:T(8,128)S(1)}, bf16[256,768]{1,0:T(8,128)(2,1)S(1)}, f32[8,768]{1,0:T(8,128)S(1)}) custom-call(s32[3]{0:T(128)S(1)} %copy-done.9, bf16[4,256,768]{2,1,0:T(8,128)(2,1)S(1)} %get-tuple-element.126.act_ref, f32[256,768]{1,0:T(8,128)S(1)} %get-tuple-element.127.n1_ref, ...), custom_call_target="tpu_custom_call" | custom-call | flops 1024 | bytes 1024 | tf_op jit(solution)/shard_map/down/pallas_call | solution.py:742
  73.5 3.0 %hidden_back.1 = (bf16[256,768]{1,0:T(8,128)(2,1)S(1)}, bf16[256,768]{1,0:T(8,128)(2,1)S(1)}, bf16[256,768]{1,0:T(8,128)(2,1)S(1)}, bf16[256,768]{1,0:T(8,128)(2,1)S(1)}, f32[8,768]{1,0:T(8,128)S(1)}) custom-call(s32[3]{0:T(128)S(1)} %copy-done.9, bf16[256,768]{1,0:T(8,128)(2,1)S(1)} %get-tuple-element.162.glow_ref.refs_4_, ...), custom_call_target="tpu_custom_call" | custom-call | flops 1024 | bytes 1024 | tf_op jit(solution)/shard_map/hidden_back/pallas_call | solution.py:753
  77.5 1.1 collective-permute-done.26.got_ref
  79.5 1.2 collective-permute-start.37
  80.7 5.2 %norm_back.1 = (f32[256,768]{1,0:T(8,128)}, bf16[256,768]{1,0:T(8,128)(2,1)S(1)}, bf16[256,768]{1,0:T(8,128)(2,1)S(1)}, f32[8,768]{1,0:T(8,128)S(1)}) custom-call(s32[3]{0:T(128)S(1)} %copy-done.9, f32[256,768]{1,0:T(8,128)S(1)} %get-tuple-element.136.gsec_ref, f32[256,768]{1,0:T(8,128)S(1)} %get-tuple-element.127.n1_ref, ...), custom_call_target="tpu_custom_call" | custom-call | flops 1024 | bytes 1024 | tf_op jit(solution)/shard_map/norm_back/pallas_call | solution.py:763
  87.2 3.7 %near_up.1 = (bf16[2,48,3072]{2,1,0:T(8,128)(2,1)}, bf16[2,48,3072]{2,1,0:T(8,128)(2,1)}, bf16[2,48,3072]{2,1,0:T(8,128)(2,1)}, bf16[2,48,3072]{2,1,0:T(8,128)(2,1)}) custom-call(s32[3]{0:T(128)S(1)} %copy-done.9, bf16[2,256,192]{2,1,0:T(8,128)(2,1)} %get-tuple-element.146.own_ref, bf16[2,256,192]{2,1,0:T(8,128)(2,1)} %copy-done.28, ...), custom_call_target="tpu_custom_call" | custom-call | flops 1024 | bytes 1024 | tf_op jit(solution)/shard_map/near_up/pallas_call | solution.py:777
  90.9 6.2 %attend_back.1 = (bf16[256,768]{1,0:T(8,128)(2,1)S(1)}, bf16[256,768]{1,0:T(8,128)(2,1)S(1)}, bf16[256,768]{1,0:T(8,128)(2,1)S(1)}) custom-call(bf16[256,768]{1,0:T(8,128)(2,1)S(1)} %get-tuple-element.121.q_ref, bf16[256,768]{1,0:T(8,128)(2,1)S(1)} %get-tuple-element.152.k_ref, bf16[256,768]{1,0:T(8,128)(2,1)S(1)} %get-tuple-element.153.v_ref, ...), custom_call_target="tpu_custom_call" | custom-call | flops 1024 | bytes 1024 | tf_op jit(solution)/shard_map/attend_back/pallas_call | solution.py:780
  100.7 4.4 %down_grad.1 = (bf16[384,768]{1,0:T(8,128)(2,1)}, bf16[384,768]{1,0:T(8,128)(2,1)}) custom-call(s32[3]{0:T(128)S(1)} %copy-done.9, bf16[256,768]{1,0:T(8,128)(2,1)} %get-tuple-element.130.refs_0_, bf16[256,768]{1,0:T(8,128)(2,1)} %copy-done.25, bf16[2,256,768]{2,1,0:T(8,128)(2,1)} %copy-done.17, bf16[256,768]{1,0:T(8,128)(2,1)} %copy-done.26, ...), custom_call_target="tpu_custom_call" | custom-call | flops 1024 | bytes 1024 | tf_op jit(solution)/shard_map/down_grad/pallas_call | solution.py:806
  105.1 1.4 collective-permute-start.31
  106.5 1.0 collective-permute-start.46
  107.5 4.3 %near_attn.1 = (bf16[2,192,768]{2,1,0:T(8,128)(2,1)}, bf16[2,192,768]{2,1,0:T(8,128)(2,1)}, bf16[2,192,768]{2,1,0:T(8,128)(2,1)}, bf16[2,192,768]{2,1,0:T(8,128)(2,1)}) custom-call(s32[3]{0:T(128)S(1)} %copy-done.9, bf16[4,256,192]{2,1,0:T(8,128)(2,1)} %get-tuple-element.166.own_ref, bf16[4,256,192]{2,1,0:T(8,128)(2,1)} %copy-done.22, ...), custom_call_target="tpu_custom_call" | custom-call | flops 1024 | bytes 1024 | tf_op jit(solution)/shard_map/near_attn/pallas_call | solution.py:812
  113.6 1.3 select_bitcast_fusion.7
  114.8 1.3 collective-permute-start.45
  116.1 5.2 %collective-permute-done.31 = bf16[2,48,3072]{2,1,0:T(8,128)(2,1)S(1)} collective-permute-done((bf16[2,48,3072]{2,1,0:T(8,128)(2,1)S(1)}, bf16[2,48,3072]{2,1,0:T(8,128)(2,1)S(1)}, u32[]{:S(2)}, u32[]{:S(2)}) %collective-permute-start.31) | collective-permute-done | bytes 589856 | tf_op jit(solution)/shard_map/swap_dp2/ppermute | solution.py:45
  121.4 1.3 collective-permute-start.51
  122.7 4.7 %input_back.1 = (bf16[256,768]{1,0:T(8,128)(2,1)}, f32[16,768]{1,0:T(8,128)S(1)}) custom-call(s32[3]{0:T(128)S(1)} %copy-done.9, s32[2]{0:T(128)S(1)} %copy-done.11, f32[256,768]{1,0:T(8,128)S(1)} %copy-done.6, bf16[256,768]{1,0:T(8,128)(2,1)S(1)} %get-tuple-element.156.refs_2_.gq_ref, bf16[256,768]{1,0:T(8,128)(2,1)S(1)} %get-tuple-element.169.refs_3_.gk_ref, ...), custom_call_target="tpu_custom_call" | custom-call | flops 1024 | bytes 1024 | tf_op jit(solution)/shard_map/input_back/pallas_call | solution.py:817
  128.5 1.2 fusion.4
  129.8 1.4 collective-permute-start.47
  131.3 1.1 collective-permute-start.53
  132.4 1.8 collective-permute-done.47
  134.2 1.1 collective-permute-start.49
  135.5 1.1 collective-permute-start.58
  136.6 1.1 collective-permute-start.52
  137.8 2.7 %collective-permute-start.57 = (bf16[192,768]{1,0:T(8,128)(2,1)S(1)}, bf16[192,768]{1,0:T(8,128)(2,1)S(1)}, u32[]{:S(2)}, u32[]{:S(2)}) collective-permute-start(bf16[192,768]{1,0:T(8,128)(2,1)S(1)} %add_convert_fusion.5), channel_id=1, source_target_pairs={{0,16},{4,20},{8,24},{12,28},{16,0},{20,4},{24,8},{28,12},{1,17},{... | collective-permute-start | bytes 884744 | tf_op jit(solution)/shard_map/swap_dp4/ppermute | solution.py:45
  141.5 3.1 %collective-permute-done.52 = bf16[192,768]{1,0:T(8,128)(2,1)S(1)} collective-permute-done((bf16[192,768]{1,0:T(8,128)(2,1)S(1)}, bf16[192,768]{1,0:T(8,128)(2,1)S(1)}, u32[]{:S(2)}, u32[]{:S(2)}) %collective-permute-start.52) | collective-permute-done | bytes 294944 | tf_op jit(solution)/shard_map/swap_fsdp2/ppermute | solution.py:45
  144.8 1.3 collective-permute-start.56
  146.9 1.2 collective-permute-done.58
  148.3 2.7 %collective-permute-start.62 = (bf16[48,3072]{1,0:T(8,128)(2,1)S(1)}, bf16[48,3072]{1,0:T(8,128)(2,1)S(1)}, u32[]{:S(2)}, u32[]{:S(2)}) collective-permute-start(bf16[48,3072]{1,0:T(8,128)(2,1)S(1)} %add_convert_fusion.4), channel_id=1, source_target_pairs={{0,16},{4,20},{8,24},{12,28},{16,0},{20,4},{24,8},{28,12},{1,17},{... | collective-permute-start | bytes 884744 | tf_op jit(solution)/shard_map/swap_dp4/ppermute | solution.py:45
  151.0 3.7 %collective-permute-done.57 = bf16[192,768]{1,0:T(8,128)(2,1)S(1)} collective-permute-done((bf16[192,768]{1,0:T(8,128)(2,1)S(1)}, bf16[192,768]{1,0:T(8,128)(2,1)S(1)}, u32[]{:S(2)}, u32[]{:S(2)}) %collective-permute-start.57) | collective-permute-done | bytes 294944 | tf_op jit(solution)/shard_map/swap_dp4/ppermute | solution.py:45
  154.8 9.4 %collective-permute-done.56 = bf16[192,768]{1,0:T(8,128)(2,1)S(1)} collective-permute-done((bf16[192,768]{1,0:T(8,128)(2,1)S(1)}, bf16[192,768]{1,0:T(8,128)(2,1)S(1)}, u32[]{:S(2)}, u32[]{:S(2)}) %collective-permute-start.56) | collective-permute-done | bytes 294944 | tf_op jit(solution)/shard_map/swap_dp2/ppermute | solution.py:45
  164.4 2.6 %collective-permute-done.55 = f32[16,768]{1,0:T(8,128)S(1)} collective-permute-done((f32[16,768]{1,0:T(8,128)S(1)}, f32[16,768]{1,0:T(8,128)S(1)}, u32[]{:S(2)}, u32[]{:S(2)}) %collective-permute-start.55) | collective-permute-done | bytes 49184 | tf_op jit(solution)/shard_map/swap_dp2/ppermute | solution.py:45
  167.7 1.8 collective-permute-start.64
  169.5 4.1 %collective-permute-done.61 = bf16[192,768]{1,0:T(8,128)(2,1)S(1)} collective-permute-done((bf16[192,768]{1,0:T(8,128)(2,1)S(1)}, bf16[192,768]{1,0:T(8,128)(2,1)S(1)}, u32[]{:S(2)}, u32[]{:S(2)}) %collective-permute-start.61) | collective-permute-done | bytes 294944 | tf_op jit(solution)/shard_map/swap_dp2/ppermute | solution.py:45
  173.7 1.4 collective-permute-start.67
  175.1 4.8 %collective-permute-done.60 = bf16[192,768]{1,0:T(8,128)(2,1)S(1)} collective-permute-done((bf16[192,768]{1,0:T(8,128)(2,1)S(1)}, bf16[192,768]{1,0:T(8,128)(2,1)S(1)}, u32[]{:S(2)}, u32[]{:S(2)}) %collective-permute-start.60) | collective-permute-done | bytes 294944 | tf_op jit(solution)/shard_map/swap_dp4/ppermute | solution.py:45
  180.2 2.0 collective-permute-start.66
  184.2 5.7 %collective-permute-done.63 = bf16[192,768]{1,0:T(8,128)(2,1)S(1)} collective-permute-done((bf16[192,768]{1,0:T(8,128)(2,1)S(1)}, bf16[192,768]{1,0:T(8,128)(2,1)S(1)}, u32[]{:S(2)}, u32[]{:S(2)}) %collective-permute-start.63) | collective-permute-done | bytes 294944 | tf_op jit(solution)/shard_map/swap_dp2/ppermute | solution.py:45
  190.0 1.5 collective-permute-start.65
  191.5 1.6 fusion
  193.1 6.9 %collective-permute-done.66 = bf16[2,48,3072]{2,1,0:T(8,128)(2,1)S(1)} collective-permute-done((bf16[2,48,3072]{2,1,0:T(8,128)(2,1)S(1)}, bf16[2,48,3072]{2,1,0:T(8,128)(2,1)S(1)}, u32[]{:S(2)}, u32[]{:S(2)}) %collective-permute-start.66) | collective-permute-done | bytes 589856 | tf_op jit(solution)/shard_map/swap_dp2/ppermute | solution.py:45
  200.2 1.7 bitcast_convert_fusion
  202.1 1.1 fusion.9
  203.1 1.1 fusion.10
  (191 shorter events, 22.8 us)
Async XLA Ops:
  4.0 11.1 %collective-permute-start.6 = (bf16[384,384]{1,0:T(8,128)(2,1)}, bf16[384,384]{1,0:T(8,128)(2,1)}, u32[]{:S(2)}, u32[]{:S(2)}) collective-permute-start(bf16[384,384]{1,0:T(8,128)(2,1)} %get-tuple-element.117), channel_id=1, source_target_pairs={{0,2},{1,3},{2,0},{3,1},{4,6},{5,7},{6,4},{7,5},{8,10},{9,11},{10,... | collective-permute-start | bytes 884744 | tf_op jit(solution)/shard_map/swap_fsdp2/ppermute | solution.py:45
  6.9 14.0 %collective-permute-start.1 = (bf16[400,384]{1,0:T(8,128)(2,1)}, bf16[400,384]{1,0:T(8,128)(2,1)}, u32[]{:S(2)}, u32[]{:S(2)}) collective-permute-start(bf16[400,384]{1,0:T(8,128)(2,1)} %get-tuple-element.114), channel_id=1, source_target_pairs={{0,2},{1,3},{2,0},{3,1},{4,6},{5,7},{6,4},{7,5},{8,10},{9,11},{10,... | collective-permute-start | bytes 921608 | tf_op jit(solution)/shard_map/swap_fsdp2/ppermute | solution.py:45
  7.0 17.4 %collective-permute-start.5 = (bf16[384,768]{1,0:T(8,128)(2,1)}, bf16[384,768]{1,0:T(8,128)(2,1)S(1)}, u32[]{:S(2)}, u32[]{:S(2)}) collective-permute-start(bf16[384,768]{1,0:T(8,128)(2,1)} %get-tuple-element.115.refs_6_.refs_12_), channel_id=1, source_target_pairs={{0,1},{1,0},{2,3},{3,2},{4,5},{5,4},{6,7},{7,6},{8,9},{9,8},{10,11... | collective-permute-start | bytes 1769480 | tf_op jit(solution)/shard_map/swap_fsdp1/ppermute | solution.py:45
  7.0 26.4 %collective-permute-start = (bf16[400,768]{1,0:T(8,128)(2,1)}, bf16[400,768]{1,0:T(8,128)(2,1)}, u32[]{:S(2)}, u32[]{:S(2)}) collective-permute-start(bf16[400,768]{1,0:T(8,128)(2,1)} %get-tuple-element.113.refs_0_), channel_id=1, source_target_pairs={{0,1},{1,0},{2,3},{3,2},{4,5},{5,4},{6,7},{7,6},{8,9},{9,8},{10,11... | collective-permute-start | bytes 1843208 | tf_op jit(solution)/shard_map/swap_fsdp1/ppermute | solution.py:45
  15.1 7.8 %collective-permute-start.7 = (bf16[384,384]{1,0:T(8,128)(2,1)}, bf16[384,384]{1,0:T(8,128)(2,1)}, u32[]{:S(2)}, u32[]{:S(2)}) collective-permute-start(bf16[384,384]{1,0:T(8,128)(2,1)} %collective-permute-done.6.refs_8_.refs_14_), channel_id=1, source_target_pairs={{0,4},{4,0},{8,12},{12,8},{16,20},{20,16},{24,28},{28,24},{1,5},{5... | collective-permute-start | bytes 884744 | tf_op jit(solution)/shard_map/swap_dp1/ppermute | solution.py:45
  18.3 4.6 %collective-permute-start.8 = (bf16[384,384]{1,0:T(8,128)(2,1)}, bf16[384,384]{1,0:T(8,128)(2,1)S(1)}, u32[]{:S(2)}, u32[]{:S(2)}) collective-permute-start(bf16[384,384]{1,0:T(8,128)(2,1)} %collective-permute-done.6.refs_8_.refs_14_), channel_id=1, source_target_pairs={{0,1},{1,0},{2,3},{3,2},{4,5},{5,4},{6,7},{7,6},{8,9},{9,8},{10,11... | collective-permute-start | bytes 884744 | tf_op jit(solution)/shard_map/swap_fsdp1/ppermute | solution.py:45
  20.9 8.2 %collective-permute-start.11 = (bf16[96,1536]{1,0:T(8,128)(2,1)S(1)}, bf16[96,1536]{1,0:T(8,128)(2,1)S(1)}, u32[]{:S(2)}, u32[]{:S(2)}) collective-permute-start(bf16[96,1536]{1,0:T(8,128)(2,1)S(1)} %constant_dynamic-slice_fusion.3), channel_id=1, source_target_pairs={{0,2},{1,3},{2,0},{3,1},{4,6},{5,7},{6,4},{7,5},{8,10},{9,11},{10,... | collective-permute-start | bytes 884744 | tf_op jit(solution)/shard_map/swap_fsdp2/ppermute | solution.py:45
  22.9 27.1 %collective-permute-start.10 = (bf16[192,3072]{1,0:T(8,128)(2,1)S(1)}, bf16[192,3072]{1,0:T(8,128)(2,1)}, u32[]{:S(2)}, u32[]{:S(2)}) collective-permute-start(bf16[192,3072]{1,0:T(8,128)(2,1)S(1)} %copy-done), channel_id=1, source_target_pairs={{0,1},{1,0},{2,3},{3,2},{4,5},{5,4},{6,7},{7,6},{8,9},{9,8},{10,11... | collective-permute-start | bytes 3538952 | tf_op jit(solution)/shard_map/swap_fsdp1/ppermute | solution.py:45
  22.9 10.0 %collective-permute-start.2 = (bf16[400,384]{1,0:T(8,128)(2,1)}, bf16[400,384]{1,0:T(8,128)(2,1)}, u32[]{:S(2)}, u32[]{:S(2)}) collective-permute-start(bf16[400,384]{1,0:T(8,128)(2,1)} %collective-permute-done.1.refs_2_), channel_id=1, source_target_pairs={{0,4},{4,0},{8,12},{12,8},{16,20},{20,16},{24,28},{28,24},{1,5},{5... | collective-permute-start | bytes 921608 | tf_op jit(solution)/shard_map/swap_dp1/ppermute | solution.py:45
  24.4 8.5 %collective-permute-start.3 = (bf16[400,384]{1,0:T(8,128)(2,1)}, bf16[400,384]{1,0:T(8,128)(2,1)}, u32[]{:S(2)}, u32[]{:S(2)}) collective-permute-start(bf16[400,384]{1,0:T(8,128)(2,1)} %collective-permute-done.1.refs_2_), channel_id=1, source_target_pairs={{0,1},{1,0},{2,3},{3,2},{4,5},{5,4},{6,7},{7,6},{8,9},{9,8},{10,11... | collective-permute-start | bytes 921608 | tf_op jit(solution)/shard_map/swap_fsdp1/ppermute | solution.py:45
  29.2 20.2 %collective-permute-start.15 = (bf16[96,3072]{1,0:T(8,128)(2,1)}, bf16[96,3072]{1,0:T(8,128)(2,1)S(1)}, u32[]{:S(2)}, u32[]{:S(2)}) collective-permute-start(bf16[96,3072]{1,0:T(8,128)(2,1)} %get-tuple-element.124), channel_id=1, source_target_pairs={{0,2},{1,3},{2,0},{3,1},{4,6},{5,7},{6,4},{7,5},{8,10},{9,11},{10,... | collective-permute-start | bytes 1769480 | tf_op jit(solution)/shard_map/swap_fsdp2/ppermute | solution.py:45
  32.9 29.3 %collective-permute-start.17 = (bf16[768,768]{1,0:T(8,128)(2,1)S(1)}, bf16[768,768]{1,0:T(8,128)(2,1)S(1)}, u32[]{:S(2)}, u32[]{:S(2)}) collective-permute-start(bf16[768,768]{1,0:T(8,128)(2,1)S(1)} %copy-done.1), channel_id=1, source_target_pairs={{0,1},{1,0},{2,3},{3,2},{4,5},{5,4},{6,7},{7,6},{8,9},{9,8},{10,11... | collective-permute-start | bytes 3538952 | tf_op jit(solution)/shard_map/swap_fsdp1/ppermute | solution.py:45
  32.9 3.3 %collective-permute-start.9 = (bf16[384,384]{1,0:T(8,128)(2,1)}, bf16[384,384]{1,0:T(8,128)(2,1)S(1)}, u32[]{:S(2)}, u32[]{:S(2)}) collective-permute-start(bf16[384,384]{1,0:T(8,128)(2,1)} %collective-permute-done.7.refs_9_.refs_15_), channel_id=1, source_target_pairs={{0,1},{1,0},{2,3},{3,2},{4,5},{5,4},{6,7},{7,6},{8,9},{9,8},{10,11... | collective-permute-start | bytes 884744 | tf_op jit(solution)/shard_map/swap_fsdp1/ppermute | solution.py:45
  33.4 4.2 %collective-permute-start.4 = (bf16[400,384]{1,0:T(8,128)(2,1)}, bf16[400,384]{1,0:T(8,128)(2,1)S(1)}, u32[]{:S(2)}, u32[]{:S(2)}) collective-permute-start(bf16[400,384]{1,0:T(8,128)(2,1)} %collective-permute-done.2.refs_3_), channel_id=1, source_target_pairs={{0,1},{1,0},{2,3},{3,2},{4,5},{5,4},{6,7},{7,6},{8,9},{9,8},{10,11... | collective-permute-start | bytes 921608 | tf_op jit(solution)/shard_map/swap_fsdp1/ppermute | solution.py:45
  36.2 13.8 %collective-permute-start.18 = (bf16[384,384]{1,0:T(8,128)(2,1)S(1)}, bf16[384,384]{1,0:T(8,128)(2,1)S(1)}, u32[]{:S(2)}, u32[]{:S(2)}) collective-permute-start(bf16[384,384]{1,0:T(8,128)(2,1)S(1)} %get-tuple-element.128), channel_id=1, source_target_pairs={{0,2},{1,3},{2,0},{3,1},{4,6},{5,7},{6,4},{7,5},{8,10},{9,11},{10,... | collective-permute-start | bytes 884744 | tf_op jit(solution)/shard_map/swap_fsdp2/ppermute | solution.py:45
  37.6 11.8 %collective-permute-start.12 = (bf16[96,1536]{1,0:T(8,128)(2,1)S(1)}, bf16[96,1536]{1,0:T(8,128)(2,1)S(1)}, u32[]{:S(2)}, u32[]{:S(2)}) collective-permute-start(bf16[96,1536]{1,0:T(8,128)(2,1)S(1)} %collective-permute-done.11.refs_2_.refs_6_), channel_id=1, source_target_pairs={{0,8},{4,12},{8,0},{12,4},{16,24},{20,28},{24,16},{28,20},{1,9},{5... | collective-permute-start | bytes 884744 | tf_op jit(solution)/shard_map/swap_dp2/ppermute | solution.py:45
  49.3 4.0 %collective-permute-start.16 = (bf16[96,3072]{1,0:T(8,128)(2,1)S(1)}, bf16[96,3072]{1,0:T(8,128)(2,1)S(1)}, u32[]{:S(2)}, u32[]{:S(2)}) collective-permute-start(bf16[96,3072]{1,0:T(8,128)(2,1)S(1)} %collective-permute-done.15.refs_6_.refs_10_), channel_id=1, source_target_pairs={{0,1},{1,0},{2,3},{3,2},{4,5},{5,4},{6,7},{7,6},{8,9},{9,8},{10,11... | collective-permute-start | bytes 1769480 | tf_op jit(solution)/shard_map/swap_fsdp1/ppermute | solution.py:45
  49.4 2.4 %collective-permute-start.14 = (bf16[96,1536]{1,0:T(8,128)(2,1)S(1)}, bf16[96,1536]{1,0:T(8,128)(2,1)S(1)}, u32[]{:S(2)}, u32[]{:S(2)}) collective-permute-start(bf16[96,1536]{1,0:T(8,128)(2,1)S(1)} %collective-permute-done.12.refs_3_.refs_7_), channel_id=1, source_target_pairs={{0,1},{1,0},{2,3},{3,2},{4,5},{5,4},{6,7},{7,6},{8,9},{9,8},{10,11... | collective-permute-start | bytes 884744 | tf_op jit(solution)/shard_map/swap_fsdp1/ppermute | solution.py:45
  49.9 3.4 %collective-permute-start.13 = (bf16[96,1536]{1,0:T(8,128)(2,1)S(1)}, bf16[96,1536]{1,0:T(8,128)(2,1)S(1)}, u32[]{:S(2)}, u32[]{:S(2)}) collective-permute-start(bf16[96,1536]{1,0:T(8,128)(2,1)S(1)} %collective-permute-done.11.refs_2_.refs_6_), channel_id=1, source_target_pairs={{0,1},{1,0},{2,3},{3,2},{4,5},{5,4},{6,7},{7,6},{8,9},{9,8},{10,11... | collective-permute-start | bytes 884744 | tf_op jit(solution)/shard_map/swap_fsdp1/ppermute | solution.py:45
  50.0 9.5 %collective-permute-start.22 = (bf16[384,384]{1,0:T(8,128)(2,1)S(1)}, bf16[384,384]{1,0:T(8,128)(2,1)S(1)}, u32[]{:S(2)}, u32[]{:S(2)}) collective-permute-start(bf16[384,384]{1,0:T(8,128)(2,1)S(1)} %get-tuple-element.133), channel_id=1, source_target_pairs={{0,2},{1,3},{2,0},{3,1},{4,6},{5,7},{6,4},{7,5},{8,10},{9,11},{10,... | collective-permute-start | bytes 884744 | tf_op jit(solution)/shard_map/swap_fsdp2/ppermute | solution.py:45
  51.8 9.9 %collective-permute-start.19 = (bf16[384,384]{1,0:T(8,128)(2,1)S(1)}, bf16[384,384]{1,0:T(8,128)(2,1)S(1)}, u32[]{:S(2)}, u32[]{:S(2)}) collective-permute-start(bf16[384,384]{1,0:T(8,128)(2,1)S(1)} %collective-permute-done.18.refs_2_), channel_id=1, source_target_pairs={{0,4},{4,0},{8,12},{12,8},{16,20},{20,16},{24,28},{28,24},{1,5},{5... | collective-permute-start | bytes 884744 | tf_op jit(solution)/shard_map/swap_dp1/ppermute | solution.py:45
  59.5 8.8 %collective-permute-start.23 = (bf16[384,384]{1,0:T(8,128)(2,1)S(1)}, bf16[384,384]{1,0:T(8,128)(2,1)S(1)}, u32[]{:S(2)}, u32[]{:S(2)}) collective-permute-start(bf16[384,384]{1,0:T(8,128)(2,1)S(1)} %collective-permute-done.22.refs_6_), channel_id=1, source_target_pairs={{0,8},{4,12},{8,0},{12,4},{16,24},{20,28},{24,16},{28,20},{1,9},{5... | collective-permute-start | bytes 884744 | tf_op jit(solution)/shard_map/swap_dp2/ppermute | solution.py:45
  60.3 19.2 %collective-permute-start.34 = (bf16[2,256,768]{2,1,0:T(8,128)(2,1)}, bf16[2,256,768]{2,1,0:T(8,128)(2,1)S(1)}, u32[]{:S(2)}, u32[]{:S(2)}) collective-permute-start(bf16[2,256,768]{2,1,0:T(8,128)(2,1)} %get-tuple-element.160), channel_id=1, source_target_pairs={{0,2},{1,3},{2,0},{3,1},{4,6},{5,7},{6,4},{7,5},{8,10},{9,11},{10,... | collective-permute-start | bytes 2359304 | tf_op jit(solution)/shard_map/swap_fsdp2/ppermute | solution.py:45
  61.7 6.6 %collective-permute-start.24 = (bf16[384,384]{1,0:T(8,128)(2,1)S(1)}, bf16[384,384]{1,0:T(8,128)(2,1)S(1)}, u32[]{:S(2)}, u32[]{:S(2)}) collective-permute-start(bf16[384,384]{1,0:T(8,128)(2,1)S(1)} %collective-permute-done.22.refs_6_), channel_id=1, source_target_pairs={{0,1},{1,0},{2,3},{3,2},{4,5},{5,4},{6,7},{7,6},{8,9},{9,8},{10,11... | collective-permute-start | bytes 884744 | tf_op jit(solution)/shard_map/swap_fsdp1/ppermute | solution.py:45
  61.7 6.6 %collective-permute-start.21 = (bf16[384,384]{1,0:T(8,128)(2,1)S(1)}, bf16[384,384]{1,0:T(8,128)(2,1)S(1)}, u32[]{:S(2)}, u32[]{:S(2)}) collective-permute-start(bf16[384,384]{1,0:T(8,128)(2,1)S(1)} %collective-permute-done.19.refs_3_), channel_id=1, source_target_pairs={{0,1},{1,0},{2,3},{3,2},{4,5},{5,4},{6,7},{7,6},{8,9},{9,8},{10,11... | collective-permute-start | bytes 884744 | tf_op jit(solution)/shard_map/swap_fsdp1/ppermute | solution.py:45
  62.2 6.1 %collective-permute-start.20 = (bf16[384,384]{1,0:T(8,128)(2,1)S(1)}, bf16[384,384]{1,0:T(8,128)(2,1)S(1)}, u32[]{:S(2)}, u32[]{:S(2)}) collective-permute-start(bf16[384,384]{1,0:T(8,128)(2,1)S(1)} %collective-permute-done.18.refs_2_), channel_id=1, source_target_pairs={{0,1},{1,0},{2,3},{3,2},{4,5},{5,4},{6,7},{7,6},{8,9},{9,8},{10,11... | collective-permute-start | bytes 884744 | tf_op jit(solution)/shard_map/swap_fsdp1/ppermute | solution.py:45
  76.5 9.5 %collective-permute-start.27 = (bf16[256,768]{1,0:T(8,128)(2,1)S(1)}, bf16[256,768]{1,0:T(8,128)(2,1)S(1)}, u32[]{:S(2)}, u32[]{:S(2)}) collective-permute-start(bf16[256,768]{1,0:T(8,128)(2,1)S(1)} %get-tuple-element.140.refs_0_), channel_id=1, source_target_pairs={{0,1},{1,0},{2,3},{3,2},{4,5},{5,4},{6,7},{7,6},{8,9},{9,8},{10,11... | collective-permute-start | bytes 1179656 | tf_op jit(solution)/shard_map/swap_fsdp1/ppermute | solution.py:45
  77.0 9.0 %collective-permute-start.28 = (bf16[256,768]{1,0:T(8,128)(2,1)S(1)}, bf16[256,768]{1,0:T(8,128)(2,1)S(1)}, u32[]{:S(2)}, u32[]{:S(2)}) collective-permute-start(bf16[256,768]{1,0:T(8,128)(2,1)S(1)} %get-tuple-element.141.refs_1_), channel_id=1, source_target_pairs={{0,1},{1,0},{2,3},{3,2},{4,5},{5,4},{6,7},{7,6},{8,9},{9,8},{10,11... | collective-permute-start | bytes 1179656 | tf_op jit(solution)/shard_map/swap_fsdp1/ppermute | solution.py:45
  77.2 9.5 %collective-permute-start.29 = (bf16[256,768]{1,0:T(8,128)(2,1)S(1)}, bf16[256,768]{1,0:T(8,128)(2,1)S(1)}, u32[]{:S(2)}, u32[]{:S(2)}) collective-permute-start(bf16[256,768]{1,0:T(8,128)(2,1)S(1)} %get-tuple-element.142.refs_2_), channel_id=1, source_target_pairs={{0,1},{1,0},{2,3},{3,2},{4,5},{5,4},{6,7},{7,6},{8,9},{9,8},{10,11... | collective-permute-start | bytes 1179656 | tf_op jit(solution)/shard_map/swap_fsdp1/ppermute | solution.py:45
  78.6 8.1 %collective-permute-start.30 = (bf16[256,768]{1,0:T(8,128)(2,1)S(1)}, bf16[256,768]{1,0:T(8,128)(2,1)S(1)}, u32[]{:S(2)}, u32[]{:S(2)}) collective-permute-start(bf16[256,768]{1,0:T(8,128)(2,1)S(1)} %get-tuple-element.143.refs_3_), channel_id=1, source_target_pairs={{0,1},{1,0},{2,3},{3,2},{4,5},{5,4},{6,7},{7,6},{8,9},{9,8},{10,11... | collective-permute-start | bytes 1179656 | tf_op jit(solution)/shard_map/swap_fsdp1/ppermute | solution.py:45
  79.5 17.6 %collective-permute-start.37 = (bf16[256,768]{1,0:T(8,128)(2,1)S(1)}, bf16[256,768]{1,0:T(8,128)(2,1)S(1)}, u32[]{:S(2)}, u32[]{:S(2)}) collective-permute-start(bf16[256,768]{1,0:T(8,128)(2,1)S(1)} %get-tuple-element.162.glow_ref.refs_4_), channel_id=1, source_target_pairs={{0,2},{1,3},{2,0},{3,1},{4,6},{5,7},{6,4},{7,5},{8,10},{9,11},{10,... | collective-permute-start | bytes 1179656 | tf_op jit(solution)/shard_map/swap_fsdp2/ppermute | solution.py:45
  85.9 11.3 %collective-permute-start.39 = (bf16[4,256,192]{2,1,0:T(8,128)(2,1)S(1)}, bf16[4,256,192]{2,1,0:T(8,128)(2,1)S(1)}, u32[]{:S(2)}, u32[]{:S(2)}) collective-permute-start(bf16[4,256,192]{2,1,0:T(8,128)(2,1)S(1)} %copy-done.30), channel_id=1, source_target_pairs={{0,1},{1,0},{2,3},{3,2},{4,5},{5,4},{6,7},{7,6},{8,9},{9,8},{10,11... | collective-permute-start | bytes 1179656 | tf_op jit(solution)/shard_map/swap_fsdp1/ppermute | solution.py:45
  86.1 12.0 %collective-permute-start.36 = (bf16[256,768]{1,0:T(8,128)(2,1)S(1)}, bf16[256,768]{1,0:T(8,128)(2,1)S(1)}, u32[]{:S(2)}, u32[]{:S(2)}) collective-permute-start(bf16[256,768]{1,0:T(8,128)(2,1)S(1)} %get-tuple-element.162.glow_ref.refs_4_), channel_id=1, source_target_pairs={{0,1},{1,0},{2,3},{3,2},{4,5},{5,4},{6,7},{7,6},{8,9},{9,8},{10,11... | collective-permute-start | bytes 1179656 | tf_op jit(solution)/shard_map/swap_fsdp1/ppermute | solution.py:45
  86.7 11.6 %collective-permute-start.33 = (bf16[256,768]{1,0:T(8,128)(2,1)S(1)}, bf16[256,768]{1,0:T(8,128)(2,1)S(1)}, u32[]{:S(2)}, u32[]{:S(2)}) collective-permute-start(bf16[256,768]{1,0:T(8,128)(2,1)S(1)} %copy-done.31), channel_id=1, source_target_pairs={{0,1},{1,0},{2,3},{3,2},{4,5},{5,4},{6,7},{7,6},{8,9},{9,8},{10,11... | collective-permute-start | bytes 1179656 | tf_op jit(solution)/shard_map/swap_fsdp1/ppermute | solution.py:45
  86.7 11.9 %collective-permute-start.35 = (bf16[256,768]{1,0:T(8,128)(2,1)S(1)}, bf16[256,768]{1,0:T(8,128)(2,1)S(1)}, u32[]{:S(2)}, u32[]{:S(2)}) collective-permute-start(bf16[256,768]{1,0:T(8,128)(2,1)S(1)} %slice_bitcast_fusion), channel_id=1, source_target_pairs={{0,1},{1,0},{2,3},{3,2},{4,5},{5,4},{6,7},{7,6},{8,9},{9,8},{10,11... | collective-permute-start | bytes 1179656 | tf_op jit(solution)/shard_map/swap_fsdp1/ppermute | solution.py:45
  97.3 16.3 %collective-permute-start.32 = (bf16[2,48,3072]{2,1,0:T(8,128)(2,1)}, bf16[2,48,3072]{2,1,0:T(8,128)(2,1)}, u32[]{:S(2)}, u32[]{:S(2)}) collective-permute-start(bf16[2,48,3072]{2,1,0:T(8,128)(2,1)} %get-tuple-element.151), channel_id=1, source_target_pairs={{0,2},{1,3},{2,0},{3,1},{4,6},{5,7},{6,4},{7,5},{8,10},{9,11},{10,... | collective-permute-start | bytes 1769480 | tf_op jit(solution)/shard_map/swap_fsdp2/ppermute | solution.py:45
  98.1 7.0 %collective-permute-start.40 = (bf16[256,768]{1,0:T(8,128)(2,1)S(1)}, bf16[256,768]{1,0:T(8,128)(2,1)}, u32[]{:S(2)}, u32[]{:S(2)}) collective-permute-start(bf16[256,768]{1,0:T(8,128)(2,1)S(1)} %get-tuple-element.144.refs_0_), channel_id=1, source_target_pairs={{0,1},{1,0},{2,3},{3,2},{4,5},{5,4},{6,7},{7,6},{8,9},{9,8},{10,11... | collective-permute-start | bytes 1179656 | tf_op jit(solution)/shard_map/swap_fsdp1/ppermute | solution.py:45
  98.2 8.2 %collective-permute-start.41 = (bf16[256,768]{1,0:T(8,128)(2,1)S(1)}, bf16[256,768]{1,0:T(8,128)(2,1)}, u32[]{:S(2)}, u32[]{:S(2)}) collective-permute-start(bf16[256,768]{1,0:T(8,128)(2,1)S(1)} %get-tuple-element.168.refs_1_.gv_ref), channel_id=1, source_target_pairs={{0,1},{1,0},{2,3},{3,2},{4,5},{5,4},{6,7},{7,6},{8,9},{9,8},{10,11... | collective-permute-start | bytes 1179656 | tf_op jit(solution)/shard_map/swap_fsdp1/ppermute | solution.py:45
  98.6 8.9 %collective-permute-start.42 = (bf16[256,768]{1,0:T(8,128)(2,1)S(1)}, bf16[256,768]{1,0:T(8,128)(2,1)}, u32[]{:S(2)}, u32[]{:S(2)}) collective-permute-start(bf16[256,768]{1,0:T(8,128)(2,1)S(1)} %get-tuple-element.156.refs_2_.gq_ref), channel_id=1, source_target_pairs={{0,1},{1,0},{2,3},{3,2},{4,5},{5,4},{6,7},{7,6},{8,9},{9,8},{10,11... | collective-permute-start | bytes 1179656 | tf_op jit(solution)/shard_map/swap_fsdp1/ppermute | solution.py:45
  99.7 7.8 %collective-permute-start.43 = (bf16[256,768]{1,0:T(8,128)(2,1)S(1)}, bf16[256,768]{1,0:T(8,128)(2,1)}, u32[]{:S(2)}, u32[]{:S(2)}) collective-permute-start(bf16[256,768]{1,0:T(8,128)(2,1)S(1)} %get-tuple-element.169.refs_3_.gk_ref), channel_id=1, source_target_pairs={{0,1},{1,0},{2,3},{3,2},{4,5},{5,4},{6,7},{7,6},{8,9},{9,8},{10,11... | collective-permute-start | bytes 1179656 | tf_op jit(solution)/shard_map/swap_fsdp1/ppermute | solution.py:45
  105.1 16.3 %collective-permute-start.31 = (bf16[2,48,3072]{2,1,0:T(8,128)(2,1)S(1)}, bf16[2,48,3072]{2,1,0:T(8,128)(2,1)S(1)}, u32[]{:S(2)}, u32[]{:S(2)}) collective-permute-start(bf16[2,48,3072]{2,1,0:T(8,128)(2,1)S(1)} %copy-done.29), channel_id=1, source_target_pairs={{0,8},{4,12},{8,0},{12,4},{16,24},{20,28},{24,16},{28,20},{1,9},{5... | collective-permute-start | bytes 1769480 | tf_op jit(solution)/shard_map/swap_dp2/ppermute | solution.py:45
  106.5 20.9 %collective-permute-start.46 = (bf16[384,768]{1,0:T(8,128)(2,1)}, bf16[384,768]{1,0:T(8,128)(2,1)S(1)}, u32[]{:S(2)}, u32[]{:S(2)}) collective-permute-start(bf16[384,768]{1,0:T(8,128)(2,1)} %get-tuple-element.180), channel_id=1, source_target_pairs={{0,4},{4,0},{8,12},{12,8},{16,20},{20,16},{24,28},{28,24},{1,5},{5... | collective-permute-start | bytes 1769480 | tf_op jit(solution)/shard_map/swap_dp1/ppermute | solution.py:45
  111.8 19.3 %collective-permute-start.48 = (bf16[2,192,768]{2,1,0:T(8,128)(2,1)}, bf16[2,192,768]{2,1,0:T(8,128)(2,1)S(1)}, u32[]{:S(2)}, u32[]{:S(2)}) collective-permute-start(bf16[2,192,768]{2,1,0:T(8,128)(2,1)} %get-tuple-element.170), channel_id=1, source_target_pairs={{0,2},{1,3},{2,0},{3,1},{4,6},{5,7},{6,4},{7,5},{8,10},{9,11},{10,... | collective-permute-start | bytes 1769480 | tf_op jit(solution)/shard_map/swap_fsdp2/ppermute | solution.py:45
  112.7 23.9 %collective-permute-start.50 = (bf16[2,192,768]{2,1,0:T(8,128)(2,1)}, bf16[2,192,768]{2,1,0:T(8,128)(2,1)S(1)}, u32[]{:S(2)}, u32[]{:S(2)}) collective-permute-start(bf16[2,192,768]{2,1,0:T(8,128)(2,1)} %get-tuple-element.188), channel_id=1, source_target_pairs={{0,4},{4,0},{8,12},{12,8},{16,20},{20,16},{24,28},{28,24},{1,5},{5... | collective-permute-start | bytes 1769480 | tf_op jit(solution)/shard_map/swap_dp1/ppermute | solution.py:45
  114.8 12.8 %collective-permute-start.45 = (bf16[48,3072]{1,0:T(8,128)(2,1)S(1)}, bf16[48,3072]{1,0:T(8,128)(2,1)S(1)}, u32[]{:S(2)}, u32[]{:S(2)}) collective-permute-start(bf16[48,3072]{1,0:T(8,128)(2,1)S(1)} %select_bitcast_fusion.7), channel_id=1, source_target_pairs={{0,8},{4,12},{8,0},{12,4},{16,24},{20,28},{24,16},{28,20},{1,9},{5... | collective-permute-start | bytes 884744 | tf_op jit(solution)/shard_map/swap_dp2/ppermute | solution.py:45
  121.4 13.9 %collective-permute-start.51 = (bf16[48,3072]{1,0:T(8,128)(2,1)S(1)}, bf16[48,3072]{1,0:T(8,128)(2,1)S(1)}, u32[]{:S(2)}, u32[]{:S(2)}) collective-permute-start(bf16[48,3072]{1,0:T(8,128)(2,1)S(1)} %fusion.5), channel_id=1, source_target_pairs={{0,2},{1,3},{2,0},{3,1},{4,6},{5,7},{6,4},{7,5},{8,10},{9,11},{10,... | collective-permute-start | bytes 884744 | tf_op jit(solution)/shard_map/swap_fsdp2/ppermute | solution.py:45
  127.6 10.1 %collective-permute-start.54 = (bf16[192,768]{1,0:T(8,128)(2,1)S(1)}, bf16[192,768]{1,0:T(8,128)(2,1)S(1)}, u32[]{:S(2)}, u32[]{:S(2)}) collective-permute-start(bf16[192,768]{1,0:T(8,128)(2,1)S(1)} %add_convert_fusion.12), channel_id=1, source_target_pairs={{0,8},{4,12},{8,0},{12,4},{16,24},{20,28},{24,16},{28,20},{1,9},{5... | collective-permute-start | bytes 884744 | tf_op jit(solution)/shard_map/swap_dp2/ppermute | solution.py:45
  129.8 4.5 %collective-permute-start.47 = (f32[16,768]{1,0:T(8,128)S(1)}, f32[16,768]{1,0:T(8,128)S(1)}, u32[]{:S(2)}, u32[]{:S(2)}) collective-permute-start(f32[16,768]{1,0:T(8,128)S(1)} %add.121), channel_id=1, source_target_pairs={{0,2},{1,3},{2,0},{3,1},{4,6},{5,7},{6,4},{7,5},{8,10},{9,11},{10,... | collective-permute-start | bytes 147464 | tf_op jit(solution)/shard_map/swap_fsdp2/ppermute | solution.py:45
  131.3 10.0 %collective-permute-start.53 = (bf16[192,768]{1,0:T(8,128)(2,1)S(1)}, bf16[192,768]{1,0:T(8,128)(2,1)S(1)}, u32[]{:S(2)}, u32[]{:S(2)}) collective-permute-start(bf16[192,768]{1,0:T(8,128)(2,1)S(1)} %select_bitcast_fusion.6), channel_id=1, source_target_pairs={{0,4},{4,0},{8,12},{12,8},{16,20},{20,16},{24,28},{28,24},{1,5},{5... | collective-permute-start | bytes 884744 | tf_op jit(solution)/shard_map/swap_dp1/ppermute | solution.py:45
  134.2 11.8 %collective-permute-start.49 = (f32[16,768]{1,0:T(8,128)S(1)}, f32[16,768]{1,0:T(8,128)S(1)}, u32[]{:S(2)}, u32[]{:S(2)}) collective-permute-start(f32[16,768]{1,0:T(8,128)S(1)} %add.124), channel_id=1, source_target_pairs={{0,4},{4,0},{8,12},{12,8},{16,20},{20,16},{24,28},{28,24},{1,5},{5... | collective-permute-start | bytes 147464 | tf_op jit(solution)/shard_map/swap_dp1/ppermute | solution.py:45
  135.5 12.7 %collective-permute-start.58 = (bf16[48,3072]{1,0:T(8,128)(2,1)S(1)}, bf16[48,3072]{1,0:T(8,128)(2,1)S(1)}, u32[]{:S(2)}, u32[]{:S(2)}) collective-permute-start(bf16[48,3072]{1,0:T(8,128)(2,1)S(1)} %broadcast_select_fusion.2), channel_id=1, source_target_pairs={{0,4},{4,0},{8,12},{12,8},{16,20},{20,16},{24,28},{28,24},{1,5},{5... | collective-permute-start | bytes 884744 | tf_op jit(solution)/shard_map/swap_dp1/ppermute | solution.py:45
  136.6 8.0 %collective-permute-start.52 = (bf16[192,768]{1,0:T(8,128)(2,1)S(1)}, bf16[192,768]{1,0:T(8,128)(2,1)S(1)}, u32[]{:S(2)}, u32[]{:S(2)}) collective-permute-start(bf16[192,768]{1,0:T(8,128)(2,1)S(1)} %fusion.8), channel_id=1, source_target_pairs={{0,2},{1,3},{2,0},{3,1},{4,6},{5,7},{6,4},{7,5},{8,10},{9,11},{10,... | collective-permute-start | bytes 884744 | tf_op jit(solution)/shard_map/swap_fsdp2/ppermute | solution.py:45
  137.8 16.8 %collective-permute-start.57 = (bf16[192,768]{1,0:T(8,128)(2,1)S(1)}, bf16[192,768]{1,0:T(8,128)(2,1)S(1)}, u32[]{:S(2)}, u32[]{:S(2)}) collective-permute-start(bf16[192,768]{1,0:T(8,128)(2,1)S(1)} %add_convert_fusion.5), channel_id=1, source_target_pairs={{0,16},{4,20},{8,24},{12,28},{16,0},{20,4},{24,8},{28,12},{1,17},{... | collective-permute-start | bytes 884744 | tf_op jit(solution)/shard_map/swap_dp4/ppermute | solution.py:45
  144.8 19.4 %collective-permute-start.56 = (bf16[192,768]{1,0:T(8,128)(2,1)S(1)}, bf16[192,768]{1,0:T(8,128)(2,1)S(1)}, u32[]{:S(2)}, u32[]{:S(2)}) collective-permute-start(bf16[192,768]{1,0:T(8,128)(2,1)S(1)} %broadcast_select_fusion.3), channel_id=1, source_target_pairs={{0,8},{4,12},{8,0},{12,4},{16,24},{20,28},{24,16},{28,20},{1,9},{5... | collective-permute-start | bytes 884744 | tf_op jit(solution)/shard_map/swap_dp2/ppermute | solution.py:45
  146.0 21.0 %collective-permute-start.55 = (f32[16,768]{1,0:T(8,128)S(1)}, f32[16,768]{1,0:T(8,128)S(1)}, u32[]{:S(2)}, u32[]{:S(2)}) collective-permute-start(f32[16,768]{1,0:T(8,128)S(1)} %add.134), channel_id=1, source_target_pairs={{0,8},{4,12},{8,0},{12,4},{16,24},{20,28},{24,16},{28,20},{1,9},{5... | collective-permute-start | bytes 147464 | tf_op jit(solution)/shard_map/swap_dp2/ppermute | solution.py:45
  148.3 19.3 %collective-permute-start.62 = (bf16[48,3072]{1,0:T(8,128)(2,1)S(1)}, bf16[48,3072]{1,0:T(8,128)(2,1)S(1)}, u32[]{:S(2)}, u32[]{:S(2)}) collective-permute-start(bf16[48,3072]{1,0:T(8,128)(2,1)S(1)} %add_convert_fusion.4), channel_id=1, source_target_pairs={{0,16},{4,20},{8,24},{12,28},{16,0},{20,4},{24,8},{28,12},{1,17},{... | collective-permute-start | bytes 884744 | tf_op jit(solution)/shard_map/swap_dp4/ppermute | solution.py:45
  154.7 18.8 %collective-permute-start.61 = (bf16[192,768]{1,0:T(8,128)(2,1)S(1)}, bf16[192,768]{1,0:T(8,128)(2,1)S(1)}, u32[]{:S(2)}, u32[]{:S(2)}) collective-permute-start(bf16[192,768]{1,0:T(8,128)(2,1)S(1)} %add_convert_fusion.3), channel_id=1, source_target_pairs={{0,8},{4,12},{8,0},{12,4},{16,24},{20,28},{24,16},{28,20},{1,9},{5... | collective-permute-start | bytes 884744 | tf_op jit(solution)/shard_map/swap_dp2/ppermute | solution.py:45
  164.4 15.5 %collective-permute-start.60 = (bf16[192,768]{1,0:T(8,128)(2,1)S(1)}, bf16[192,768]{1,0:T(8,128)(2,1)S(1)}, u32[]{:S(2)}, u32[]{:S(2)}) collective-permute-start(bf16[192,768]{1,0:T(8,128)(2,1)S(1)} %add_convert_fusion.2), channel_id=1, source_target_pairs={{0,16},{4,20},{8,24},{12,28},{16,0},{20,4},{24,8},{28,12},{1,17},{... | collective-permute-start | bytes 884744 | tf_op jit(solution)/shard_map/swap_dp4/ppermute | solution.py:45
  167.0 15.2 %collective-permute-start.59 = (f32[16,768]{1,0:T(8,128)S(1)}, f32[16,768]{1,0:T(8,128)S(1)}, u32[]{:S(2)}, u32[]{:S(2)}) collective-permute-start(f32[16,768]{1,0:T(8,128)S(1)} %add.138), channel_id=1, source_target_pairs={{0,16},{4,20},{8,24},{12,28},{16,0},{20,4},{24,8},{28,12},{1,17},{... | collective-permute-start | bytes 147464 | tf_op jit(solution)/shard_map/swap_dp4/ppermute | solution.py:45
  167.7 12.5 %collective-permute-start.64 = (bf16[48,3072]{1,0:T(8,128)(2,1)S(1)}, bf16[48,3072]{1,0:T(8,128)(2,1)S(1)}, u32[]{:S(2)}, u32[]{:S(2)}) collective-permute-start(bf16[48,3072]{1,0:T(8,128)(2,1)S(1)} %add_convert_fusion.1), channel_id=1, source_target_pairs={{0,4},{4,0},{8,12},{12,8},{16,20},{20,16},{24,28},{28,24},{1,5},{5... | collective-permute-start | bytes 884744 | tf_op jit(solution)/shard_map/swap_dp1/ppermute | solution.py:45
  173.7 17.8 %collective-permute-start.67 = (bf16[384,768]{1,0:T(8,128)(2,1)S(1)}, bf16[384,768]{1,0:T(8,128)(2,1)S(1)}, u32[]{:S(2)}, u32[]{:S(2)}) collective-permute-start(bf16[384,768]{1,0:T(8,128)(2,1)S(1)} %maximum_select_fusion.1), channel_id=1, source_target_pairs={{0,4},{4,0},{8,12},{12,8},{16,20},{20,16},{24,28},{28,24},{1,5},{5... | collective-permute-start | bytes 1769480 | tf_op jit(solution)/shard_map/swap_dp1/ppermute | solution.py:45
  180.0 9.9 %collective-permute-start.63 = (bf16[192,768]{1,0:T(8,128)(2,1)S(1)}, bf16[192,768]{1,0:T(8,128)(2,1)S(1)}, u32[]{:S(2)}, u32[]{:S(2)}) collective-permute-start(bf16[192,768]{1,0:T(8,128)(2,1)S(1)} %add_convert_fusion), channel_id=1, source_target_pairs={{0,8},{4,12},{8,0},{12,4},{16,24},{20,28},{24,16},{28,20},{1,9},{5... | collective-permute-start | bytes 884744 | tf_op jit(solution)/shard_map/swap_dp2/ppermute | solution.py:45
  180.2 19.8 %collective-permute-start.66 = (bf16[2,48,3072]{2,1,0:T(8,128)(2,1)S(1)}, bf16[2,48,3072]{2,1,0:T(8,128)(2,1)S(1)}, u32[]{:S(2)}, u32[]{:S(2)}) collective-permute-start(bf16[2,48,3072]{2,1,0:T(8,128)(2,1)S(1)} %pad_maximum_fusion.1), channel_id=1, source_target_pairs={{0,8},{4,12},{8,0},{12,4},{16,24},{20,28},{24,16},{28,20},{1,9},{5... | collective-permute-start | bytes 1769480 | tf_op jit(solution)/shard_map/swap_dp2/ppermute | solution.py:45
  190.0 11.9 %collective-permute-start.65 = (bf16[2,192,768]{2,1,0:T(8,128)(2,1)S(1)}, bf16[2,192,768]{2,1,0:T(8,128)(2,1)S(1)}, u32[]{:S(2)}, u32[]{:S(2)}) collective-permute-start(bf16[2,192,768]{2,1,0:T(8,128)(2,1)S(1)} %pad_maximum_fusion.2), channel_id=1, source_target_pairs={{0,4},{4,0},{8,12},{12,8},{16,20},{20,16},{24,28},{28,24},{1,5},{5... | collective-permute-start | bytes 1769480 | tf_op jit(solution)/shard_map/swap_dp1/ppermute | solution.py:45
  (37 other events, 238.4 us)
